TPU v7x, 32 devices: a whole 2x2x4 slice. The times are simulated.
32 devices in a mesh: items: 4 (over y, x), rows: 8 (over z, core).
Axes of the slice: x: 2, y: 2, z: 4, core: 2. Of those that a mesh axis runs over, the one named last changes fastest.
Arguments:
- image: bfloat16 [4, 64, 64, 512], P('items', 'rows'), may hold values from -18 to 18
- embed: bfloat16 [4, 2048], P('items'), may hold values from -6 to 6
- text: bfloat16 [4, 128, 2048], P('items', 'rows'), may hold values from -6 to 6
- extent: int32 [4, 2], P('items'), may hold values from 32 to 64, as said below
- first_norm_gain1: float32 [512], replicated, may hold values from 0.1 to 1.9
- conv1_w: bfloat16 [3, 3, 512, 512], replicated, may hold values from -0.09375 to 0.09375
- embed_w: bfloat16 [2048, 1024], replicated, may hold values from -0.125 to 0.125
- second_norm_gain2: float32 [512], replicated, may hold values from 0.1 to 1.9
- conv2_w: bfloat16 [3, 3, 512, 512], replicated, may hold values from -0.09375 to 0.09375
- attention_norm_gain: float32 [512], replicated, may hold values from 0.1 to 1.9
- qkv_w: bfloat16 [512, 1536], replicated, may hold values from -0.25 to 0.25
- text_w: bfloat16 [2048, 1024], replicated, may hold values from -0.125 to 0.125
- proj_w: bfloat16 [512, 512], replicated, may hold values from -6 to 6
- cotangent: bfloat16 [4, 64, 64, 512], P('items', 'rows'), may hold values from -6 to 6
Outputs:
- output: bfloat16 [4, 64, 64, 512], P('items', 'rows')
- image_grad: float32 [4, 64, 64, 512], P('items', 'rows')
- embed_grad: float32 [4, 2048], P('items')
- text_grad: float32 [4, 128, 2048], P('items', 'rows')
- norm1_gain_grad: float32 [512], P('rows')
- conv1_w_grad: float32 [3, 3, 512, 512], P(None, None, None, 'rows')
- embed_w_grad: float32 [2048, 1024], P('rows')
- norm2_gain_grad: float32 [512], P('rows')
- conv2_w_grad: float32 [3, 3, 512, 512], P(None, None, None, 'rows')
- attn_gain_grad: float32 [512], P('rows')
- qkv_w_grad: float32 [512, 1536], P(None, 'rows')
- text_w_grad: float32 [2048, 1024], P('rows')
- proj_w_grad: float32 [512, 512], P(None, 'rows')
Inputs may be any that keep to these rules, and one draw needn't show every extreme that they name: `extent`: each image's valid rows and columns are 64 and 64 minus the same multiple 0, 1 or 2 of a quarter of them; in every draw some image fills its frame and some other image keeps half of its rows and half of its columns.
All inputs are finite; a program needn't handle non-finite values.
Results may differ from a plain program's by a relative error of at most 0.018.
Values may be sent and summed in bfloat16 or wider, within the bound.
A program may use at most 192 MiB of HBM per device.

v0:
```python
import functools

import jax
import jax.numpy as jnp
from jax import lax
from jax.experimental import pallas as pl
from jax.experimental.pallas import tpu as pltpu
from jax.sharding import PartitionSpec as P

GROUPS = 32
HEADS = 8
F32, BF16 = jnp.float32, jnp.bfloat16
NEG = -1e30


def dot(a, b, ca, cb):
    return lax.dot_general(a, b, (((ca,), (cb,)), ((), ())), preferred_element_type=F32)

def attention_kernel(width, step, bq, ext_ref, qkv_ref, text_ref, go_ref, out_ref, dqkv_ref, dtext_ref,
                     kn, vn, kt, vt, s0, s1, e0, e1, dkt, dvt):
    scores, raised = (s0, s1), (e0, e1)
    chunks, _, span = qkv_ref.shape
    tlen = text_ref.shape[0]
    d = go_ref.shape[1]
    pix = chunks * span
    keys = pix + tlen
    steps = keys // step
    rows_ok, cols_ok = ext_ref[0, 0], ext_ref[0, 1]
    def stage(c, carry):
        base = pl.multiple_of(c * span, span)
        pos = base + lax.broadcasted_iota(jnp.int32, (16, span), 1)
        row = lax.broadcasted_iota(jnp.int32, (16, span), 0)
        ok = (pos // width < rows_ok) & (pos % width < cols_ok)
        extra = jnp.where((row == 0) & jnp.logical_not(ok), NEG, 0.0)
        k = qkv_ref[c, d:2 * d, :]
        v = qkv_ref[c, 2 * d:, :]
        kt[:, pl.ds(base, span)] = k
        vt[:, pl.ds(base, span)] = v
        rest = jnp.zeros((128 - d - 16, span), F32)
        ka = jnp.concatenate([k.astype(F32), extra, rest], axis=0)
        va = jnp.concatenate([v.astype(F32), jnp.where(row < 3, 1.0, 0.0), rest], axis=0)
        kn[pl.ds(base, span), :] = ka.T.astype(BF16)
        vn[pl.ds(base, span), :] = va.T.astype(BF16)
        return carry
    lax.fori_loop(0, chunks, stage, 0)
    tk = text_ref[:, :d].astype(F32)
    tv = text_ref[:, d:].astype(F32)
    kt[:, pix:] = tk.T.astype(BF16)
    vt[:, pix:] = tv.T.astype(BF16)
    lanes = lax.broadcasted_iota(jnp.int32, (tlen, 128 - d), 1)
    kn[pix:, :] = jnp.concatenate([tk, jnp.zeros((tlen, 128 - d), F32)], axis=1).astype(BF16)
    vn[pix:, :] = jnp.concatenate([tv, jnp.where(lanes < 3, 1.0, 0.0)], axis=1).astype(BF16)
    dkt[...] = jnp.zeros_like(dkt)
    dvt[...] = jnp.zeros_like(dvt)

    low_peak = jnp.full((8, bq), -3e38, F32)

    def q_aug(c, half):
        q = qkv_ref[c, :d, half * bq:(half + 1) * bq].astype(F32) * (d ** -0.5)
        r = lax.broadcasted_iota(jnp.int32, (128 - d, bq), 0)
        return jnp.concatenate([q, jnp.where(r == 0, 1.0, 0.0)], axis=0).astype(BF16)

    def run(score, exp, back):
        def body(j, carry):
            pk, total, acc, dq = carry
            at = pl.ds(pl.multiple_of(j * step, step), step)
            if score:
                slot, qa = score
                s = dot(kn[at, :], qa, 1, 0)
                scores[slot][at, :] = s
                pk = jnp.maximum(pk, jnp.max(s.reshape(step // 8, 8, bq), axis=0))
            if exp:
                slot, peak = exp
                e = jnp.exp(scores[slot][at, :] - peak)
                total = total + jnp.sum(e.reshape(step // 8, 8, bq), axis=0)
                low = e.astype(BF16)
                raised[slot][at, :] = low
                acc = acc + dot(vt[:, at], low, 1, 0)
            if back:
                slot, goa, gs, q = back
                dp = dot(vn[at, :], goa, 1, 0)
                e = raised[slot][at, :]
                ds = (e.astype(F32) * dp).astype(BF16)
                dvt[:, at] += dot(gs, e, 1, 1)
                dkt[:, at] += dot(q, ds, 1, 1)
                dq = dq + dot(kt[:, at], ds, 1, 0)
            return pk, total, acc, dq
        init = (low_peak, jnp.zeros((8, bq), F32), jnp.zeros((d, bq), F32), jnp.zeros((d, bq), F32))
        return lax.fori_loop(0, steps, body, init)

    def finish_exp(c, half, total, acc):
        inv = 1.0 / jnp.sum(total, axis=0, keepdims=True)
        o = acc * inv
        cols = slice(half * bq, (half + 1) * bq)
        out_ref[c, :, cols] = o.astype(BF16)
        go = go_ref[c, :, cols].astype(F32)
        nd = -jnp.sum(go * o, axis=0, keepdims=True) * inv
        gs = go * inv
        hi = nd.astype(BF16).astype(F32)
        mid = (nd - hi).astype(BF16).astype(F32)
        lo = nd - hi - mid
        r = lax.broadcasted_iota(jnp.int32, (16, bq), 0)
        extra = jnp.where(r == 0, hi, jnp.where(r == 1, mid, jnp.where(r == 2, lo, 0.0)))
        goa = jnp.concatenate([gs, extra, jnp.zeros((128 - d - 16, bq), F32)], axis=0).astype(BF16)
        return goa

    def put_dq(c, half, dq):
        dqkv_ref[c, :d, half * bq:(half + 1) * bq] = (dq * (d ** -0.5)).astype(BF16)

    def top(pk):
        return jnp.max(pk, axis=0, keepdims=True)

    def q_of(c, half):
        return qkv_ref[c, :d, half * bq:(half + 1) * bq]

    pk, _, _, _ = run((0, q_aug(0, 0)), None, None)
    pk, total, acc, _ = run((1, q_aug(0, 1)), (0, top(pk)), None)
    goa = finish_exp(0, 0, total, acc)

    def two(h, carry):
        pk, goa = carry
        pk2, total, acc, dq = run((0, q_aug(h + 1, 0)), (1, top(pk)), (0, goa, goa[:d], q_of(h, 0)))
        put_dq(h, 0, dq)
        goa = finish_exp(h, 1, total, acc)
        pk3, total, acc, dq = run((1, q_aug(h + 1, 1)), (0, top(pk2)), (1, goa, goa[:d], q_of(h, 1)))
        put_dq(h, 1, dq)
        return pk3, finish_exp(h + 1, 0, total, acc)
    pk, goa = lax.fori_loop(0, chunks - 1, two, (pk, goa))
    last = chunks - 1
    _, total, acc, dq = run(None, (1, top(pk)), (0, goa, goa[:d], q_of(last, 0)))
    put_dq(last, 0, dq)
    goa = finish_exp(last, 1, total, acc)
    _, _, _, dq = run(None, None, (1, goa, goa[:d], q_of(last, 1)))
    put_dq(last, 1, dq)

    def finish(c, carry):
        at = pl.ds(pl.multiple_of(c * span, span), span)
        dqkv_ref[c, d:2 * d, :] = (dkt[:, at] * (d ** -0.5)).astype(BF16)
        dqkv_ref[c, 2 * d:, :] = dvt[:, at].astype(BF16)
        return carry
    lax.fori_loop(0, chunks, finish, 0)
    dtext_ref[:d, :] = (dkt[:, pix:] * (d ** -0.5)).astype(BF16)
    dtext_ref[d:, :] = dvt[:, pix:].astype(BF16)

def attention(ext, qkv, text, go, width):
    chunks, wide, span = qkv.shape
    d = wide // 3
    tlen = text.shape[0]
    keys = chunks * span + tlen
    bq = span // 2
    lanes = keys // 128
    step = 128 * max(n for n in range(1, 12) if lanes % n == 0)
    vm = pl.BlockSpec(memory_space=pltpu.VMEM)
    flops = 2 * 6 * chunks * span * keys * d
    return pl.pallas_call(
        functools.partial(attention_kernel, width, step, bq),
        out_shape=(
            jax.ShapeDtypeStruct(go.shape, BF16),
            jax.ShapeDtypeStruct(qkv.shape, BF16),
            jax.ShapeDtypeStruct((2 * d, tlen), BF16),
        ),
        in_specs=[pl.BlockSpec(memory_space=pltpu.SMEM), vm, vm, vm],
        out_specs=(vm, vm, vm),
        scratch_shapes=[
            pltpu.VMEM((keys, 128), BF16),
            pltpu.VMEM((keys, 128), BF16),
            pltpu.VMEM((d, keys), BF16),
            pltpu.VMEM((d, keys), BF16),
            pltpu.VMEM((keys, bq), F32),
            pltpu.VMEM((keys, bq), F32),
            pltpu.VMEM((keys, bq), BF16),
            pltpu.VMEM((keys, bq), BF16),
            pltpu.VMEM((d, keys), F32),
            pltpu.VMEM((d, keys), F32),
        ],
        compiler_params=pltpu.CompilerParams(vmem_limit_bytes=56 << 20),
        cost_estimate=pl.CostEstimate(
            flops=4 * flops, bytes_accessed=16 * chunks * span * d, transcendentals=chunks * span * keys
        ),
    )(ext, qkv, text, go)


MESH = pl.DeviceIdType.MESH
EPS = 1e-05
WHOLE = pl.BlockSpec(memory_space=pltpu.VMEM)
SCALARS = pl.BlockSpec(memory_space=pltpu.SMEM)
ANYWHERE = pl.BlockSpec(memory_space=pl.ANY)


def exchange_kernel(n, count, gathers, *refs):
    inputs, refs = refs[: 1 + count + gathers], refs[1 + count + gathers :]
    outputs, refs = refs[: 1 + 2 * count + gathers], refs[1 + 2 * count + gathers :]
    stats_ref, rows, given = inputs[0], inputs[1 : 1 + count], inputs[1 + count :]
    total_ref, outs, gathered = outputs[0], outputs[1 : 1 + 2 * count], outputs[1 + 2 * count :]
    slots, lands = refs[0], refs[1 : 1 + 2 * count]
    send, recv, row_send, row_recv, own = refs[1 + 2 * count :]
    me = lax.axis_index("rows")
    barrier = pltpu.get_barrier_semaphore()

    def greet(k, carry):
        pl.semaphore_signal(
            barrier, inc=1, device_id={"rows": lax.rem(me + k, n)}, device_id_type=MESH
        )
        return carry

    lax.fori_loop(1, n, greet, 0)
    slots[me] = stats_ref[...]
    pl.semaphore_wait(barrier, n - 1)
    shared = [(stats_ref, slots)] + list(zip(given, gathered))

    def share(j, k):
        return pltpu.make_async_remote_copy(
            src_ref=shared[j][0],
            dst_ref=shared[j][1].at[me],
            send_sem=send.at[j, k],
            recv_sem=recv.at[j, k],
            device_id={"rows": lax.rem(me + k, n)},
            device_id_type=MESH,
        )

    def start(k, carry):
        share(0, k).start()
        return carry

    lax.fori_loop(1, n, start, 0)

    def row_copy(j, side):
        last = rows[j].shape[1] - 1
        at = last if side == 0 else 0
        return pltpu.make_async_remote_copy(
            src_ref=rows[j].at[:, at : at + 1],
            dst_ref=lands[2 * j + side],
            send_sem=row_send.at[2 * j + side],
            recv_sem=row_recv.at[2 * j + side],
            device_id={"rows": me + 1 if side == 0 else me - 1},
            device_id_type=MESH,
        )

    for j in range(count):

        @pl.when(me < n - 1)
        def _():
            row_copy(j, 0).start()

        @pl.when(me > 0)
        def _():
            row_copy(j, 1).start()

    for j in range(gathers):

        def start_given(k, carry):
            share(1 + j, k).start()
            return carry

        lax.fori_loop(1, n, start_given, 0)
        pltpu.make_async_copy(given[j], gathered[j].at[me], own.at[j]).start()

    def finish(k, carry):
        share(0, k).wait()
        return carry

    lax.fori_loop(1, n, finish, 0)
    total_ref[...] = lax.fori_loop(1, n, lambda k, s: s + slots[k], slots[0])
    for j in range(count):

        @pl.when(me > 0)
        def _():
            row_copy(j, 0).wait_recv()
            outs[2 * j][...] = lands[2 * j][...]

        @pl.when(me == 0)
        def _():
            outs[2 * j][...] = jnp.zeros_like(outs[2 * j])

        @pl.when(me < n - 1)
        def _():
            row_copy(j, 1).wait_recv()
            outs[2 * j + 1][...] = lands[2 * j + 1][...]
            row_copy(j, 0).wait_send()

        @pl.when(me == n - 1)
        def _():
            outs[2 * j + 1][...] = jnp.zeros_like(outs[2 * j + 1])

        @pl.when(me > 0)
        def _():
            row_copy(j, 1).wait_send()

    for j in range(gathers):

        def finish_given(k, carry):
            share(1 + j, k).wait()
            return carry

        lax.fori_loop(1, n, finish_given, 0)
        pltpu.make_async_copy(given[j], gathered[j].at[me], own.at[j]).wait()


def exchange(stats, rows, identity, given=()):
    n = lax.axis_size("rows")
    edge = []
    for array in rows:
        edge += [jax.ShapeDtypeStruct(array.shape[:1] + (1,) + array.shape[2:], array.dtype)] * 2
    whole = [jax.ShapeDtypeStruct((n,) + array.shape, array.dtype) for array in given]
    count, gathers = len(rows), len(given)
    nbytes = 4 * stats.size * n + sum(2 * e.size * e.dtype.itemsize for e in (*edge, *whole))
    return pl.pallas_call(
        functools.partial(exchange_kernel, n, count, gathers),
        out_shape=(jax.ShapeDtypeStruct(stats.shape, F32), *edge, *whole),
        in_specs=[WHOLE] + [ANYWHERE] * (count + gathers),
        out_specs=(WHOLE,) * (1 + 2 * count) + (ANYWHERE,) * gathers,
        scratch_shapes=[
            pltpu.VMEM((n,) + stats.shape, F32),
            *[pltpu.VMEM(e.shape, e.dtype) for e in edge],
            pltpu.SemaphoreType.DMA((1 + gathers, n)),
            pltpu.SemaphoreType.DMA((1 + gathers, n)),
            pltpu.SemaphoreType.DMA((max(1, 2 * count),)),
            pltpu.SemaphoreType.DMA((max(1, 2 * count),)),
            pltpu.SemaphoreType.DMA((max(1, gathers),)),
        ],
        compiler_params=pltpu.CompilerParams(collective_id=identity, has_side_effects=True),
        cost_estimate=pl.CostEstimate(
            flops=6_000_000_000, bytes_accessed=nbytes, transcendentals=0
        ),
        name=f"exchange{identity}",
    )(stats, *rows, *given)


def group_sums(rows):
    channels = rows.shape[1]
    size = channels // GROUPS
    one = lax.broadcasted_iota(jnp.int32, (channels, channels), 0) // size
    two = lax.broadcasted_iota(jnp.int32, (channels, channels), 1) // size
    same = jnp.where(one == two, 1.0, 0.0).astype(BF16)
    high = rows.astype(BF16)
    rest = rows - high.astype(F32)
    mid = rest.astype(BF16)
    tail = (rest - mid.astype(F32)).astype(BF16)
    return dot(high, same, 1, 0) + dot(mid, same, 1, 0) + dot(tail, same, 1, 0)


def image_count(info, i, channels):
    return (info[i, 0] * info[i, 1]).astype(F32) * (channels // GROUPS)


def norm_of(stats, count):
    sums = group_sums(stats)
    average = sums[0:1] / count
    square = sums[1:2] / count
    return average, lax.rsqrt(square - average * average + EPS)


def means_of(stats, weight, count):
    sums = group_sums(stats * weight)
    return sums[0:1] / count, sums[1:2] / count


def window(info, i, row, shape):
    ok = (row >= 0) & (row < info[i, 0])
    limit = jnp.where(ok, info[i, 1], 0)
    return jnp.where(lax.broadcasted_iota(jnp.int32, shape, 0) < limit, 1.0, 0.0)


def padded_row(center, above, below, i, r):
    if r == 0:
        return above[i, 0]
    if r == center.shape[1] + 1:
        return below[i, 0]
    return center[i, r - 1]


def put_shifted(out, i, r, value, plain=None):
    width, channels = value.shape
    column = lax.broadcasted_iota(jnp.int32, value.shape, 0)
    left = jnp.where(column == 0, 0.0, pltpu.roll(value, 1, 0))
    right = jnp.where(column == width - 1, 0.0, pltpu.roll(value, width - 1, 0))
    out[i, r, :, :channels] = left.astype(BF16)
    low = value.astype(BF16)
    out[i, r, :, channels : 2 * channels] = low
    if plain is not None:
        plain[i, r] = low
    out[i, r, :, 2 * channels :] = right.astype(BF16)


def sigmoid(v):
    return 1.0 / (1.0 + jnp.exp(-v))


def silu_slope(v):
    s = sigmoid(v)
    return s * (1.0 + v * (1.0 - s))


def put_stats(stats_ref, i, first, second):
    channels = first.shape[1]
    one = jnp.sum(first, axis=0, keepdims=True)
    two = jnp.sum(second, axis=0, keepdims=True)
    row = lax.broadcasted_iota(jnp.int32, (8, channels), 0)
    stats_ref[i] = jnp.where(row == 0, one, jnp.where(row == 1, two, 0.0))


def tap_rows(shifted, tap, images, rows_dev, width):
    block = shifted[:, pl.ds(tap, rows_dev)]
    return block.reshape(images * rows_dev * width, shifted.shape[3])


def conv1_kernel(info, image, above, below, stats, gain, weight, first, out_stats, hidden, acc, shifted):
    images, rows_dev, width, channels = image.shape
    tap = pl.program_id(0)
    base = info[0, 2]

    @pl.when(tap == 0)
    def _():
        for i in range(images):
            average, inverse = norm_of(stats[i], image_count(info, i, channels))
            for r in range(rows_dev + 2):
                inside = window(info, i, base + r - 1, (width, channels))
                start = padded_row(image, above, below, i, r).astype(F32) * inside
                value = (start - average) * inverse * inside * gain[...]
                put_shifted(shifted, i, r, value * sigmoid(value) * inside, hidden)

    part = dot(tap_rows(shifted, tap, images, rows_dev, width), weight[0], 1, 0)

    @pl.when(tap == 0)
    def _():
        acc[...] = part

    @pl.when(tap > 0)
    def _():
        acc[...] += part

    @pl.when(tap == 2)
    def _():
        for i in range(images):
            one = two = jnp.zeros((width, channels), F32)
            for r in range(rows_dev):
                inside = window(info, i, base + r, (width, channels))
                at = (i * rows_dev + r) * width
                value = acc[at : at + width] * inside
                first[i, r] = value
                one = one + value
                two = two + value * value
            put_stats(out_stats, i, one, two)


def moved_of(value, inside, average, inverse, gain, scale, shift):
    normal = (value - average) * inverse * inside
    return normal, normal * gain * (1.0 + scale) + shift


def conv2_kernel(
    info, first, above, below, stats, gain, shifts, image, weight, middle, out_stats, second, acc,
    shifted,
):
    images, rows_dev, width, channels = first.shape
    tap = pl.program_id(0)
    base = info[0, 2]

    @pl.when(tap == 0)
    def _():
        for i in range(images):
            average, inverse = norm_of(stats[i], image_count(info, i, channels))
            scale, shift = shifts[i : i + 1, :channels], shifts[i : i + 1, channels:]
            for r in range(rows_dev + 2):
                inside = window(info, i, base + r - 1, (width, channels))
                value = padded_row(first, above, below, i, r)
                _, moved = moved_of(value, inside, average, inverse, gain[...], scale, shift)
                put_shifted(shifted, i, r, moved * sigmoid(moved) * inside, second)

    part = dot(tap_rows(shifted, tap, images, rows_dev, width), weight[0], 1, 0)

    @pl.when(tap == 0)
    def _():
        acc[...] = part

    @pl.when(tap > 0)
    def _():
        acc[...] += part

    @pl.when(tap == 2)
    def _():
        for i in range(images):
            one = two = jnp.zeros((width, channels), F32)
            for r in range(rows_dev):
                inside = window(info, i, base + r, (width, channels))
                at = (i * rows_dev + r) * width
                value = (image[i, r].astype(F32) + acc[at : at + width]) * inside
                middle[i, r] = value
                one = one + value
                two = two + value * value
            put_stats(out_stats, i, one, two)


def dgrad(shifted, tap, weight, images, rows_dev, width):
    channels = weight.shape[2]
    lhs = tap_rows(shifted, tap, images, rows_dev, width)
    part = None
    for b in range(3):
        term = dot(
            lhs[:, b * channels : (b + 1) * channels],
            weight[0, (2 - b) * channels : (3 - b) * channels, :],
            1,
            1,
        )
        part = term if part is None else part + term
    return part


def back2_kernel(
    info, grad, grad_above, grad_below, middle, mid_above, mid_below, cot, cot_above, cot_below,
    mid_stats, grad_stats, attn_gain, first, first_stats, gain, shifts, weight,
    grad_middle, moved_grad, out_stats, plain, acc, shifted,
):
    images, rows_dev, width, channels = first.shape
    tap = pl.program_id(0)
    base = info[0, 2]

    @pl.when(tap == 0)
    def _():
        for i in range(images):
            count = image_count(info, i, channels)
            average, inverse = norm_of(mid_stats[i], count)
            mean, cross = means_of(grad_stats[i], attn_gain[...], count)
            for r in range(rows_dev + 2):
                inside = window(info, i, base + r - 1, (width, channels))
                normal = (padded_row(middle, mid_above, mid_below, i, r) - average) * inverse
                dx = padded_row(grad, grad_above, grad_below, i, r) * attn_gain[...]
                term = (dx - mean - normal * cross) * inverse * inside
                total = padded_row(cot, cot_above, cot_below, i, r).astype(F32) + term
                if 0 < r <= rows_dev:
                    grad_middle[i, r - 1] = total
                put_shifted(shifted, i, r, total * inside, plain)

    part = dgrad(shifted, tap, weight, images, rows_dev, width)

    @pl.when(tap == 0)
    def _():
        acc[...] = part

    @pl.when(tap > 0)
    def _():
        acc[...] += part

    @pl.when(tap == 2)
    def _():
        for i in range(images):
            average, inverse = norm_of(first_stats[i], image_count(info, i, channels))
            scale, shift = shifts[i : i + 1, :channels], shifts[i : i + 1, channels:]
            one = two = jnp.zeros((width, channels), F32)
            for r in range(rows_dev):
                inside = window(info, i, base + r, (width, channels))
                at = (i * rows_dev + r) * width
                normal, moved = moved_of(
                    first[i, r], inside, average, inverse, gain[...], scale, shift
                )
                value = acc[at : at + width] * inside * silu_slope(moved)
                moved_grad[i, r] = value
                one = one + value
                two = two + value * normal
            put_stats(out_stats, i, one, two)


def back1_kernel(
    info, grad, grad_above, grad_below, first, first_above, first_below, first_stats, grad_stats,
    gain, shifts, image, image_stats, first_gain, weight,
    pre_grad, out_stats, plain, acc, shifted,
):
    images, rows_dev, width, channels = first.shape
    tap = pl.program_id(0)
    base = info[0, 2]

    @pl.when(tap == 0)
    def _():
        for i in range(images):
            count = image_count(info, i, channels)
            average, inverse = norm_of(first_stats[i], count)
            factor = gain[...] * (1.0 + shifts[i : i + 1, :channels])
            mean, cross = means_of(grad_stats[i], factor, count)
            for r in range(rows_dev + 2):
                inside = window(info, i, base + r - 1, (width, channels))
                normal = (padded_row(first, first_above, first_below, i, r) - average) * inverse
                dx = padded_row(grad, grad_above, grad_below, i, r) * factor
                put_shifted(shifted, i, r, (dx - mean - normal * cross) * inverse * inside, plain)

    part = dgrad(shifted, tap, weight, images, rows_dev, width)

    @pl.when(tap == 0)
    def _():
        acc[...] = part

    @pl.when(tap > 0)
    def _():
        acc[...] += part

    @pl.when(tap == 2)
    def _():
        for i in range(images):
            average, inverse = norm_of(image_stats[i], image_count(info, i, channels))
            one = two = jnp.zeros((width, channels), F32)
            for r in range(rows_dev):
                inside = window(info, i, base + r, (width, channels))
                at = (i * rows_dev + r) * width
                normal = (image[i, r].astype(F32) - average) * inverse * inside
                slope = silu_slope(normal * first_gain[...])
                value = acc[at : at + width] * inside * slope
                pre_grad[i, r] = value
                one = one + value
                two = two + value * normal
            put_stats(out_stats, i, one, two)


def conv_call(kernel, info, inputs, weight, outs, flipped):
    images, rows_dev, width, channels = outs[0].shape

    def whole(shape):
        return pl.BlockSpec(shape, lambda tap: (0,) * len(shape))

    def tap_of(tap):
        return ((2 - tap) if flipped else tap, 0, 0)

    weight = weight.reshape(3, 3 * channels, channels)
    flops = 2 * 9 * images * rows_dev * width * channels * channels
    moved = sum(a.size * a.dtype.itemsize for a in (*inputs, weight, *outs))
    return pl.pallas_call(
        kernel,
        grid=(3,),
        out_shape=tuple(outs),
        in_specs=[SCALARS]
        + [whole(a.shape) for a in inputs]
        + [pl.BlockSpec((1, 3 * channels, channels), tap_of)],
        out_specs=tuple(whole(o.shape) for o in outs),
        scratch_shapes=[
            pltpu.VMEM((images * rows_dev * width, channels), F32),
            pltpu.VMEM((images, rows_dev + 2, width, 3 * channels), BF16),
        ],
        compiler_params=pltpu.CompilerParams(vmem_limit_bytes=48 << 20),
        cost_estimate=pl.CostEstimate(flops=flops, bytes_accessed=moved, transcendentals=0),
        name=kernel.__name__,
    )(info, *inputs, weight)


def weight_grad_kernel(grads, hidden, out, turned, shifted):
    images, padded, width, channels = hidden.shape
    rows_dev = padded - 2
    pixels = images * rows_dev * width
    tap = pl.program_id(0)

    @pl.when(tap == 0)
    def _():
        center = grads[:, 1 : rows_dev + 1]
        turned[...] = center.reshape(pixels, channels).astype(F32).T.astype(BF16)
        for i in range(images):
            for r in range(padded):
                put_shifted(shifted, i, r, hidden[i, r].astype(F32))

    column = pl.multiple_of((tap % 3) * channels, channels)
    rhs = shifted[:, pl.ds(tap // 3, rows_dev), :, pl.ds(column, channels)]
    out[...] = dot(turned[...], rhs.reshape(pixels, channels), 1, 0).astype(BF16)


def weight_grad(grads, hidden):
    images, padded, width, channels = hidden.shape
    pixels = images * (padded - 2) * width

    def whole(shape):
        return pl.BlockSpec(shape, lambda tap: (0,) * len(shape))

    return pl.pallas_call(
        weight_grad_kernel,
        grid=(9,),
        out_shape=jax.ShapeDtypeStruct((channels, 9 * channels), BF16),
        in_specs=[whole(grads.shape), whole(hidden.shape)],
        out_specs=pl.BlockSpec((channels, channels), lambda tap: (0, tap)),
        scratch_shapes=[
            pltpu.VMEM((channels, pixels), BF16),
            pltpu.VMEM(hidden.shape[:3] + (3 * channels,), BF16),
        ],
        compiler_params=pltpu.CompilerParams(vmem_limit_bytes=32 << 20),
        cost_estimate=pl.CostEstimate(
            flops=18 * pixels * channels * channels,
            bytes_accessed=18 * channels * channels,
            transcendentals=0,
        ),
        name="weight_grad",
    )(grads, hidden)


def reduce_kernel(items, chips, has_extra, *refs):
    if has_extra:
        grads, hidden, extra, vector, out, extra_out, vectors, *refs = refs
    else:
        grads, hidden, out, *refs = refs
    (turned, quarter, shifted, part, from_core, chip_sum, from_chip, final, g_send, g_recv, c_send, c_recv,
     z_send, z_recv, f_send, f_recv, *refs) = refs
    _, padded, width, channels = grads.shape
    rows_dev = padded - 2
    pixels = rows_dev * width
    share = channels // (2 * chips)
    slice_rows = share // items
    item, row = lax.axis_index("items"), lax.axis_index("rows")
    chip, core = row // 2, lax.rem(row, 2)
    barrier = pltpu.get_barrier_semaphore()
    peers = [{"items": lax.rem(item + k, items), "rows": row} for k in range(1, items)]
    others = [
        {"items": item, "rows": lax.rem(chip + k, chips) * 2 + core} for k in range(1, chips)
    ]
    sibling = {"items": item, "rows": row + 1 - 2 * core}
    for device in (sibling, *peers, *others):
        pl.semaphore_signal(barrier, inc=1, device_id=device, device_id_type=MESH)

    for r in range(rows_dev):
        block = grads[0, 1 + r].astype(F32).T.astype(BF16)
        for z in range(chips):
            for c in range(2):
                for q in range(items):
                    at = (z * 2 + c) * share + q * slice_rows
                    to = (c * chips + z) * slice_rows
                    turned[q, to : to + slice_rows, r * width : (r + 1) * width] = block[
                        at : at + slice_rows
                    ]
    pl.semaphore_wait(barrier, items + chips - 1)

    def copy(src, dst, send, recv, device):
        return pltpu.make_async_remote_copy(
            src_ref=src,
            dst_ref=dst,
            send_sem=send,
            recv_sem=recv,
            device_id=device,
            device_id_type=MESH,
        )

    started = []

    def go(*args):
        c = copy(*args)
        c.start()
        started.append(c)
        return c

    g_copies = [
        go(
            turned.at[lax.rem(item + k, items)],
            quarter.at[item],
            g_send.at[k],
            g_recv.at[k],
            peers[k - 1],
        )
        for k in range(1, items)
    ]
    if has_extra:
        land, summed, v_land, e_send, e_recv, h_send, h_recv, v_send, v_recv = refs
        e_copies = [
            go(
                extra.at[lax.rem(item + k, items)],
                land.at[item],
                e_send.at[k],
                e_recv.at[k],
                peers[k - 1],
            )
            for k in range(1, items)
        ]
        v_copies = [
            go(vector, v_land.at[item], v_send.at[k], v_recv.at[k], peers[k - 1])
            for k in range(1, items)
        ]
        land[item] = extra[item]
        v_land[item] = vector[...]
    quarter[item] = turned[item]
    for g in range(items):

        def shift(r, carry):
            put_shifted(shifted, g, r, hidden[g, r].astype(F32))
            return carry

        lax.fori_loop(0, padded, shift, 0)
    for c in g_copies:
        c.wait_recv()
    if has_extra:
        for c in e_copies:
            c.wait_recv()
        total = land[0].astype(F32)
        for g in range(1, items):
            total = total + land[g].astype(F32)
        summed[item] = total.astype(BF16)
        h_copies = [
            go(summed.at[item], summed.at[item], h_send.at[k], h_recv.at[k], peers[k - 1])
            for k in range(1, items)
        ]

    half = chips * slice_rows
    core_copies, chip_copies, final_copies = [], [], []

    def compute(a):
        for b in range(3):
            acc = None
            for g in range(items):
                rhs = shifted[g, a : a + rows_dev, :, b * channels : (b + 1) * channels]
                term = dot(quarter[g], rhs.reshape(pixels, channels), 1, 0)
                acc = term if acc is None else acc + term
            part[a, 0, b] = acc[:half].astype(BF16)
            part[a, 1, b] = acc[half:].astype(BF16)
        core_copies.append(
            go(part.at[a, 1 - core], from_core.at[a], c_send.at[a], c_recv.at[a], sibling)
        )

    def over_chips(a):
        core_copies[a].wait_recv()
        for b in range(3):
            both = part[a, core, b].astype(F32) + from_core[a, b].astype(F32)
            for z in range(chips):
                chip_sum[a, z, b] = both[z * slice_rows : (z + 1) * slice_rows].astype(BF16)
        chip_copies.append(
            [
                go(
                    chip_sum.at[a, lax.rem(chip + k, chips)],
                    from_chip.at[a, k],
                    z_send.at[a, k],
                    z_recv.at[a, k],
                    others[k - 1],
                )
                for k in range(1, chips)
            ]
        )

    def over_items(a):
        for c in chip_copies[a]:
            c.wait_recv()
        total = chip_sum[a, chip].astype(F32)
        for k in range(1, chips):
            total = total + from_chip[a, k].astype(F32)
        final[a, item] = total.astype(BF16)
        final_copies.append(
            [
                go(
                    final.at[a, item],
                    final.at[a, item],
                    f_send.at[a, k],
                    f_recv.at[a, k],
                    peers[k - 1],
                )
                for k in range(1, items)
            ]
        )

    def put(a):
        for c in final_copies[a]:
            c.wait_recv()
        for b in range(3):
            rows = jnp.concatenate([final[a, q, b].astype(F32) for q in range(items)], axis=0)
            at = (a * 3 + b) * channels
            out[at : at + channels] = rows.T

    compute(0)
    compute(1)
    over_chips(0)
    compute(2)
    over_chips(1)
    over_chips(2)
    over_items(0)
    over_items(1)
    over_items(2)
    if has_extra:
        for c in h_copies:
            c.wait_recv()
        for q in range(items):
            rows = summed.shape[1]
            extra_out[q * rows : (q + 1) * rows] = summed[q].astype(F32)
        for c in v_copies:
            c.wait_recv()
        vectors[...] = v_land[...]
    put(0)
    put(1)
    put(2)
    for c in started:
        c.wait_send()


def reduce_weight(grads, hidden, identity, extra=None, vector=None):
    items, chips = lax.axis_size("items"), lax.axis_size("rows") // 2
    _, padded, width, channels = grads.shape
    pixels = (padded - 2) * width
    share = channels // (2 * chips)
    rows = share // items
    inputs = [grads, hidden]
    outs = [jax.ShapeDtypeStruct((9 * channels, share), F32)]
    sem = pltpu.SemaphoreType.DMA
    scratch = [
        pltpu.VMEM((items, channels // items, pixels), BF16),
        pltpu.VMEM((items, channels // items, pixels), BF16),
        pltpu.VMEM((items, padded, width, 3 * channels), BF16),
        pltpu.VMEM((3, 2, 3, chips * rows, channels), BF16),
        pltpu.VMEM((3, 3, chips * rows, channels), BF16),
        pltpu.VMEM((3, chips, 3, rows, channels), BF16),
        pltpu.VMEM((3, chips, 3, rows, channels), BF16),
        pltpu.VMEM((3, items, 3, rows, channels), BF16),
        sem((items,)),
        sem((items,)),
        sem((3,)),
        sem((3,)),
        sem((3, chips)),
        sem((3, chips)),
        sem((3, items)),
        sem((3, items)),
    ]
    if extra is not None:
        inputs += [extra.reshape(items, extra.shape[0] // items, extra.shape[1]), vector]
        outs += [
            jax.ShapeDtypeStruct(extra.shape, F32),
            jax.ShapeDtypeStruct((items,) + vector.shape, F32),
        ]
        scratch += [
            pltpu.VMEM(inputs[2].shape, BF16),
            pltpu.VMEM(inputs[2].shape, BF16),
            pltpu.VMEM((items,) + vector.shape, F32),
        ] + [sem((items,))] * 6
    return pl.pallas_call(
        functools.partial(reduce_kernel, items, chips, extra is not None),
        out_shape=tuple(outs),
        in_specs=[WHOLE] * len(inputs),
        out_specs=(WHOLE,) * len(outs),
        scratch_shapes=scratch,
        compiler_params=pltpu.CompilerParams(
            collective_id=identity, has_side_effects=True, vmem_limit_bytes=48 << 20
        ),
        cost_estimate=pl.CostEstimate(
            flops=20_000_000_000, bytes_accessed=40 * channels * channels, transcendentals=0
        ),
        name=f"reduce{identity}",
    )(*inputs)


def project_kernel(info, middle, stats, gain, weight, attn, qkv):
    images, rows_dev, width, channels = middle.shape
    pixels = rows_dev * width
    heads, wide = HEADS, weight.shape[0] // HEADS
    base = info[0, 2]
    for i in range(images):
        average, inverse = norm_of(stats[i], image_count(info, i, channels))
        for r in range(rows_dev):
            inside = window(info, i, base + r, (width, channels))
            value = (middle[i, r] - average) * inverse * inside * gain[...]
            attn[i, r * width : (r + 1) * width] = value.astype(BF16)
        for h in range(heads):
            block = dot(weight[h * wide : (h + 1) * wide], attn[i], 1, 1)
            qkv[i * heads + h] = block.astype(BF16)


def project(info, middle, stats, gain, weight):
    images, rows_dev, width, channels = middle.shape
    pixels = rows_dev * width
    return pl.pallas_call(
        project_kernel,
        out_shape=(
            jax.ShapeDtypeStruct((images, pixels, channels), BF16),
            jax.ShapeDtypeStruct((images * HEADS, weight.shape[0] // HEADS, pixels), BF16),
        ),
        in_specs=[SCALARS, WHOLE, WHOLE, WHOLE, WHOLE],
        out_specs=(WHOLE, WHOLE),
        compiler_params=pltpu.CompilerParams(vmem_limit_bytes=32 << 20),
        name="project",
    )(info, middle, stats, gain, weight)


def unproject_kernel(info, middle, stats, grads, weight, out, out_stats):
    images, rows_dev, width, channels = middle.shape
    wide, pixels = grads.shape[1], grads.shape[2]
    base = info[0, 2]
    for i in range(images):
        average, inverse = norm_of(stats[i], image_count(info, i, channels))
        acc = None
        for h in range(HEADS):
            turned = grads[i * HEADS + h].astype(F32).T.astype(BF16)
            term = dot(turned, weight[h * wide : (h + 1) * wide], 1, 0)
            acc = term if acc is None else acc + term
        one = two = jnp.zeros((width, channels), F32)
        for r in range(rows_dev):
            inside = window(info, i, base + r, (width, channels))
            value = acc[r * width : (r + 1) * width] * inside
            out[i, r] = value
            one = one + value
            two = two + value * ((middle[i, r] - average) * inverse)
        put_stats(out_stats, i, one, two)


def unproject(info, middle, stats, grads, weight):
    images, rows_dev, width, channels = middle.shape
    return pl.pallas_call(
        unproject_kernel,
        out_shape=(
            jax.ShapeDtypeStruct(middle.shape, F32),
            jax.ShapeDtypeStruct(stats.shape, F32),
        ),
        in_specs=[SCALARS, WHOLE, WHOLE, WHOLE, WHOLE],
        out_specs=(WHOLE, WHOLE),
        compiler_params=pltpu.CompilerParams(vmem_limit_bytes=32 << 20),
        name="unproject",
    )(info, middle, stats, grads, weight)


def finish_kernel(info, pre_grad, grad_stats, image, stats, gain, grad_middle, out):
    images, rows_dev, width, channels = image.shape
    base = info[0, 2]
    for i in range(images):
        count = image_count(info, i, channels)
        average, inverse = norm_of(stats[i], count)
        mean, cross = means_of(grad_stats[i], gain[...], count)
        for r in range(rows_dev):
            inside = window(info, i, base + r, (width, channels))
            normal = (image[i, r].astype(F32) - average) * inverse
            term = (pre_grad[i, r] * gain[...] - mean - normal * cross) * inverse
            out[i, r] = (grad_middle[i, r] + term) * inside


def finish(info, pre_grad, grad_stats, image, stats, gain, grad_middle):
    return pl.pallas_call(
        finish_kernel,
        out_shape=jax.ShapeDtypeStruct(image.shape, F32),
        in_specs=[SCALARS] + [WHOLE] * 6,
        out_specs=WHOLE,
        compiler_params=pltpu.CompilerParams(vmem_limit_bytes=32 << 20),
        name="finish",
    )(info, pre_grad, grad_stats, image, stats, gain, grad_middle)


DMA = pltpu.SemaphoreType.DMA


def remote(src, dst, send, recv, device):
    return pltpu.make_async_remote_copy(
        src_ref=src,
        dst_ref=dst,
        send_sem=send,
        recv_sem=recv,
        device_id=device,
        device_id_type=MESH,
    )


class Grid:
    def __init__(self, items, n):
        self.items, self.n = items, n
        self.item, self.me = lax.axis_index("items"), lax.axis_index("rows")

    def row(self, k):
        return {"items": self.item, "rows": lax.rem(self.me + k, self.n)}

    def peer(self, k):
        return {"items": lax.rem(self.item + k, self.items), "rows": self.me}

    def greet(self):
        barrier = pltpu.get_barrier_semaphore()

        def rows(k, carry):
            pl.semaphore_signal(barrier, inc=1, device_id=self.row(k), device_id_type=MESH)
            return carry

        def items(k, carry):
            pl.semaphore_signal(barrier, inc=1, device_id=self.peer(k), device_id_type=MESH)
            return carry

        lax.fori_loop(1, self.n, rows, 0)
        lax.fori_loop(1, self.items, items, 0)

    def met(self):
        pl.semaphore_wait(pltpu.get_barrier_semaphore(), self.n + self.items - 2)

    def loop(self, count, body):
        def step(k, carry):
            body(k)
            return carry

        lax.fori_loop(1, count, step, 0)


class Sums:
    def __init__(self, grid, own, slots, send, recv):
        self.grid, self.own, self.slots, self.send, self.recv = grid, own, slots, send, recv

    def copy(self, k):
        return remote(
            self.own, self.slots.at[self.grid.me], self.send.at[k], self.recv.at[k], self.grid.row(k)
        )

    def start(self):
        self.grid.loop(self.grid.n, lambda k: self.copy(k).start())
        self.slots[self.grid.me] = self.own[...]

    def result(self):
        self.grid.loop(self.grid.n, lambda k: self.copy(k).wait())
        slots = self.slots
        return lax.fori_loop(1, self.grid.n, lambda k, s: s + slots[k], slots[0])


class Edges:
    def __init__(self, grid, field, send, recv):
        self.grid, self.field, self.send, self.recv = grid, field, send, recv

    def copy(self, side):
        last = self.field.shape[0] - 1
        at, to = (last - 1, 0) if side == 0 else (1, last)
        grid = self.grid
        return remote(
            self.field.at[at : at + 1],
            self.field.at[to : to + 1],
            self.send.at[side],
            self.recv.at[side],
            {"items": grid.item, "rows": grid.me + 1 if side == 0 else grid.me - 1},
        )

    def both(self, down, up):
        @pl.when(self.grid.me < self.grid.n - 1)
        def _():
            down()

        @pl.when(self.grid.me > 0)
        def _():
            up()

    def clear(self):
        last = self.field.shape[0] - 1

        @pl.when(self.grid.me == 0)
        def _():
            self.field[0] = jnp.zeros(self.field.shape[1:], self.field.dtype)

        @pl.when(self.grid.me == self.grid.n - 1)
        def _():
            self.field[last] = jnp.zeros(self.field.shape[1:], self.field.dtype)

    def start(self):
        self.both(lambda: self.copy(0).start(), lambda: self.copy(1).start())

    def wait(self):
        self.both(lambda: self.copy(1).wait_recv(), lambda: self.copy(0).wait_recv())
        self.both(lambda: self.copy(0).wait_send(), lambda: self.copy(1).wait_send())


def shift_into(out, r, value):
    width, channels = value.shape
    column = lax.broadcasted_iota(jnp.int32, value.shape, 0)
    left = jnp.where(column == 0, 0.0, pltpu.roll(value, 1, 0))
    right = jnp.where(column == width - 1, 0.0, pltpu.roll(value, width - 1, 0))
    out[r, :, :channels] = left.astype(BF16)
    out[r, :, channels : 2 * channels] = value.astype(BF16)
    out[r, :, 2 * channels :] = right.astype(BF16)


def row_stats(rows, width, channels, row):
    def step(r, carry):
        one, two = row(r)
        return carry[0] + one, carry[1] + two

    zero = jnp.zeros((width, channels), F32)
    one, two = lax.fori_loop(0, rows, step, (zero, zero))
    one = jnp.sum(one, axis=0, keepdims=True)
    two = jnp.sum(two, axis=0, keepdims=True)
    at = lax.broadcasted_iota(jnp.int32, (8, channels), 0)
    return jnp.where(at == 0, one, jnp.where(at == 1, two, 0.0))


def each_row(rows, body):
    def step(r, carry):
        body(r)
        return carry

    lax.fori_loop(0, rows, step, 0)


def conv_taps(shifted, weight, acc, rows_dev):
    pixels, wide = acc.shape[0], shifted.shape[2]
    acc[...] = jnp.zeros_like(acc)

    def step(tap, carry):
        acc[...] += dot(shifted[pl.ds(tap, rows_dev)].reshape(pixels, wide), weight[tap], 1, 0)
        return carry

    lax.fori_loop(0, 3, step, 0)


def forward_kernel(items, n, *refs):
    (info, image, cot, text, embed, gain1, gain2, gain3, w1_in, w2_in, embed_in, text_in, qkv_in, proj_in,
     first_out, mid_out, cot_out, hidden_all, second_all, attn_out, turned_out, qkv_pair, go_pair, text_pair,
     text_cols, stats_out, shifts_out,
     image_v, cot_v, text_v, w1, w2, embed_w, text_w, qkv_w, proj_w, first_v, mid_v, hidden, second, attn,
     turned, qkv, go, text_kv, cols, shifted, acc, own, slots,
     load, sum_send, sum_recv, edge_send, edge_recv, row_send, row_recv, item_send, item_recv) = refs
    grid = Grid(items, n)
    item, me = grid.item, grid.me
    rows_dev, width, channels = image.shape
    pixels = rows_dev * width
    heads, head_dim, wide = HEADS, channels // HEADS, 3 * channels // HEADS
    base = me * rows_dev
    count = (info[0, 0] * info[0, 1]).astype(F32) * (channels // GROUPS)

    def inside(row):
        return window(info, 0, row, (width, channels))

    loads = []

    def fetch(src, dst):
        c = pltpu.make_async_copy(src, dst, load.at[len(loads)])
        c.start()
        loads.append(c)
        return c

    center = slice(1, rows_dev + 1)
    got_image = fetch(image, image_v.at[center])
    got_cot = fetch(cot, cot_v.at[center])
    got_proj = fetch(proj_in, proj_w)
    got_text = fetch(text, text_v)
    got_text_w = fetch(text_in, text_w)
    got_w1 = fetch(w1_in, w1)
    got_embed_w = fetch(embed_in, embed_w)
    got_w2 = fetch(w2_in, w2)
    got_qkv_w = fetch(qkv_in, qkv_w)
    edges = [
        Edges(grid, field, edge_send.at[j], edge_recv.at[j])
        for j, field in enumerate((image_v, cot_v, first_v, mid_v))
    ]
    sums = [Sums(grid, own.at[j], slots.at[j], sum_send.at[j], sum_recv.at[j]) for j in range(3)]
    grid.greet()
    for e in edges:
        e.clear()
    got_image.wait()

    def start_row(r):
        return image_v[1 + r].astype(F32) * inside(base + r)

    def start_stats(r):
        v = start_row(r)
        return v, v * v

    own[0] = row_stats(rows_dev, width, channels, start_stats)
    grid.met()
    sums[0].start()
    edges[0].start()
    got_cot.wait()
    edges[1].start()

    got_text.wait()
    got_text_w.wait()
    text_all = dot(text_v[...], text_w[...], 1, 0).astype(BF16)
    share = text_v.shape[1] // n
    for h in range(heads):
        text_kv[h] = text_all[:, h * 2 * head_dim : (h + 1) * 2 * head_dim]
    for r in range(n):
        cols[r] = text_v[:, r * share : (r + 1) * share]

    def scatter(j, src, dst):
        def copy(k):
            to = lax.rem(me + k, n)
            return remote(src.at[to], dst.at[me], row_send.at[j, k], row_recv.at[j, k], grid.row(k))

        return copy

    kv_copy = scatter(0, text_kv, text_pair)
    col_copy = scatter(1, cols, text_cols.at[item])
    grid.loop(n, lambda k: kv_copy(k).start())
    grid.loop(n, lambda k: col_copy(k).start())
    own_kv = fetch(text_kv.at[me], text_pair.at[me])
    own_col = fetch(cols.at[me], text_cols.at[item, me])

    got_proj.wait()

    def to_grad(r):
        attn[pl.ds(r * width, width)] = (cot_v[1 + r].astype(F32) * inside(base + r)).astype(BF16)

    each_row(rows_dev, to_grad)
    for h in range(heads):
        go[h] = dot(proj_w[h * head_dim : (h + 1) * head_dim], attn[...], 1, 1).astype(BF16)
    go_copy = scatter(2, go, go_pair)
    own_go = fetch(go.at[me], go_pair.at[me])

    stats = sums[0].result()
    stats_out[0] = stats
    average, inverse = norm_of(stats, count)
    edges[0].wait()
    grid.loop(n, lambda k: go_copy(k).start())

    def to_hidden(r):
        ok = inside(base + r - 1)
        value = (image_v[r].astype(F32) * ok - average) * inverse * ok * gain1[...]
        value = value * sigmoid(value) * ok
        shift_into(shifted, r, value)
        hidden[r] = value.astype(BF16)

    each_row(rows_dev + 2, to_hidden)

    def spread(j, src, dst):
        def copy(k):
            return remote(src, dst.at[item], item_send.at[j, k], item_recv.at[j, k], grid.peer(k))

        return copy

    hidden_copy = spread(0, hidden, hidden_all)
    grid.loop(items, lambda k: hidden_copy(k).start())
    own_hidden = fetch(hidden, hidden_all.at[item])
    got_w1.wait()
    conv_taps(shifted, w1, acc, rows_dev)

    def first_row(r):
        value = acc[pl.ds(r * width, width)] * inside(base + r)
        first_v[1 + r] = value
        return value, value * value

    own[1] = row_stats(rows_dev, width, channels, first_row)
    sums[1].start()
    edges[2].start()

    e = embed[...].astype(F32)
    low = (e * sigmoid(e)).astype(BF16)
    got_embed_w.wait()
    shifts_out[...] = dot(low, embed_w[...], 1, 0)
    scale, shift = shifts_out[:, :channels], shifts_out[:, channels:]

    stats = sums[1].result()
    stats_out[1] = stats
    average, inverse = norm_of(stats, count)
    edges[2].wait()
    own_first = fetch(first_v, first_out)

    def to_second(r):
        ok = inside(base + r - 1)
        _, moved = moved_of(first_v[r], ok, average, inverse, gain2[...], scale, shift)
        value = moved * sigmoid(moved) * ok
        shift_into(shifted, r, value)
        second[r] = value.astype(BF16)

    each_row(rows_dev + 2, to_second)
    second_copy = spread(1, second, second_all)
    grid.loop(items, lambda k: second_copy(k).start())
    own_second = fetch(second, second_all.at[item])
    got_w2.wait()
    conv_taps(shifted, w2, acc, rows_dev)

    def middle_row(r):
        value = (image_v[1 + r].astype(F32) + acc[pl.ds(r * width, width)]) * inside(base + r)
        mid_v[1 + r] = value
        return value, value * value

    own[2] = row_stats(rows_dev, width, channels, middle_row)
    sums[2].start()
    edges[3].start()
    own_go.wait()
    edges[1].wait()
    own_cot = fetch(cot_v, cot_out)
    got_qkv_w.wait()
    for j in range(3):
        block = qkv_w[:, j * channels : (j + 1) * channels].astype(F32).T
        turned[j * channels : (j + 1) * channels] = block.astype(BF16)
    own_turned = fetch(turned, turned_out)

    stats = sums[2].result()
    stats_out[2] = stats
    average, inverse = norm_of(stats, count)

    def to_attn(r):
        value = (mid_v[1 + r] - average) * inverse * inside(base + r) * gain3[...]
        attn[pl.ds(r * width, width)] = value.astype(BF16)

    each_row(rows_dev, to_attn)
    own_attn = fetch(attn, attn_out)
    qkv_copy = scatter(3, qkv, qkv_pair)

    def head(k, carry):
        to = lax.rem(me + k, n)
        rows = pl.ds(pl.multiple_of(to * wide, wide), wide)
        qkv[to] = dot(turned[rows], attn[...], 1, 1).astype(BF16)
        return carry

    def send_head(k, carry):
        head(k, carry)
        qkv_copy(k).start()
        return carry

    lax.fori_loop(1, n, send_head, 0)
    head(0, 0)
    own_qkv = fetch(qkv.at[me], qkv_pair.at[me])
    edges[3].wait()
    own_mid = fetch(mid_v, mid_out)

    grid.loop(n, lambda k: kv_copy(k).wait())
    grid.loop(n, lambda k: col_copy(k).wait())
    own_col.wait()
    cols_copy = spread(2, text_cols.at[item], text_cols)
    grid.loop(items, lambda k: cols_copy(k).start())
    grid.loop(n, lambda k: go_copy(k).wait())
    grid.loop(n, lambda k: qkv_copy(k).wait())
    grid.loop(items, lambda k: hidden_copy(k).wait())
    grid.loop(items, lambda k: second_copy(k).wait())
    grid.loop(items, lambda k: cols_copy(k).wait())
    for c in (own_kv, own_hidden, own_first, own_second, own_cot, own_turned, own_attn, own_qkv, own_mid):
        c.wait()


def forward_call(info, image, cot, text, embed, gains, weights, identity):
    items, n = lax.axis_size("items"), lax.axis_size("rows")
    rows_dev, width, channels = image.shape
    pixels = rows_dev * width
    padded = (rows_dev + 2, width, channels)
    tokens, text_width = text.shape
    head_dim = channels // HEADS
    w1, w2, embed_w, text_w, qkv_w, proj_w = weights
    sds = jax.ShapeDtypeStruct
    outs = (
        sds(padded, F32),
        sds(padded, F32),
        sds(padded, BF16),
        sds((items,) + padded, BF16),
        sds((items,) + padded, BF16),
        sds((pixels, channels), BF16),
        sds((3 * channels, channels), BF16),
        sds((n, 3 * head_dim, pixels), BF16),
        sds((n, head_dim, pixels), BF16),
        sds((n, tokens, 2 * head_dim), BF16),
        sds((items, n, tokens, text_width // n), BF16),
        sds((3, 8, channels), F32),
        sds((1, 2 * channels), F32),
    )
    v = pltpu.VMEM
    scratch = [
        v(padded, BF16),
        v(padded, BF16),
        v(text.shape, BF16),
        v(w1.shape, BF16),
        v(w2.shape, BF16),
        v(embed_w.shape, BF16),
        v(text_w.shape, BF16),
        v(qkv_w.shape, BF16),
        v(proj_w.shape, BF16),
        v(padded, F32),
        v(padded, F32),
        v(padded, BF16),
        v(padded, BF16),
        v((pixels, channels), BF16),
        v((3 * channels, channels), BF16),
        v((n, 3 * head_dim, pixels), BF16),
        v((n, head_dim, pixels), BF16),
        v((n, tokens, 2 * head_dim), BF16),
        v((n, tokens, text_width // n), BF16),
        v((rows_dev + 2, width, 3 * channels), BF16),
        v((pixels, channels), F32),
        v((3, 8, channels), F32),
        v((3, n, 8, channels), F32),
        DMA((24,)),
        DMA((3, n)),
        DMA((3, n)),
        DMA((4, 2)),
        DMA((4, 2)),
        DMA((4, n)),
        DMA((4, n)),
        DMA((3, items)),
        DMA((3, items)),
    ]
    return pl.pallas_call(
        functools.partial(forward_kernel, items, n),
        out_shape=outs,
        in_specs=[SCALARS] + [ANYWHERE] * 3 + [WHOLE] * 4 + [ANYWHERE] * 6,
        out_specs=(ANYWHERE,) * 11 + (WHOLE,) * 2,
        scratch_shapes=scratch,
        compiler_params=pltpu.CompilerParams(
            collective_id=identity, has_side_effects=True, vmem_limit_bytes=56 << 20
        ),
        cost_estimate=pl.CostEstimate(
            flops=40 * pixels * channels * channels, bytes_accessed=60 << 20, transcendentals=0
        ),
        name="forward",
    )(info, image, cot, text, embed, *gains, *weights)


def own_shards(
    info, image, embed, text, gain1, conv1_w, embed_w, gain2, conv2_w, gain3, qkv_w, text_w, proj_w,
    cotangent, image_window,
):
    _, rows_dev, width, channels = image.shape
    items, parts = lax.axis_size("items"), lax.axis_size("rows")
    me = lax.axis_index("rows")
    head_dim = channels // HEADS
    pixels = rows_dev * width
    tokens = text.shape[1]
    share = channels // parts
    embed_float = embed.astype(F32)
    embed_low = jax.nn.silu(embed_float).astype(BF16)
    (first, middle, cot, hidden_all, second_all, attn_flat, qkv_turned, qkv_pair, go_pair, text_pair, text_cols,
     stats, shifts) = forward_call(
        info,
        image[0],
        cotangent[0],
        text[0],
        embed,
        (gain1, gain2, gain3),
        (
            conv1_w.reshape(3, 3 * channels, channels),
            conv2_w.reshape(3, 3 * channels, channels),
            embed_w,
            text_w,
            qkv_w,
            proj_w,
        ),
        0,
    )
    stats1, stats2, stats3 = stats[0:1], stats[1:2], stats[2:3]
    attended, qkv_grad_pair, text_grad_pair = attention(
        info[:, :2], qkv_pair, text_pair.reshape(parts * tokens, 2 * head_dim), go_pair, width
    )

    def swap(values):
        return lax.all_to_all(values, "rows", split_axis=0, concat_axis=0, tiled=True)

    qkv_back = swap(qkv_grad_pair)
    heads_out = swap(attended)
    mid = middle[None, 1 : rows_dev + 1]
    attn_grad, sums = unproject(info, mid, stats3, qkv_back, qkv_turned)
    stats4, grad_above, grad_below, text_back = exchange(sums, (attn_grad,), 3, (text_grad_pair,))
    text_all = lax.all_gather(text_back[None], "items", axis=0, tiled=True)
    proj_shaped = proj_w.reshape(HEADS, head_dim, channels)
    grad_proj = (cotangent.astype(F32) * image_window).astype(BF16).reshape(pixels, channels)
    proj_grad = jnp.einsum("pc,hdp->chd", grad_proj, heads_out, preferred_element_type=F32)
    qkv_grad = jnp.einsum(
        "hwdp,pc->hdwc",
        qkv_back.reshape(HEADS, 3, head_dim, pixels),
        attn_flat,
        preferred_element_type=F32,
    )
    side = jnp.concatenate(
        [
            qkv_grad.astype(BF16).reshape(channels, 3 * channels),
            proj_grad.astype(BF16).reshape(channels, channels),
        ],
        axis=1,
    )
    side = lax.psum_scatter(side, "rows", scatter_dimension=0, tiled=True)
    full = jax.ShapeDtypeStruct(image.shape, F32)
    summed = jax.ShapeDtypeStruct((1, 8, channels), F32)
    padded = jax.ShapeDtypeStruct((1, rows_dev + 2, width, channels), BF16)
    own_first = first[None, 1 : rows_dev + 1]
    last = rows_dev + 1
    grad_middle, moved_grad, sums, conv2_grad = conv_call(
        back2_kernel,
        info,
        (attn_grad, grad_above, grad_below, mid, middle[None, :1], middle[None, last:], cotangent,
         cot[None, :1], cot[None, last:], stats3, stats4, gain3, own_first, stats2, gain2, shifts),
        conv2_w,
        (full, full, summed, padded),
        True,
    )
    stats5, moved_above, moved_below = exchange(sums, (moved_grad,), 4)
    pre_grad, sums, conv1_grad = conv_call(
        back1_kernel,
        info,
        (moved_grad, moved_above, moved_below, own_first, first[None, :1], first[None, last:], stats2,
         stats5, gain2, shifts, image, stats1, gain1),
        conv1_w,
        (full, summed, padded),
        True,
    )
    (stats6,) = exchange(sums, (), 5)
    image_grad = finish(info, pre_grad, stats6, image, stats1, gain1, grad_middle)
    projected = jnp.einsum("hdp,hdc->pc", heads_out, proj_shaped, preferred_element_type=F32)
    output = (mid + projected.reshape(image.shape) * image_window).astype(BF16)
    grad_shifts = jnp.concatenate([stats5[:, 1] * gain2, stats5[:, 0]], axis=1).astype(BF16)
    gains = jnp.concatenate(
        [stats6[:, 1], stats5[:, 1] * (1.0 + shifts[:, :channels]), stats4[:, 1]], axis=0
    )
    vector = jnp.concatenate(
        [
            gains,
            grad_shifts.astype(F32).reshape(2, channels),
            embed_low.astype(F32).reshape(-1, channels),
        ],
        axis=0,
    )
    filled = vector.shape[0]
    vector = jnp.pad(vector, ((0, -filled % 8), (0, 0)))
    (conv2_total,) = reduce_weight(conv2_grad, second_all, 6)
    conv1_total, side, vectors = reduce_weight(conv1_grad, hidden_all, 7, side, vector)
    own_text = lax.dynamic_slice_in_dim(text_all, lax.axis_index("items"), 1, 0)
    own_text = lax.dynamic_slice_in_dim(own_text[0], me * tokens, tokens, 2)
    text_shaped = text_w.reshape(text_w.shape[0], HEADS, 2 * head_dim)
    text_grad = jnp.einsum("hkt,chk->tc", own_text, text_shaped, preferred_element_type=F32)
    text_w_grad = jnp.einsum(
        "gtc,ghkt->chk",
        text_cols.reshape(items, parts * tokens, text.shape[2] // parts),
        text_all,
        preferred_element_type=F32,
    )
    embed_grad = jnp.einsum(
        "ik,ck->ic", grad_shifts, embed_w, preferred_element_type=F32
    ) * silu_slope(embed_float)
    all_shifts = vectors[:, 3:5].reshape(items, 2 * channels).astype(BF16)
    all_embed = vectors[:, 5:filled].reshape(items, embed.shape[1]).astype(BF16)
    embed_share = embed_w.shape[0] // parts
    embed_rows = lax.dynamic_slice_in_dim(all_embed, me * embed_share, embed_share, 1)
    embed_w_grad = jnp.einsum("ic,ik->ck", embed_rows, all_shifts, preferred_element_type=F32)
    gains = jnp.sum(vectors[:, :3], axis=0)
    gains = lax.dynamic_slice_in_dim(gains, me * share, share, 1)
    qkv_total = side[:, : 3 * channels].reshape(head_dim, 3, channels)
    qkv_total = jnp.transpose(qkv_total, (2, 1, 0)).reshape(channels, 3 * share)
    return (
        output,
        image_grad,
        embed_grad,
        text_grad[None],
        gains[0],
        conv1_total.reshape(3, 3, channels, share),
        embed_w_grad,
        gains[1],
        conv2_total.reshape(3, 3, channels, share),
        gains[2],
        qkv_total,
        text_w_grad.reshape(-1, 2 * channels),
        side[:, 3 * channels :].T,
    )


def shards(
    image, embed, text, extent, first_norm_gain1, conv1_w, embed_w, second_norm_gain2, conv2_w,
    attention_norm_gain, qkv_w, text_w, proj_w, cotangent,
):
    images, rows_dev, width, channels = image.shape
    parts = lax.axis_size("rows")
    me = lax.axis_index("rows")
    pairs = images * HEADS // parts
    head_dim = channels // HEADS
    pixels = rows_dev * width
    group = max(1, 512 // pixels)
    span = group * pixels
    chunks = parts // group
    tokens = text.shape[1]
    first_row = jnp.full((images, 1), me * rows_dev, jnp.int32)
    info = jnp.concatenate([extent, first_row], axis=1)
    gain1 = first_norm_gain1.reshape(1, channels)
    gain2 = second_norm_gain2.reshape(1, channels)
    gain3 = attention_norm_gain.reshape(1, channels)
    rowpos = me * rows_dev + jnp.arange(rows_dev, dtype=jnp.int32)
    colpos = jnp.arange(width, dtype=jnp.int32)
    inside = (rowpos[None, :, None] < extent[:, 0, None, None]) & (
        colpos[None, None, :] < extent[:, 1, None, None]
    )
    image_window = inside.astype(F32)[..., None]

    items = lax.axis_size("items")
    own_path = (
        images == 1
        and parts == HEADS
        and channels % (16 * items * parts) == 0
        and pixels % 512 == 0
        and tokens % 16 == 0
        and text.shape[2] % (128 * parts) == 0
    )
    if own_path:
        return own_shards(
            info, image, embed, text, gain1, conv1_w, embed_w, gain2, conv2_w, gain3, qkv_w, text_w,
            proj_w, cotangent, image_window,
        )

    embed_float = embed.astype(F32)
    embed_low = jax.nn.silu(embed_float).astype(BF16)
    shifts = jnp.dot(embed_low, embed_w, preferred_element_type=F32)
    qkv_turned = qkv_w.T
    proj_shaped = proj_w.reshape(HEADS, head_dim, channels)

    start = image.astype(F32) * image_window
    zeros = jnp.zeros((images, 6, channels), F32)
    stats0 = jnp.concatenate(
        [
            jnp.sum(start, axis=(1, 2))[:, None],
            jnp.sum(start * start, axis=(1, 2))[:, None],
            zeros,
        ],
        axis=1,
    )
    stats1, image_above, image_below, cot_above, cot_below = exchange(
        stats0, (image, cotangent), 0
    )
    full = jax.ShapeDtypeStruct(image.shape, F32)
    sums = jax.ShapeDtypeStruct((images, 8, channels), F32)
    padded = jax.ShapeDtypeStruct((images, rows_dev + 2, width, channels), BF16)
    first, stats, hidden = conv_call(
        conv1_kernel,
        info,
        (image, image_above, image_below, stats1, gain1),
        conv1_w,
        (full, sums, padded),
        False,
    )
    stats2, first_above, first_below, all_text = exchange(stats, (first,), 1, (text,))
    gathered_text = jnp.moveaxis(all_text, 0, 1).reshape(images, parts * tokens, text.shape[2])
    text_share = text.shape[2] // parts
    text_cols = lax.dynamic_slice_in_dim(gathered_text, me * text_share, text_share, 2)
    text_cols = lax.all_gather(text_cols, "items", axis=0, tiled=True)
    middle, stats, second = conv_call(
        conv2_kernel,
        info,
        (first, first_above, first_below, stats2, gain2, shifts, image),
        conv2_w,
        (full, sums, padded),
        False,
    )
    stats3, mid_above, mid_below = exchange(stats, (middle,), 2)
    attn_flat, qkv_pix = project(info, middle, stats3, gain3, qkv_turned)

    def to_pairs(values):
        wide = values.shape[1]
        moved = lax.all_to_all(values, "rows", split_axis=0, concat_axis=0, tiled=True)
        moved = moved.reshape(chunks, group, pairs, wide, pixels)
        return jnp.transpose(moved, (2, 0, 3, 1, 4)).reshape(pairs, chunks, wide, span)

    def from_pairs(values):
        wide = values.shape[2]
        moved = values.reshape(pairs, chunks, wide, group, pixels)
        moved = jnp.transpose(moved, (1, 3, 0, 2, 4)).reshape(parts * pairs, wide, pixels)
        return lax.all_to_all(moved, "rows", split_axis=0, concat_axis=0, tiled=True)

    qkv_pair = to_pairs(qkv_pix)
    grad_proj = (cotangent.astype(F32) * image_window).astype(BF16).reshape(images, pixels, channels)
    grad_heads = jnp.einsum(
        "ipc,hdc->ihdp", grad_proj, proj_shaped, preferred_element_type=F32
    ).astype(BF16)
    grad_pair = to_pairs(grad_heads.reshape(images * HEADS, head_dim, pixels))
    pair_results = []
    for p in range(pairs):
        pair = me * pairs + p
        item, head = pair // HEADS, pair % HEADS
        weight = lax.dynamic_slice_in_dim(text_w, head * 2 * head_dim, 2 * head_dim, 1)
        own = lax.dynamic_index_in_dim(gathered_text, item, 0, False)
        text_pair = jnp.dot(own, weight, preferred_element_type=F32).astype(BF16)
        pair_extent = lax.dynamic_slice_in_dim(extent, item, 1, 0)
        pair_results.append(attention(pair_extent, qkv_pair[p], text_pair, grad_pair[p], width))
    attended, qkv_grad_pair, text_grad_pair = (jnp.stack(r) for r in zip(*pair_results))
    qkv_back = from_pairs(qkv_grad_pair)
    heads_out = from_pairs(attended).reshape(images, HEADS, head_dim, pixels)

    attn_grad, stats = unproject(info, middle, stats3, qkv_back, qkv_turned)
    stats4, grad_above, grad_below, text_back = exchange(stats, (attn_grad,), 3, (text_grad_pair,))
    text_back = text_back.reshape(images, HEADS, 2 * head_dim, parts * tokens)
    text_all = lax.all_gather(text_back, "items", axis=0, tiled=True)
    proj_grad = jnp.einsum("ipc,ihdp->chd", grad_proj, heads_out, preferred_element_type=F32)
    qkv_grad = jnp.einsum(
        "ihwdp,ipc->hdwc",
        qkv_back.reshape(images, HEADS, 3, head_dim, pixels),
        attn_flat,
        preferred_element_type=F32,
    )
    grad_middle, moved_grad, stats, conv2_grad = conv_call(
        back2_kernel,
        info,
        (attn_grad, grad_above, grad_below, middle, mid_above, mid_below, cotangent, cot_above,
         cot_below, stats3, stats4, gain3, first, stats2, gain2, shifts),
        conv2_w,
        (full, full, sums, padded),
        True,
    )
    stats5, moved_above, moved_below = exchange(stats, (moved_grad,), 4)
    pre_grad, stats, conv1_grad = conv_call(
        back1_kernel,
        info,
        (moved_grad, moved_above, moved_below, first, first_above, first_below, stats2, stats5,
         gain2, shifts, image, stats1, gain1),
        conv1_w,
        (full, sums, padded),
        True,
    )
    (stats6,) = exchange(stats, (), 5)
    image_grad = finish(info, pre_grad, stats6, image, stats1, gain1, grad_middle)

    projected = jnp.einsum(
        "ihdp,hdc->ipc", heads_out, proj_shaped, preferred_element_type=F32
    ).reshape(image.shape)
    output = (middle + projected * image_window).astype(BF16)
    own_text = lax.dynamic_slice_in_dim(text_back, me * tokens, tokens, 3)
    text_shaped = text_w.reshape(text_w.shape[0], HEADS, 2 * head_dim)
    text_grad = jnp.einsum("ihkt,chk->itc", own_text, text_shaped, preferred_element_type=F32)
    text_w_grad = jnp.einsum(
        "gtc,ghkt->chk", text_cols, text_all, preferred_element_type=F32
    ).reshape(text_share, 2 * channels)
    scale_sum = stats5[:, 1] * gain2
    grad_shifts = jnp.concatenate([scale_sum, stats5[:, 0]], axis=1).astype(BF16)
    embed_grad = jnp.einsum(
        "ik,ck->ic", grad_shifts, embed_w, preferred_element_type=F32
    ) * silu_slope(embed_float)
    embed_share = embed_w.shape[0] // parts
    gains = jnp.stack(
        [
            jnp.sum(stats6[:, 1], axis=0),
            jnp.sum(stats5[:, 1] * (1.0 + shifts[:, :channels]), axis=0),
            jnp.sum(stats4[:, 1], axis=0),
        ]
    )
    share = channels // parts
    def total(values):
        return lax.psum(
            lax.psum_scatter(values.astype(BF16), "rows", scatter_dimension=0, tiled=True),
            "items",
        ).astype(F32)

    def kernel_total(values):
        return total(values).T.reshape(3, 3, channels, share)

    conv1_total = kernel_total(weight_grad(conv1_grad, hidden))
    conv2_total = kernel_total(weight_grad(conv2_grad, second))
    by_head = jnp.swapaxes(qkv_grad, 1, 2).reshape(3 * channels, channels)
    qkv_total = total(by_head).T
    proj_total = total(proj_grad.reshape(channels, channels)).T
    gains = lax.psum(gains, "items")
    all_shifts = lax.all_gather(grad_shifts, "items", axis=0, tiled=True)
    embed_rows = lax.dynamic_slice_in_dim(embed_low, me * embed_share, embed_share, 1)
    embed_rows = lax.all_gather(embed_rows, "items", axis=0, tiled=True)
    embed_w_grad = jnp.einsum("ic,ik->ck", embed_rows, all_shifts, preferred_element_type=F32)
    gains = lax.dynamic_slice_in_dim(gains, me * share, share, 1)
    return (
        output,
        image_grad,
        embed_grad,
        text_grad,
        gains[0],
        conv1_total,
        embed_w_grad,
        gains[1],
        conv2_total,
        gains[2],
        qkv_total,
        text_w_grad,
        proj_total,
    )


def solution(mesh):
    in_specs = (
        P("items", "rows", None, None),
        P("items", None),
        P("items", "rows", None),
        P("items", None),
        P(),
        P(),
        P(),
        P(),
        P(),
        P(),
        P(),
        P(),
        P(),
        P("items", "rows", None, None),
    )
    out_specs = (
        P("items", "rows", None, None),
        P("items", "rows", None, None),
        P("items", None),
        P("items", "rows", None),
        P("rows"),
        P(None, None, None, "rows"),
        P("rows", None),
        P("rows"),
        P(None, None, None, "rows"),
        P("rows"),
        P(None, "rows"),
        P("rows", None),
        P(None, "rows"),
    )
    return jax.shard_map(shards, mesh=mesh, in_specs=in_specs, out_specs=out_specs, check_vma=False)
```

profile of v0, /device:TPU:0, one launch (start us, length us, event | category | flops | bytes accessed | tf_op | source)
XLA Modules:
  0.0 383.5 jit_solution(16464554009983488547)
XLA Ops:
  8.0 1.2 pad_add_fusion.refs_0_.info
  9.3 74.7 %forward.1 = (f32[10,64,512]{2,1,0:T(8,128)}, f32[10,64,512]{2,1,0:T(8,128)}, bf16[10,64,512]{2,1,0:T(8,128)(2,1)}, bf16[4,10,64,512]{3,2,1,0:T(8,128)(2,1)}, bf...) custom-call(s32[1,3]{1,0:T(1,128)} %pad_add_fusion.refs_0_.info, ...), custom_call_target="tpu_custom_call" | custom-call | flops 5368709120 | bytes 62914560 | tf_op jit(solution)/shard_map/forward/pallas_call | solution.py:1456
  83.9 62.0 %shard_map.237 = (bf16[8,64,512]{2,1,0:T(8,128)(2,1)}, bf16[8,192,512]{2,1,0:T(8,128)(2,1)}, bf16[128,128]{1,0:T(8,128)(2,1)}) custom-call(s32[1,2]{1,0:T(1,128)} %ext_ref.1, bf16[8,192,512]{2,1,0:T(8,128)(2,1)} %get-tuple-element.49.qkv_ref, bf16[128,128]{1,0:T(8,128)(2,1)} %bitcast.156, bf16[8,64,512]{2,1,0:T(8,128)(2,1)} %get-tuple-element.51.go_ref), custom_call_target="tpu_custom_call" | custom-call | flops 53150220288 | bytes 4194304 | tf_op jit(solution)/shard_map/pallas_call | solution.py:155
  145.9 5.7 %all-to-all-start.1 = ((bf16[8,192,512]{2,1,0:T(8,128)(2,1)}), bf16[8,192,512]{2,1,0:T(8,128)(2,1)S(1)}, u32[]{:S(2)}, u32[]{:S(2)}) async-start(bf16[8,192,512]{2,1,0:T(8,128)(2,1)} %get-tuple-element.54), calls=%async_computation.1 | async-start | bytes 3145728 | tf_op jit(solution)/shard_map/all_to_all | solution.py:1509
  155.4 1.8 slice_bitcast_fusion.3
  157.2 2.8 slice_bitcast_fusion
  160.0 29.4 %all-to-all-done.1.grads = bf16[8,192,512]{2,1,0:T(8,128)(2,1)S(1)} async-done(((bf16[8,192,512]{2,1,0:T(8,128)(2,1)}), bf16[8,192,512]{2,1,0:T(8,128)(2,1)S(1)}, u32[]{:S(2)}, u32[]{:S(2)}) %all-to-all-start.1) | async-done | bytes 1572896 | tf_op jit(solution)/shard_map/all_to_all | solution.py:1509
  189.4 4.1 %all-to-all-start = ((bf16[8,64,512]{2,1,0:T(8,128)(2,1)}), bf16[8,64,512]{2,1,0:T(8,128)(2,1)}, u32[]{:S(2)}, u32[]{:S(2)}) async-start(bf16[8,64,512]{2,1,0:T(8,128)(2,1)} %get-tuple-element.52), calls=%async_computation | async-start | bytes 1048576 | tf_op jit(solution)/shard_map/all_to_all | solution.py:1509
  193.6 1.4 copy-done.3
  195.0 2.1 unproject.1
  197.1 1.0 copy-done.6
  198.7 20.1 %exchange3.1 = (f32[1,8,512]{2,1,0:T(8,128)}, f32[1,1,64,512]{3,2,1,0:T(8,128)}, f32[1,1,64,512]{3,2,1,0:T(8,128)}, bf16[8,128,128]{2,1,0:T(8,128)(2,1)}) custom-call(f32[1,8,512]{2,1,0:T(8,128)} %copy-done.32, f32[1,8,64,512]{3,2,1,0:T(8,128)} %copy-done.6, bf16[128,128]{1,0:T(8,128)(2,1)} %get-tuple-element.58.refs_2_), custom_call_target="tpu_custom_call" | custom-call | flops 6000000000 | bytes 1179648 | tf_op jit(solution)/shard_map/exchange3/pallas_call | solution.py:307
  219.0 0.9 slice_bitcast_fusion.7
  219.9 1.6 multiply_convert_fusion
  221.5 2.4 convolution_convert_fusion.1
  224.0 2.1 copy.56
  226.0 2.4 dot_general.32
  228.4 3.0 fusion.10
  231.4 1.0 fusion.6
  232.4 1.4 copy.55
  234.8 1.6 pad_maximum_fusion
  236.5 1.1 copy-done.7
  237.7 7.7 %back2_kernel.1 = (f32[1,8,64,512]{3,2,1,0:T(8,128)S(1)}, f32[1,8,64,512]{3,2,1,0:T(8,128)S(1)}, f32[1,8,512]{2,1,0:T(8,128)S(1)}, bf16[1,10,64,512]{3,2,1,0:T(8,128)(2,1)S(1)}) custom-call(s32[1,3]{1,0:T(1,128)S(1)} %copy-done.22, f32[1,8,64,512]{3,2,1,0:T(8,128)S(1)} %copy-done.7, f32[1,1,64,512]{3,2,1,0:T(8,128)S(1)} %copy-done.8, ...), custom_call_target="tpu_custom_call" | custom-call | flops 2415919104 | bytes 11870208 | tf_op jit(solution)/shard_map/back2_kernel/pallas_call | solution.py:624
  245.4 1.0 copy-done.4
  246.4 1.0 copy-done.28
  247.4 36.7 %reduce6.1 = f32[4608,64]{1,0:T(8,128)S(1)} custom-call(bf16[1,10,64,512]{3,2,1,0:T(8,128)(2,1)S(1)} %get-tuple-element.79.refs_0_, bf16[4,10,64,512]{3,2,1,0:T(8,128)(2,1)S(1)} %copy-done.27), custom_call_target="tpu_custom_call" | custom-call | flops 20000000000 | bytes 10485760 | tf_op jit(solution)/shard_map/reduce6/pallas_call | solution.py:917
  284.1 1.7 copy.60
  285.9 8.4 %exchange4.1 = (f32[1,8,512]{2,1,0:T(8,128)}, f32[1,1,64,512]{3,2,1,0:T(8,128)}, f32[1,1,64,512]{3,2,1,0:T(8,128)}) custom-call(f32[1,8,512]{2,1,0:T(8,128)} %copy-done.31, f32[1,8,64,512]{3,2,1,0:T(8,128)} %copy-done.28), custom_call_target="tpu_custom_call" | custom-call | flops 6000000000 | bytes 655360 | tf_op jit(solution)/shard_map/exchange4/pallas_call | solution.py:307
  294.3 0.7 slice.94
  295.0 0.7 convert_bitcast_fusion
  295.9 0.7 copy-done.26
  296.6 1.2 copy-done.29
  297.9 0.9 copy-done.35
  298.8 0.9 copy-done.36
  299.7 7.0 %back1_kernel.1 = (f32[1,8,64,512]{3,2,1,0:T(8,128)S(1)}, f32[1,8,512]{2,1,0:T(8,128)S(1)}, bf16[1,10,64,512]{3,2,1,0:T(8,128)(2,1)S(1)}) custom-call(s32[1,3]{1,0:T(1,128)S(1)} %copy-done.23, f32[1,8,64,512]{3,2,1,0:T(8,128)S(1)} %copy-done.29, f32[1,1,64,512]{3,2,1,0:T(8,128)S(1)} %copy-done.35, f32[1,1,64,512]{3,2,1,0:T(8,128)S(1)} %copy-done.36, ...), custom_call_target="tpu_custom_call" | custom-call | flops 2415919104 | bytes 9641984 | tf_op jit(solution)/shard_map/back1_kernel/pallas_call | solution.py:624
  306.7 0.8 copy-done.33
  308.1 8.8 %exchange5.1.grad_stats = f32[1,8,512]{2,1,0:T(8,128)} custom-call(f32[1,8,512]{2,1,0:T(8,128)} %copy-done.37), custom_call_target="tpu_custom_call" | custom-call | flops 6000000000 | bytes 131072 | tf_op jit(solution)/shard_map/exchange5/pallas_call | solution.py:307
  317.7 2.4 finish.1
  320.1 0.7 slice_bitcast_fusion.11
  320.9 0.7 bitcast_multiply_fusion
  321.8 4.0 %convolution_multiply_fusion = f32[1,2048]{1,0:T(1,128)} fusion(bf16[1024,1]{0,1:T(2,128)(2,1)S(1)} %reshape.217, bf16[2048,1024]{1,0:T(8,128)(2,1)} %refs_10_.1, bf16[1,2048]{1,0:T(2,128)(2,1)S(1)} %copy-done.41), kind=kOutput, calls=%fused_computation.4 | convolution fusion | flops 4212736 | bytes 4208640 | tf_op jit(solution)/shard_map/ik,ck->ic/dot_general | solution.py:1588
  325.8 2.7 convolution_bitcast_fusion
  328.5 4.4 %fusion.3 = f32[1,16,2048]{2,1,0:T(8,128)} fusion(bf16[4,8,128,128]{3,2,1,0:T(8,128)(2,1)} %bitcast.147, s32[]{:T(128)S(6)} %select_n.17, s32[]{:T(128)S(6)} %select_n.19, bf16[2048,1024]{1,0:T(8,128)(2,1)} %refs_11_.1), kind=kOutput, calls=%fused_computation.3 | convolution fusion | flops 67108864 | bytes 4587528 | tf_op jit(solution)/shard_map/hkt,chk->tc/dot_general | solution.py:1581
  332.9 0.9 copy-done.30
  333.8 36.7 %reduce7.1 = (f32[4608,64]{1,0:T(8,128)S(1)}, f32[64,2048]{1,0:T(8,128)S(1)}, f32[4,16,512]{2,1,0:T(8,128)S(1)}) custom-call(bf16[1,10,64,512]{3,2,1,0:T(8,128)(2,1)S(1)} %copy-done.34, bf16[4,10,64,512]{3,2,1,0:T(8,128)(2,1)} %get-tuple-element.75.refs_1_, bf16[4,16,2048]{2,1,0:T(8,128)(2,1)S(1)} %bitcast.137, f32[16,512]{1,0:T(8,128)S(1)} %pad.4.refs_3_), custom_call_target="tpu_custom_call" | custom-call | flops 20000000000 | bytes 10485760 | tf_op jit(solution)/shard_map/reduce7/pallas_call | solution.py:917
  371.3 1.7 copy.59
  373.9 0.9 copy.57
  374.8 1.3 fusion.16
  (116 shorter events, 9.1 us)
Async XLA Ops:
  145.9 5.7 %copy-start.40 = (bf16[1,2048]{1,0:T(2,128)(2,1)S(1)}, bf16[1,2048]{1,0:T(2,128)(2,1)}, u32[]{:S(2)}) copy-start(bf16[1,2048]{1,0:T(2,128)(2,1)} %refs_4_.1) | copy-start | bytes 12292
  145.9 6.3 %copy-start.44 = (s32[1,2]{1,0:T(1,128)S(1)}, s32[1,2]{1,0:T(1,128)}, u32[]{:S(2)}) copy-start(s32[1,2]{1,0:T(1,128)} %ext_ref.1) | copy-start | bytes 28
  145.9 8.9 %copy-start.42 = (f32[3,8,512]{2,1,0:T(8,128)S(1)}, f32[3,8,512]{2,1,0:T(8,128)}, u32[]{:S(2)}) copy-start(f32[3,8,512]{2,1,0:T(8,128)} %get-tuple-element.53) | copy-start | bytes 147460
  145.9 43.5 %all-to-all-start.1 = ((bf16[8,192,512]{2,1,0:T(8,128)(2,1)}), bf16[8,192,512]{2,1,0:T(8,128)(2,1)S(1)}, u32[]{:S(2)}, u32[]{:S(2)}) async-start(bf16[8,192,512]{2,1,0:T(8,128)(2,1)} %get-tuple-element.54), calls=%async_computation.1 | async-start | bytes 3145728 | tf_op jit(solution)/shard_map/all_to_all | solution.py:1509
  157.2 36.4 %copy-start.21 = (s32[1,3]{1,0:T(1,128)S(1)}, s32[1,3]{1,0:T(1,128)}, u32[]{:S(2)}) copy-start(s32[1,3]{1,0:T(1,128)} %pad_add_fusion.refs_0_.info) | copy-start | bytes 40
  189.4 32.1 %all-to-all-start = ((bf16[8,64,512]{2,1,0:T(8,128)(2,1)}), bf16[8,64,512]{2,1,0:T(8,128)(2,1)}, u32[]{:S(2)}, u32[]{:S(2)}) async-start(bf16[8,64,512]{2,1,0:T(8,128)(2,1)} %get-tuple-element.52), calls=%async_computation | async-start | bytes 1048576 | tf_op jit(solution)/shard_map/all_to_all | solution.py:1509
  193.6 132.2 %all-gather.3.cloned.1.call-start = ((), (), s32[]{:S(2)}) async-start(), calls=%async_computation.4 | async-start | bytes 1310720 | tf_op jit(solution)/shard_map/all_gather | solution.py:1516
  193.6 1.4 copy-start.3
  197.1 1.0 copy-start.6
  198.7 21.2 %copy-start = (bf16[1,8,64,512]{3,2,1,0:T(8,128)(2,1)S(1)}, bf16[1,8,64,512]{3,2,1,0:T(8,128)(2,1)}, u32[]{:S(2)}) copy-start(bf16[1,8,64,512]{3,2,1,0:T(8,128)(2,1)} %cot.1) | copy-start | bytes 1572868
  218.8 114.1 %reduce-scatter.2.cloned.1.call-start = ((), (), s32[]{:S(2)}) async-start(), calls=%async_computation.3 | async-start | bytes 2359296 | tf_op jit(solution)/shard_map/reduce_scatter | solution.py:1533
  228.4 3.0 copy-start.45
  233.8 1.0 copy-start.38
  236.4 1.2 copy-start.7
  236.4 1.2 copy-start.8
  236.4 1.3 copy-start.9
  236.4 1.3 copy-start.13
  236.5 1.3 copy-start.15
  236.5 1.2 copy-start.17
  236.5 1.2 copy-start.19
  236.5 1.2 copy-start.22
  236.5 1.2 copy-start.25
  237.7 9.6 %copy-start.27 = (bf16[4,10,64,512]{3,2,1,0:T(8,128)(2,1)S(1)}, bf16[4,10,64,512]{3,2,1,0:T(8,128)(2,1)}, u32[]{:S(2)}) copy-start(bf16[4,10,64,512]{3,2,1,0:T(8,128)(2,1)} %get-tuple-element.80.refs_1_) | copy-start | bytes 7864324
  245.4 1.0 copy-start.4
  246.4 1.0 copy-start.28
  247.4 36.7 %copy-start.31 = (f32[1,8,512]{2,1,0:T(8,128)}, f32[1,8,512]{2,1,0:T(8,128)S(1)}, u32[]{:S(2)}) copy-start(f32[1,8,512]{2,1,0:T(8,128)S(1)} %get-tuple-element.66.refs_0_) | copy-start | bytes 49156
  285.8 10.0 %copy-start.1 = (f32[1,8,64,512]{3,2,1,0:T(8,128)S(1)}, f32[1,8,64,512]{3,2,1,0:T(8,128)}, u32[]{:S(2)}) copy-start(f32[1,8,64,512]{3,2,1,0:T(8,128)} %get-tuple-element.151.first) | copy-start | bytes 3145732
  285.8 10.0 %copy-start.2 = (bf16[1,8,64,512]{3,2,1,0:T(8,128)(2,1)S(1)}, bf16[1,8,64,512]{3,2,1,0:T(8,128)(2,1)}, u32[]{:S(2)}) copy-start(bf16[1,8,64,512]{3,2,1,0:T(8,128)(2,1)} %image.3) | copy-start | bytes 1572868
  285.8 10.1 %copy-start.10 = (f32[1,1,64,512]{3,2,1,0:T(8,128)S(1)}, f32[1,1,64,512]{3,2,1,0:T(8,128)}, u32[]{:S(2)}) copy-start(f32[1,1,64,512]{3,2,1,0:T(8,128)} %get-tuple-element.135.first_below) | copy-start | bytes 393220
  285.8 10.1 %copy-start.11 = (f32[1,1,64,512]{3,2,1,0:T(8,128)S(1)}, f32[1,1,64,512]{3,2,1,0:T(8,128)}, u32[]{:S(2)}) copy-start(f32[1,1,64,512]{3,2,1,0:T(8,128)} %get-tuple-element.136.first_above) | copy-start | bytes 393220
  285.8 10.1 %copy-start.12 = (f32[1,8,512]{2,1,0:T(8,128)S(1)}, f32[1,8,512]{2,1,0:T(8,128)}, u32[]{:S(2)}) copy-start(f32[1,8,512]{2,1,0:T(8,128)} %get-tuple-element.141.image_stats.stats) | copy-start | bytes 49156
  285.8 10.1 %copy-start.14 = (f32[1,8,512]{2,1,0:T(8,128)S(1)}, f32[1,8,512]{2,1,0:T(8,128)}, u32[]{:S(2)}) copy-start(f32[1,8,512]{2,1,0:T(8,128)} %get-tuple-element.142.first_stats) | copy-start | bytes 49156
  285.8 10.1 %copy-start.18 = (f32[512]{0:T(512)S(1)}, f32[512]{0:T(512)}, u32[]{:S(2)}) copy-start(f32[512]{0:T(512)} %param.21) | copy-start | bytes 6148
  285.8 10.1 %copy-start.20 = (f32[1,1024]{1,0:T(1,128)S(1)}, f32[1,1024]{1,0:T(1,128)}, u32[]{:S(2)}) copy-start(f32[1,1024]{1,0:T(1,128)} %get-tuple-element.64.shifts) | copy-start | bytes 12292
  285.8 10.1 %copy-start.23 = (s32[1,3]{1,0:T(1,128)S(1)}, s32[1,3]{1,0:T(1,128)}, u32[]{:S(2)}) copy-start(s32[1,3]{1,0:T(1,128)} %pad_add_fusion.refs_0_.info) | copy-start | bytes 40
  285.9 10.1 %copy-start.24 = (f32[512]{0:T(512)S(1)}, f32[512]{0:T(512)}, u32[]{:S(2)}) copy-start(f32[512]{0:T(512)} %param.18) | copy-start | bytes 6148
  295.9 0.7 copy-start.26
  296.6 1.2 copy-start.29
  297.9 0.9 copy-start.35
  298.8 0.9 copy-start.36
  306.7 0.8 copy-start.33
  308.1 8.8 %copy-start.5 = (f32[1,8,64,512]{3,2,1,0:T(8,128)S(1)}, f32[1,8,64,512]{3,2,1,0:T(8,128)}, u32[]{:S(2)}) copy-start(f32[1,8,64,512]{3,2,1,0:T(8,128)} %copy-done.4) | copy-start | bytes 3145732
  308.1 13.5 %copy-start.43 = (f32[4,512]{1,0:T(4,128)S(1)}, f32[4,512]{1,0:T(4,128)}, u32[]{:S(2)}) copy-start(f32[4,512]{1,0:T(4,128)} %reshape.213) | copy-start | bytes 24580
  308.1 13.6 %copy-start.41 = (bf16[1,2048]{1,0:T(2,128)(2,1)S(1)}, bf16[1,2048]{1,0:T(2,128)(2,1)}, u32[]{:S(2)}) copy-start(bf16[1,2048]{1,0:T(2,128)(2,1)} %refs_4_.1) | copy-start | bytes 12292
  317.0 0.7 copy-start.16
  321.7 4.0 %copy-start.39 = (bf16[4,8,16,256]{3,2,1,0:T(8,128)(2,1)S(1)}, bf16[4,8,16,256]{3,2,1,0:T(8,128)(2,1)}, u32[]{:S(2)}) copy-start(bf16[4,8,16,256]{3,2,1,0:T(8,128)(2,1)} %get-tuple-element.82) | copy-start | bytes 786436
  328.5 4.4 %copy-start.34 = (bf16[1,10,64,512]{3,2,1,0:T(8,128)(2,1)S(1)}, bf16[1,10,64,512]{3,2,1,0:T(8,128)(2,1)}, u32[]{:S(2)}) copy-start(bf16[1,10,64,512]{3,2,1,0:T(8,128)(2,1)} %copy-done.33) | copy-start | bytes 1966084
  332.9 1.0 copy-start.30
  (2 other events, 1.2 us)
Sparse Core Ops, SparseCore 0:
  218.9 25.4 all-gather.2
Sparse Core Ops, SparseCore 1:
  236.6 38.4 reduce-scatter.1
where the time goes:
time: 385 us; the launch traced here: 384 us
  Pallas kernels  266 us (69%)
  local copies, waits for them, and re-layouts  35.4 us (9%)
  waiting for transfers between devices  29.4 us (8%)
  matrix products  18.9 us (5%)
  between operations  16 us (4%)
  starting transfers between devices  10.1 us (3%)
  other arithmetic  7.29 us (2%)
    pallas_call x1, Pallas kernels, forward_call(): pl.pallas_call(functools.partial(forward_kernel, items, n), out_shape=out...  74.7 us
    pallas_call x2, Pallas kernels, reduce_weight(): pl.pallas_call(functools.partial(reduce_kernel, items, chips, extra is no...  73.4 us
    pallas_call x1, Pallas kernels, attention(): pl.pallas_call(functools.partial(attention_kernel, width, step, bq), out_...  62 us
    pallas_call x3, Pallas kernels, exchange(): pl.pallas_call(functools.partial(exchange_kernel, n, count, gathers), out...  37.3 us
    all_to_all x2, waiting for transfers between devices, swap(): lax.all_to_all(values, 'rows', split_axis=0, concat_axis=0, tiled=True)  29.4 us
    unnamed x99, local copies, waits for them, and re-layouts  17.5 us
    pallas_call x2, Pallas kernels, conv_call(): pl.pallas_call(kernel, grid=(3,), out_shape=tuple(outs), in_specs=[SCALAR...  14.7 us
    all_to_all x2, starting transfers between devices, swap(): lax.all_to_all(values, 'rows', split_axis=0, concat_axis=0, tiled=True)  9.8 us
  transfers between devices with their start and end apart: 4, of which 1 were waited for; matrix products, arithmetic and copies ran while one was open for 11% of the time, Pallas kernels for 24%

commit v1 on v0

--- a/solution.py
+++ b/solution.py
@@ -139,8 +139,8 @@
         dqkv_ref[c, 2 * d:, :] = dvt[:, at].astype(BF16)
         return carry
     lax.fori_loop(0, chunks, finish, 0)
-    dtext_ref[:d, :] = (dkt[:, pix:] * (d ** -0.5)).astype(BF16)
-    dtext_ref[d:, :] = dvt[:, pix:].astype(BF16)
+    dtext_ref[:, :d] = (dkt[:, pix:] * (d ** -0.5)).T.astype(BF16)
+    dtext_ref[:, d:] = dvt[:, pix:].T.astype(BF16)
 
 def attention(ext, qkv, text, go, width):
     chunks, wide, span = qkv.shape
@@ -157,7 +157,7 @@
         out_shape=(
             jax.ShapeDtypeStruct(go.shape, BF16),
             jax.ShapeDtypeStruct(qkv.shape, BF16),
-            jax.ShapeDtypeStruct((2 * d, tlen), BF16),
+            jax.ShapeDtypeStruct((tlen, 2 * d), BF16),
         ),
         in_specs=[pl.BlockSpec(memory_space=pltpu.SMEM), vm, vm, vm],
         out_specs=(vm, vm, vm),
@@ -683,251 +683,6 @@
         ),
         name="weight_grad",
     )(grads, hidden)
-
-
-def reduce_kernel(items, chips, has_extra, *refs):
-    if has_extra:
-        grads, hidden, extra, vector, out, extra_out, vectors, *refs = refs
-    else:
-        grads, hidden, out, *refs = refs
-    (turned, quarter, shifted, part, from_core, chip_sum, from_chip, final, g_send, g_recv, c_send, c_recv,
-     z_send, z_recv, f_send, f_recv, *refs) = refs
-    _, padded, width, channels = grads.shape
-    rows_dev = padded - 2
-    pixels = rows_dev * width
-    share = channels // (2 * chips)
-    slice_rows = share // items
-    item, row = lax.axis_index("items"), lax.axis_index("rows")
-    chip, core = row // 2, lax.rem(row, 2)
-    barrier = pltpu.get_barrier_semaphore()
-    peers = [{"items": lax.rem(item + k, items), "rows": row} for k in range(1, items)]
-    others = [
-        {"items": item, "rows": lax.rem(chip + k, chips) * 2 + core} for k in range(1, chips)
-    ]
-    sibling = {"items": item, "rows": row + 1 - 2 * core}
-    for device in (sibling, *peers, *others):
-        pl.semaphore_signal(barrier, inc=1, device_id=device, device_id_type=MESH)
-
-    for r in range(rows_dev):
-        block = grads[0, 1 + r].astype(F32).T.astype(BF16)
-        for z in range(chips):
-            for c in range(2):
-                for q in range(items):
-                    at = (z * 2 + c) * share + q * slice_rows
-                    to = (c * chips + z) * slice_rows
-                    turned[q, to : to + slice_rows, r * width : (r + 1) * width] = block[
-                        at : at + slice_rows
-                    ]
-    pl.semaphore_wait(barrier, items + chips - 1)
-
-    def copy(src, dst, send, recv, device):
-        return pltpu.make_async_remote_copy(
-            src_ref=src,
-            dst_ref=dst,
-            send_sem=send,
-            recv_sem=recv,
-            device_id=device,
-            device_id_type=MESH,
-        )
-
-    started = []
-
-    def go(*args):
-        c = copy(*args)
-        c.start()
-        started.append(c)
-        return c
-
-    g_copies = [
-        go(
-            turned.at[lax.rem(item + k, items)],
-            quarter.at[item],
-            g_send.at[k],
-            g_recv.at[k],
-            peers[k - 1],
-        )
-        for k in range(1, items)
-    ]
-    if has_extra:
-        land, summed, v_land, e_send, e_recv, h_send, h_recv, v_send, v_recv = refs
-        e_copies = [
-            go(
-                extra.at[lax.rem(item + k, items)],
-                land.at[item],
-                e_send.at[k],
-                e_recv.at[k],
-                peers[k - 1],
-            )
-            for k in range(1, items)
-        ]
-        v_copies = [
-            go(vector, v_land.at[item], v_send.at[k], v_recv.at[k], peers[k - 1])
-            for k in range(1, items)
-        ]
-        land[item] = extra[item]
-        v_land[item] = vector[...]
-    quarter[item] = turned[item]
-    for g in range(items):
-
-        def shift(r, carry):
-            put_shifted(shifted, g, r, hidden[g, r].astype(F32))
-            return carry
-
-        lax.fori_loop(0, padded, shift, 0)
-    for c in g_copies:
-        c.wait_recv()
-    if has_extra:
-        for c in e_copies:
-            c.wait_recv()
-        total = land[0].astype(F32)
-        for g in range(1, items):
-            total = total + land[g].astype(F32)
-        summed[item] = total.astype(BF16)
-        h_copies = [
-            go(summed.at[item], summed.at[item], h_send.at[k], h_recv.at[k], peers[k - 1])
-            for k in range(1, items)
-        ]
-
-    half = chips * slice_rows
-    core_copies, chip_copies, final_copies = [], [], []
-
-    def compute(a):
-        for b in range(3):
-            acc = None
-            for g in range(items):
-                rhs = shifted[g, a : a + rows_dev, :, b * channels : (b + 1) * channels]
-                term = dot(quarter[g], rhs.reshape(pixels, channels), 1, 0)
-                acc = term if acc is None else acc + term
-            part[a, 0, b] = acc[:half].astype(BF16)
-            part[a, 1, b] = acc[half:].astype(BF16)
-        core_copies.append(
-            go(part.at[a, 1 - core], from_core.at[a], c_send.at[a], c_recv.at[a], sibling)
-        )
-
-    def over_chips(a):
-        core_copies[a].wait_recv()
-        for b in range(3):
-            both = part[a, core, b].astype(F32) + from_core[a, b].astype(F32)
-            for z in range(chips):
-                chip_sum[a, z, b] = both[z * slice_rows : (z + 1) * slice_rows].astype(BF16)
-        chip_copies.append(
-            [
-                go(
-                    chip_sum.at[a, lax.rem(chip + k, chips)],
-                    from_chip.at[a, k],
-                    z_send.at[a, k],
-                    z_recv.at[a, k],
-                    others[k - 1],
-                )
-                for k in range(1, chips)
-            ]
-        )
-
-    def over_items(a):
-        for c in chip_copies[a]:
-            c.wait_recv()
-        total = chip_sum[a, chip].astype(F32)
-        for k in range(1, chips):
-            total = total + from_chip[a, k].astype(F32)
-        final[a, item] = total.astype(BF16)
-        final_copies.append(
-            [
-                go(
-                    final.at[a, item],
-                    final.at[a, item],
-                    f_send.at[a, k],
-                    f_recv.at[a, k],
-                    peers[k - 1],
-                )
-                for k in range(1, items)
-            ]
-        )
-
-    def put(a):
-        for c in final_copies[a]:
-            c.wait_recv()
-        for b in range(3):
-            rows = jnp.concatenate([final[a, q, b].astype(F32) for q in range(items)], axis=0)
-            at = (a * 3 + b) * channels
-            out[at : at + channels] = rows.T
-
-    compute(0)
-    compute(1)
-    over_chips(0)
-    compute(2)
-    over_chips(1)
-    over_chips(2)
-    over_items(0)
-    over_items(1)
-    over_items(2)
-    if has_extra:
-        for c in h_copies:
-            c.wait_recv()
-        for q in range(items):
-            rows = summed.shape[1]
-            extra_out[q * rows : (q + 1) * rows] = summed[q].astype(F32)
-        for c in v_copies:
-            c.wait_recv()
-        vectors[...] = v_land[...]
-    put(0)
-    put(1)
-    put(2)
-    for c in started:
-        c.wait_send()
-
-
-def reduce_weight(grads, hidden, identity, extra=None, vector=None):
-    items, chips = lax.axis_size("items"), lax.axis_size("rows") // 2
-    _, padded, width, channels = grads.shape
-    pixels = (padded - 2) * width
-    share = channels // (2 * chips)
-    rows = share // items
-    inputs = [grads, hidden]
-    outs = [jax.ShapeDtypeStruct((9 * channels, share), F32)]
-    sem = pltpu.SemaphoreType.DMA
-    scratch = [
-        pltpu.VMEM((items, channels // items, pixels), BF16),
-        pltpu.VMEM((items, channels // items, pixels), BF16),
-        pltpu.VMEM((items, padded, width, 3 * channels), BF16),
-        pltpu.VMEM((3, 2, 3, chips * rows, channels), BF16),
-        pltpu.VMEM((3, 3, chips * rows, channels), BF16),
-        pltpu.VMEM((3, chips, 3, rows, channels), BF16),
-        pltpu.VMEM((3, chips, 3, rows, channels), BF16),
-        pltpu.VMEM((3, items, 3, rows, channels), BF16),
-        sem((items,)),
-        sem((items,)),
-        sem((3,)),
-        sem((3,)),
-        sem((3, chips)),
-        sem((3, chips)),
-        sem((3, items)),
-        sem((3, items)),
-    ]
-    if extra is not None:
-        inputs += [extra.reshape(items, extra.shape[0] // items, extra.shape[1]), vector]
-        outs += [
-            jax.ShapeDtypeStruct(extra.shape, F32),
-            jax.ShapeDtypeStruct((items,) + vector.shape, F32),
-        ]
-        scratch += [
-            pltpu.VMEM(inputs[2].shape, BF16),
-            pltpu.VMEM(inputs[2].shape, BF16),
-            pltpu.VMEM((items,) + vector.shape, F32),
-        ] + [sem((items,))] * 6
-    return pl.pallas_call(
-        functools.partial(reduce_kernel, items, chips, extra is not None),
-        out_shape=tuple(outs),
-        in_specs=[WHOLE] * len(inputs),
-        out_specs=(WHOLE,) * len(outs),
-        scratch_shapes=scratch,
-        compiler_params=pltpu.CompilerParams(
-            collective_id=identity, has_side_effects=True, vmem_limit_bytes=48 << 20
-        ),
-        cost_estimate=pl.CostEstimate(
-            flops=20_000_000_000, bytes_accessed=40 * channels * channels, transcendentals=0
-        ),
-        name=f"reduce{identity}",
-    )(*inputs)
 
 
 def project_kernel(info, middle, stats, gain, weight, attn, qkv):
@@ -1469,19 +1224,677 @@
     )(info, image, cot, text, embed, *gains, *weights)
 
 
+class KernelSum:
+    def __init__(self, grid, turned, quarter, part, from_core, chip_sum, from_chip, final, item_sems, core_sems,
+                 chip_sems, final_sems):
+        self.grid = grid
+        self.turned, self.quarter, self.part, self.from_core = turned, quarter, part, from_core
+        self.chip_sum, self.from_chip, self.final = chip_sum, from_chip, final
+        self.item_sems, self.core_sems = item_sems, core_sems
+        self.chip_sems, self.final_sems = chip_sems, final_sems
+        self.chips = grid.n // 2
+        self.chip, self.core = grid.me // 2, lax.rem(grid.me, 2)
+
+    def grads_copy(self, k):
+        grid = self.grid
+        send, recv = self.item_sems
+        to = lax.rem(grid.item + k, grid.items)
+        return remote(
+            self.turned.at[to], self.quarter.at[grid.item], send.at[k], recv.at[k], grid.peer(k)
+        )
+
+    def send_grads(self, shifted):
+        grid, chips = self.grid, self.chips
+        rows_dev, width, channels = shifted.shape[0] - 2, shifted.shape[1], shifted.shape[2] // 3
+        center = shifted[1 : rows_dev + 1, :, channels : 2 * channels]
+        block = center.reshape(rows_dev * width, channels).astype(F32).T.astype(BF16)
+        share = channels // grid.n
+        rows = share // grid.items
+        for z in range(chips):
+            for c in range(2):
+                for q in range(grid.items):
+                    at = (z * 2 + c) * share + q * rows
+                    to = (c * chips + z) * rows
+                    self.turned[q, to : to + rows] = block[at : at + rows]
+        grid.loop(grid.items, lambda k: self.grads_copy(k).start())
+        self.quarter[grid.item] = self.turned[grid.item]
+
+    def wait_grads(self):
+        self.grid.loop(self.grid.items, lambda k: self.grads_copy(k).wait())
+
+    def core_copy(self, a):
+        send, recv = self.core_sems
+        grid = self.grid
+        return remote(
+            self.part.at[a, 1 - self.core],
+            self.from_core.at[a],
+            send.at[a],
+            recv.at[a],
+            {"items": grid.item, "rows": grid.me + 1 - 2 * self.core},
+        )
+
+    def compute(self, a, shifted):
+        items, padded, width, wide = shifted.shape
+        rows_dev, channels = padded - 2, wide // 3
+        half = self.turned.shape[1] // 2
+        for b in range(3):
+            acc = None
+            for g in range(items):
+                rhs = shifted[g, a : a + rows_dev, :, b * channels : (b + 1) * channels]
+                term = dot(self.quarter[g], rhs.reshape(rows_dev * width, channels), 1, 0)
+                acc = term if acc is None else acc + term
+            self.part[a, 0, b] = acc[:half].astype(BF16)
+            self.part[a, 1, b] = acc[half:].astype(BF16)
+        self.core_copy(a).start()
+
+    def chip_copy(self, a, k):
+        send, recv = self.chip_sems
+        grid = self.grid
+        to = lax.rem(self.chip + k, self.chips)
+        return remote(
+            self.chip_sum.at[a, to],
+            self.from_chip.at[a, k],
+            send.at[a, k],
+            recv.at[a, k],
+            {"items": grid.item, "rows": to * 2 + self.core},
+        )
+
+    def over_chips(self, a):
+        self.core_copy(a).wait()
+        rows = self.chip_sum.shape[3]
+        for b in range(3):
+            both = self.part[a, self.core, b].astype(F32) + self.from_core[a, b].astype(F32)
+            for z in range(self.chips):
+                self.chip_sum[a, z, b] = both[z * rows : (z + 1) * rows].astype(BF16)
+        for k in range(1, self.chips):
+            self.chip_copy(a, k).start()
+
+    def final_copy(self, a, k):
+        send, recv = self.final_sems
+        mine = self.final.at[a, self.grid.item]
+        return remote(mine, mine, send.at[a, k], recv.at[a, k], self.grid.peer(k))
+
+    def over_items(self, a):
+        for k in range(1, self.chips):
+            self.chip_copy(a, k).wait()
+        total = self.chip_sum[a, self.chip].astype(F32)
+        for k in range(1, self.chips):
+            total = total + self.from_chip[a, k].astype(F32)
+        self.final[a, self.grid.item] = total.astype(BF16)
+        for k in range(1, self.grid.items):
+            self.final_copy(a, k).start()
+
+    def put(self, a, out):
+        for k in range(1, self.grid.items):
+            self.final_copy(a, k).wait()
+        channels = self.final.shape[4]
+        for b in range(3):
+            rows = [self.final[a, q, b].astype(F32) for q in range(self.grid.items)]
+            at = (a * 3 + b) * channels
+            out[at : at + channels] = jnp.concatenate(rows, axis=0).T
+
+
+class SideSum:
+    def __init__(self, grid, values, from_core, core_sum, from_item, item_sum, from_chip, final, core_sems,
+                 item_sems, chip_sems, final_sems):
+        self.grid = grid
+        self.values, self.from_core, self.core_sum = values, from_core, core_sum
+        self.from_item, self.item_sum, self.from_chip, self.final = (
+            from_item,
+            item_sum,
+            from_chip,
+            final,
+        )
+        self.core_sems, self.item_sems = core_sems, item_sems
+        self.chip_sems, self.final_sems = chip_sems, final_sems
+        self.chips = grid.n // 2
+        self.chip, self.core = grid.me // 2, lax.rem(grid.me, 2)
+
+    def core_copy(self):
+        send, recv = self.core_sems
+        grid = self.grid
+        return remote(
+            self.values.at[1 - self.core],
+            self.from_core,
+            send.at[0],
+            recv.at[0],
+            {"items": grid.item, "rows": grid.me + 1 - 2 * self.core},
+        )
+
+    def item_copy(self, k):
+        send, recv = self.item_sems
+        grid = self.grid
+        to = lax.rem(grid.item + k, grid.items)
+        return remote(
+            self.core_sum.at[to], self.from_item.at[k], send.at[k], recv.at[k], grid.peer(k)
+        )
+
+    def over_items(self):
+        self.core_copy().wait()
+        for z in range(self.chips):
+            both = self.values[self.core, z].astype(F32) + self.from_core[z].astype(F32)
+            for q in range(self.grid.items):
+                self.core_sum[q, z] = both[q].astype(BF16)
+        for k in range(1, self.grid.items):
+            self.item_copy(k).start()
+
+    def chip_copy(self, k):
+        send, recv = self.chip_sems
+        grid = self.grid
+        to = lax.rem(self.chip + k, self.chips)
+        return remote(
+            self.item_sum.at[to],
+            self.from_chip.at[k],
+            send.at[k],
+            recv.at[k],
+            {"items": grid.item, "rows": to * 2 + self.core},
+        )
+
+    def over_chips(self):
+        for k in range(1, self.grid.items):
+            self.item_copy(k).wait()
+        total = self.core_sum[self.grid.item].astype(F32)
+        for k in range(1, self.grid.items):
+            total = total + self.from_item[k].astype(F32)
+        self.item_sum[...] = total.astype(BF16)
+        for k in range(1, self.chips):
+            self.chip_copy(k).start()
+
+    def final_copy(self, k):
+        send, recv = self.final_sems
+        mine = self.final.at[self.grid.item]
+        return remote(mine, mine, send.at[k], recv.at[k], self.grid.peer(k))
+
+    def spread(self):
+        for k in range(1, self.chips):
+            self.chip_copy(k).wait()
+        total = self.item_sum[self.chip].astype(F32)
+        for k in range(1, self.chips):
+            total = total + self.from_chip[k].astype(F32)
+        self.final[self.grid.item] = total.astype(BF16)
+        for k in range(1, self.grid.items):
+            self.final_copy(k).start()
+
+    def put(self, qkv_out, proj_out):
+        for k in range(1, self.grid.items):
+            self.final_copy(k).wait()
+        rows = jnp.concatenate(
+            [self.final[q].astype(F32) for q in range(self.grid.items)], axis=0
+        )
+        share, channels = rows.shape[0], rows.shape[1] // 4
+        for w in range(3):
+            qkv_out[:, w * share : (w + 1) * share] = rows[:, w * channels : (w + 1) * channels].T
+        proj_out[...] = rows[:, 3 * channels :].T
+
+
+def conv_taps_back(shifted, weight, acc, rows_dev):
+    pixels, channels = acc.shape
+    acc[...] = jnp.zeros_like(acc)
+
+    def step(tap, carry):
+        lhs = shifted[pl.ds(tap, rows_dev)].reshape(pixels, 3 * channels)
+        total = None
+        for b in range(3):
+            at = pl.multiple_of(((2 - tap) * 3 + 2 - b) * channels, channels)
+            term = dot(
+                lhs[:, b * channels : (b + 1) * channels], weight[pl.ds(at, channels)], 1, 1
+            )
+            total = term if total is None else total + term
+        acc[...] += total
+        return carry
+
+    lax.fori_loop(0, 3, step, 0)
+
+
+def backward_kernel(items, n, *refs):
+    (info, embed, gain1, gain2, gain3, stats_in, shifts,
+     o_pair, dqkv_pair, dtext, first, middle, cot, image, hidden_all, second_all, attn_in, turned_in, text_cols,
+     proj_in, w1_in, w2_in, text_in, embed_in,
+     output, image_grad, conv1_out, conv2_out, qkv_out, proj_out, vectors, text_grad, text_w_grad, embed_grad,
+     weight, proj_w, qkv_turned, first_v, mid_v, cot_v, image_v, attn, cols, rows_v, dq, o, dt, own_dt,
+     grad_v, grad_mid, moved_v, pre, acc, shifted, shifted_all, masked, out_v, image_out,
+     turned, quarter, part, from_core, chip_sum, from_chip, final,
+     side_v, side_core, side_sum, side_item, side_total, side_chip, side_final,
+     vector, vector_land, own, slots,
+     load, sum_send, sum_recv, edge_send, edge_recv, row_send, row_recv, dt_send, dt_recv, vec_send, vec_recv,
+     k_item_send, k_item_recv, k_core_send, k_core_recv, k_chip_send, k_chip_recv, k_final_send, k_final_recv,
+     s_core_send, s_core_recv, s_item_send, s_item_recv, s_chip_send, s_chip_recv, s_final_send,
+     s_final_recv) = refs
+    grid = Grid(items, n)
+    item, me = grid.item, grid.me
+    rows_dev, width, channels = image.shape
+    pixels = rows_dev * width
+    heads, head_dim, wide = HEADS, channels // HEADS, 3 * channels // HEADS
+    share = channels // n
+    base = me * rows_dev
+    count = (info[0, 0] * info[0, 1]).astype(F32) * (channels // GROUPS)
+    scale, shift = shifts[:, :channels], shifts[:, channels:]
+
+    def inside(row):
+        return window(info, 0, row, (width, channels))
+
+    fetched = []
+
+    def fetch(src, dst):
+        c = pltpu.make_async_copy(src, dst, load.at[len(fetched)])
+        c.start()
+        fetched.append(c)
+        return c
+
+    def scatter(j, src, dst):
+        def copy(k):
+            to = lax.rem(me + k, n)
+            return remote(src.at[to], dst.at[me], row_send.at[j, k], row_recv.at[j, k], grid.row(k))
+
+        return copy
+
+    own_dq = fetch(dqkv_pair.at[me], dq.at[me])
+    got_turned = fetch(turned_in, qkv_turned)
+    got_mid = fetch(middle, mid_v)
+    got_cot = fetch(cot, cot_v)
+    got_w2 = fetch(w2_in, weight)
+    got_first = fetch(first, first_v)
+    got_attn = fetch(attn_in, attn)
+    own_o = fetch(o_pair.at[me], o.at[me])
+    got_proj = fetch(proj_in, proj_w)
+    own_text = fetch(dtext.at[me], own_dt.at[me])
+    own_all = fetch(dtext, dt.at[item, me])
+    got_second = fetch(second_all, rows_v)
+    got_image = fetch(image, image_v)
+    got_cols = fetch(text_cols, cols)
+    grid.greet()
+    edges = [
+        Edges(grid, field, edge_send.at[j], edge_recv.at[j])
+        for j, field in enumerate((grad_v, moved_v))
+    ]
+    for e in edges:
+        e.clear()
+    sums = [Sums(grid, own.at[j], slots.at[j], sum_send.at[j], sum_recv.at[j]) for j in range(3)]
+    kernel_sums = [
+        KernelSum(grid, turned.at[j], quarter.at[j], part.at[j], from_core.at[j], chip_sum.at[j], from_chip.at[j],
+                  final.at[j], (k_item_send.at[j], k_item_recv.at[j]), (k_core_send.at[j], k_core_recv.at[j]),
+                  (k_chip_send.at[j], k_chip_recv.at[j]), (k_final_send.at[j], k_final_recv.at[j]))
+        for j in range(2)
+    ]
+    sum2, sum1 = kernel_sums
+    side = SideSum(grid, side_v, side_core, side_sum, side_item, side_total, side_chip, side_final,
+                   (s_core_send, s_core_recv), (s_item_send, s_item_recv), (s_chip_send, s_chip_recv),
+                   (s_final_send, s_final_recv))
+    dq_copy = scatter(0, dqkv_pair, dq)
+    o_copy = scatter(1, o_pair, o)
+    text_copy = scatter(2, dtext, own_dt)
+
+    def gather_copy(k):
+        return remote(
+            dtext, dt.at[item, me], row_send.at[3, k], row_recv.at[3, k], grid.row(k)
+        )
+
+    grid.met()
+    grid.loop(n, lambda k: dq_copy(k).start())
+    grid.loop(n, lambda k: o_copy(k).start())
+    grid.loop(n, lambda k: text_copy(k).start())
+    grid.loop(n, lambda k: gather_copy(k).start())
+
+    got_turned.wait()
+    own_dq.wait()
+
+    def unproject_head(h):
+        rows = pl.ds(pl.multiple_of(h * wide, wide), wide)
+        return dot(dq[h].astype(F32).T.astype(BF16), qkv_turned[rows], 1, 0)
+
+    acc[...] = unproject_head(me)
+
+    def next_head(k):
+        dq_copy(k).wait()
+        acc[...] += unproject_head(lax.rem(me + n - k, n))
+
+    grid.loop(n, next_head)
+    got_mid.wait()
+    average, inverse = norm_of(stats_in[2], count)
+
+    def grad_row(r):
+        value = acc[pl.ds(r * width, width)] * inside(base + r)
+        grad_v[1 + r] = value
+        return value, value * ((mid_v[1 + r] - average) * inverse)
+
+    own[0] = row_stats(rows_dev, width, channels, grad_row)
+    sums[0].start()
+    edges[0].start()
+
+    got_attn.wait()
+
+    def qkv_head(h):
+        block = dot(dq[h], attn[...], 1, 0).astype(BF16)
+        for w in range(3):
+            rows = block[w * head_dim : (w + 1) * head_dim]
+            side_v[lax.rem(h, 2), h // 2, :, :, w * channels : (w + 1) * channels] = rows.reshape(
+                items, share // items, channels
+            )
+
+    each_row(heads, qkv_head)
+    got_cot.wait()
+
+    def mask_row(r):
+        masked[pl.ds(r * width, width)] = (cot_v[1 + r].astype(F32) * inside(base + r)).astype(BF16)
+
+    each_row(rows_dev, mask_row)
+
+    stats4 = sums[0].result()
+    mean, cross = means_of(stats4, gain3[...], count)
+    edges[0].wait()
+
+    def to_grad2(r):
+        normal = (mid_v[r] - average) * inverse
+        ok = inside(base + r - 1)
+        term = (grad_v[r] * gain3[...] - mean - normal * cross) * inverse * ok
+        total = cot_v[r].astype(F32) + term
+        grad_mid[r] = total
+        shift_into(shifted, r, total * ok)
+
+    each_row(rows_dev + 2, to_grad2)
+    sum2.send_grads(shifted)
+    got_w2.wait()
+    conv_taps_back(shifted, weight, acc, rows_dev)
+    got_first.wait()
+    average2, inverse2 = norm_of(stats_in[1], count)
+
+    def moved_row(r):
+        ok = inside(base + r)
+        normal, moved = moved_of(first_v[1 + r], ok, average2, inverse2, gain2[...], scale, shift)
+        value = acc[pl.ds(r * width, width)] * ok * silu_slope(moved)
+        moved_v[1 + r] = value
+        return value, value * normal
+
+    own[1] = row_stats(rows_dev, width, channels, moved_row)
+    sums[1].start()
+    edges[1].start()
+    got_w1 = fetch(w1_in, weight)
+    got_second.wait()
+
+    def shift_rows():
+        for g in range(items):
+            each_row(rows_dev + 2, lambda r: shift_into(shifted_all.at[g], r, rows_v[g, r].astype(F32)))
+
+    shift_rows()
+    got_hidden = fetch(hidden_all, rows_v)
+    sum2.wait_grads()
+    for a in range(3):
+        sum2.compute(a, shifted_all)
+
+    own_o.wait()
+    grid.loop(n, lambda k: o_copy(k).wait())
+    flat_o = o[...].reshape(channels, pixels)
+    block = dot(masked[...].astype(F32).T.astype(BF16), flat_o, 1, 1).astype(BF16)
+    for r in range(n):
+        rows = block[r * share : (r + 1) * share]
+        side_v[r % 2, r // 2, :, :, 3 * channels :] = rows.reshape(items, share // items, channels)
+    side.core_copy().start()
+
+    stats5 = sums[1].result()
+    factor = gain2[...] * (1.0 + scale)
+    mean, cross = means_of(stats5, factor, count)
+    edges[1].wait()
+
+    def to_grad1(r):
+        normal = (first_v[r] - average2) * inverse2
+        value = (moved_v[r] * factor - mean - normal * cross) * inverse2
+        shift_into(shifted, r, value * inside(base + r - 1))
+
+    each_row(rows_dev + 2, to_grad1)
+    sum1.send_grads(shifted)
+    for a in range(3):
+        sum2.over_chips(a)
+    got_w1.wait()
+    conv_taps_back(shifted, weight, acc, rows_dev)
+    got_image.wait()
+    average1, inverse1 = norm_of(stats_in[0], count)
+
+    def pre_row(r):
+        ok = inside(base + r)
+        normal = (image_v[r].astype(F32) - average1) * inverse1 * ok
+        value = acc[pl.ds(r * width, width)] * ok * silu_slope(normal * gain1[...])
+        pre[r] = value
+        return value, value * normal
+
+    own[2] = row_stats(rows_dev, width, channels, pre_row)
+    sums[2].start()
+    tall = text_in.shape[0]
+    got_text_w = [
+        fetch(text_in.at[:, j * channels : (j + 1) * channels], weight.at[j * tall : (j + 1) * tall])
+        for j in range(2)
+    ]
+    side.over_items()
+    got_hidden.wait()
+    shift_rows()
+    sum1.wait_grads()
+    sum1.compute(0, shifted_all)
+    sum1.compute(1, shifted_all)
+    sum1.over_chips(0)
+    sum1.compute(2, shifted_all)
+    sum1.over_chips(1)
+    sum1.over_chips(2)
+    for a in range(3):
+        sum2.over_items(a)
+    side.over_chips()
+
+    stats6 = sums[2].result()
+    e = embed[...].astype(F32)
+    low = (e * sigmoid(e)).astype(BF16).astype(F32)
+    vector[...] = jnp.zeros_like(vector)
+    vector[0:1] = stats6[1:2]
+    vector[1:2] = stats5[1:2] * (1.0 + scale)
+    vector[2:3] = stats4[1:2]
+    vector[3:4] = (stats5[1:2] * gain2[...]).astype(BF16).astype(F32)
+    vector[4:5] = stats5[0:1].astype(BF16).astype(F32)
+    for j in range(embed.shape[1] // channels):
+        vector[5 + j : 6 + j] = low[:, j * channels : (j + 1) * channels]
+
+    def vector_copy(k):
+        return remote(
+            vector, vector_land.at[item], vec_send.at[k], vec_recv.at[k], grid.peer(k)
+        )
+
+    grid.loop(items, lambda k: vector_copy(k).start())
+    vector_land[item] = vector[...]
+
+    grid.loop(n, lambda k: gather_copy(k).wait())
+    own_all.wait()
+
+    def dt_copy(k):
+        mine = dt.at[item]
+        return remote(mine, mine, dt_send.at[k], dt_recv.at[k], grid.peer(k))
+
+    grid.loop(items, lambda k: dt_copy(k).start())
+    mean, cross = means_of(stats6, gain1[...], count)
+
+    def finish_row(r):
+        normal = (image_v[r].astype(F32) - average1) * inverse1
+        term = (pre[r] * gain1[...] - mean - normal * cross) * inverse1
+        image_out[r] = (grad_mid[1 + r] + term) * inside(base + r)
+
+    each_row(rows_dev, finish_row)
+    put_image = fetch(image_out, image_grad)
+    side.spread()
+
+    got_proj.wait()
+    acc[...] = dot(flat_o.astype(F32).T.astype(BF16), proj_w[...], 1, 0)
+
+    def output_row(r):
+        value = mid_v[1 + r] + acc[pl.ds(r * width, width)] * inside(base + r)
+        out_v[r] = value.astype(BF16)
+
+    each_row(rows_dev, output_row)
+    put_output = fetch(out_v, output)
+
+    own_text.wait()
+    grid.loop(n, lambda k: text_copy(k).wait())
+    for c in got_text_w:
+        c.wait()
+    half = heads // 2
+    total = None
+    for j in range(2):
+        lhs = jnp.concatenate([own_dt[j * half + h] for h in range(half)], axis=1)
+        term = dot(lhs, weight[j * tall : (j + 1) * tall], 1, 1)
+        total = term if total is None else total + term
+    text_grad[...] = total
+    got_embed_w = [
+        fetch(embed_in.at[:, j * channels : (j + 1) * channels], weight.at[j * tall : (j + 1) * tall])
+        for j in range(2)
+    ]
+    for a in range(3):
+        sum1.over_items(a)
+    for a in range(3):
+        sum2.put(a, conv2_out)
+
+    grid.loop(items, lambda k: dt_copy(k).wait())
+    got_cols.wait()
+    tokens = cols.shape[0] * cols.shape[1]
+    flat_cols = cols[...].reshape(tokens, cols.shape[2]).astype(F32).T.astype(BF16)
+    for h in range(heads):
+        rhs = jnp.concatenate([dt[g, h].reshape(tokens // items, 2 * head_dim) for g in range(items)], axis=0)
+        text_w_grad[:, h * 2 * head_dim : (h + 1) * 2 * head_dim] = dot(flat_cols, rhs, 1, 0)
+
+    for c in got_embed_w:
+        c.wait()
+    total = None
+    for j in range(2):
+        lhs = vector[3 + j : 4 + j] if j else vector[3:4]
+        lhs = jnp.broadcast_to(lhs, (8, channels)).astype(BF16)
+        term = dot(lhs, weight[j * tall : (j + 1) * tall], 1, 1)
+        total = term if total is None else total + term
+    embed_grad[...] = total[0:1] * silu_slope(e)
+    side.put(qkv_out, proj_out)
+    for a in range(3):
+        sum1.put(a, conv1_out)
+    grid.loop(items, lambda k: vector_copy(k).wait())
+    vectors[...] = vector_land[...]
+    put_image.wait()
+    put_output.wait()
+
+
+def backward_call(info, embed, gains, stats, shifts, arrays, identity):
+    items, n = lax.axis_size("items"), lax.axis_size("rows")
+    o_pair, dqkv_pair, dtext = arrays[:3]
+    image, text_cols, text_w = arrays[6], arrays[11], arrays[15]
+    rows_dev, width, channels = image.shape
+    pixels = rows_dev * width
+    head_dim = channels // HEADS
+    share = channels // n
+    rows = share // items
+    chips = n // 2
+    padded = (rows_dev + 2, width, channels)
+    tokens = dtext.shape[1]
+    sds = jax.ShapeDtypeStruct
+    outs = (
+        sds(image.shape, BF16),
+        sds(image.shape, F32),
+        sds((9 * channels, share), F32),
+        sds((9 * channels, share), F32),
+        sds((channels, 3 * share), F32),
+        sds((channels, share), F32),
+        sds((items, 16, channels), F32),
+        sds((tokens, text_w.shape[0]), F32),
+        sds((text_w.shape[0] // n, 2 * channels), F32),
+        sds(embed.shape, F32),
+    )
+    v = pltpu.VMEM
+    scratch = [
+        v((9 * channels, channels), BF16),
+        v((channels, channels), BF16),
+        v((3 * channels, channels), BF16),
+        v(padded, F32),
+        v(padded, F32),
+        v(padded, BF16),
+        v(image.shape, BF16),
+        v((pixels, channels), BF16),
+        v(text_cols.shape, BF16),
+        v((items,) + padded, BF16),
+        v(dqkv_pair.shape, BF16),
+        v(o_pair.shape, BF16),
+        v((items, n) + dtext.shape, BF16),
+        v(dtext.shape, BF16),
+        v(padded, F32),
+        v(padded, F32),
+        v(padded, F32),
+        v(image.shape, F32),
+        v((pixels, channels), F32),
+        v((rows_dev + 2, width, 3 * channels), BF16),
+        v((items, rows_dev + 2, width, 3 * channels), BF16),
+        v((pixels, channels), BF16),
+        v(image.shape, BF16),
+        v(image.shape, F32),
+        v((2, items, channels // items, pixels), BF16),
+        v((2, items, channels // items, pixels), BF16),
+        v((2, 3, 2, 3, chips * rows, channels), BF16),
+        v((2, 3, 3, chips * rows, channels), BF16),
+        v((2, 3, chips, 3, rows, channels), BF16),
+        v((2, 3, chips, 3, rows, channels), BF16),
+        v((2, 3, items, 3, rows, channels), BF16),
+        v((2, chips, items, rows, 4 * channels), BF16),
+        v((chips, items, rows, 4 * channels), BF16),
+        v((items, chips, rows, 4 * channels), BF16),
+        v((items, chips, rows, 4 * channels), BF16),
+        v((chips, rows, 4 * channels), BF16),
+        v((chips, rows, 4 * channels), BF16),
+        v((items, rows, 4 * channels), BF16),
+        v((16, channels), F32),
+        v((items, 16, channels), F32),
+        v((3, 8, channels), F32),
+        v((3, n, 8, channels), F32),
+        DMA((32,)),
+        DMA((3, n)),
+        DMA((3, n)),
+        DMA((2, 2)),
+        DMA((2, 2)),
+        DMA((4, n)),
+        DMA((4, n)),
+        DMA((items,)),
+        DMA((items,)),
+        DMA((items,)),
+        DMA((items,)),
+        DMA((2, items)),
+        DMA((2, items)),
+        DMA((2, 3)),
+        DMA((2, 3)),
+        DMA((2, 3, chips)),
+        DMA((2, 3, chips)),
+        DMA((2, 3, items)),
+        DMA((2, 3, items)),
+        DMA((1,)),
+        DMA((1,)),
+        DMA((items,)),
+        DMA((items,)),
+        DMA((chips,)),
+        DMA((chips,)),
+        DMA((items,)),
+        DMA((items,)),
+    ]
+    return pl.pallas_call(
+        functools.partial(backward_kernel, items, n),
+        out_shape=outs,
+        in_specs=[SCALARS] + [WHOLE] * 6 + [ANYWHERE] * len(arrays),
+        out_specs=(ANYWHERE,) * 2 + (WHOLE,) * 8,
+        scratch_shapes=scratch,
+        compiler_params=pltpu.CompilerParams(
+            collective_id=identity, has_side_effects=True, vmem_limit_bytes=62 << 20
+        ),
+        cost_estimate=pl.CostEstimate(
+            flops=80 * pixels * channels * channels, bytes_accessed=60 << 20, transcendentals=0
+        ),
+        name="backward",
+    )(info, embed, *gains, stats, shifts, *arrays)
+
+
 def own_shards(
     info, image, embed, text, gain1, conv1_w, embed_w, gain2, conv2_w, gain3, qkv_w, text_w, proj_w,
-    cotangent, image_window,
+    cotangent,
 ):
     _, rows_dev, width, channels = image.shape
     items, parts = lax.axis_size("items"), lax.axis_size("rows")
     me = lax.axis_index("rows")
     head_dim = channels // HEADS
-    pixels = rows_dev * width
     tokens = text.shape[1]
     share = channels // parts
-    embed_float = embed.astype(F32)
-    embed_low = jax.nn.silu(embed_float).astype(BF16)
     (first, middle, cot, hidden_all, second_all, attn_flat, qkv_turned, qkv_pair, go_pair, text_pair, text_cols,
      stats, shifts) = forward_call(
         info,
@@ -1505,101 +1918,46 @@
         info[:, :2], qkv_pair, text_pair.reshape(parts * tokens, 2 * head_dim), go_pair, width
     )
 
-    def swap(values):
-        return lax.all_to_all(values, "rows", split_axis=0, concat_axis=0, tiled=True)
-
-    qkv_back = swap(qkv_grad_pair)
-    heads_out = swap(attended)
-    mid = middle[None, 1 : rows_dev + 1]
-    attn_grad, sums = unproject(info, mid, stats3, qkv_back, qkv_turned)
-    stats4, grad_above, grad_below, text_back = exchange(sums, (attn_grad,), 3, (text_grad_pair,))
-    text_all = lax.all_gather(text_back[None], "items", axis=0, tiled=True)
-    proj_shaped = proj_w.reshape(HEADS, head_dim, channels)
-    grad_proj = (cotangent.astype(F32) * image_window).astype(BF16).reshape(pixels, channels)
-    proj_grad = jnp.einsum("pc,hdp->chd", grad_proj, heads_out, preferred_element_type=F32)
-    qkv_grad = jnp.einsum(
-        "hwdp,pc->hdwc",
-        qkv_back.reshape(HEADS, 3, head_dim, pixels),
-        attn_flat,
-        preferred_element_type=F32,
+    text_w_rows = text_cols.shape[3]
+    (output, image_grad, conv1_total, conv2_total, qkv_total, proj_total, vectors, text_grad, text_w_grad,
+     embed_grad) = backward_call(
+        info,
+        embed,
+        (gain1, gain2, gain3),
+        stats,
+        shifts,
+        (
+            attended,
+            qkv_grad_pair,
+            text_grad_pair.reshape(parts, tokens, 2 * head_dim),
+            first,
+            middle,
+            cot,
+            image[0],
+            hidden_all,
+            second_all,
+            attn_flat,
+            qkv_turned,
+            text_cols.reshape(items * parts, tokens, text_w_rows),
+            proj_w,
+            conv1_w.reshape(9 * channels, channels),
+            conv2_w.reshape(9 * channels, channels),
+            text_w,
+            embed_w,
+        ),
+        1,
     )
-    side = jnp.concatenate(
-        [
-            qkv_grad.astype(BF16).reshape(channels, 3 * channels),
-            proj_grad.astype(BF16).reshape(channels, channels),
-        ],
-        axis=1,
-    )
-    side = lax.psum_scatter(side, "rows", scatter_dimension=0, tiled=True)
-    full = jax.ShapeDtypeStruct(image.shape, F32)
-    summed = jax.ShapeDtypeStruct((1, 8, channels), F32)
-    padded = jax.ShapeDtypeStruct((1, rows_dev + 2, width, channels), BF16)
-    own_first = first[None, 1 : rows_dev + 1]
-    last = rows_dev + 1
-    grad_middle, moved_grad, sums, conv2_grad = conv_call(
-        back2_kernel,
-        info,
-        (attn_grad, grad_above, grad_below, mid, middle[None, :1], middle[None, last:], cotangent,
-         cot[None, :1], cot[None, last:], stats3, stats4, gain3, own_first, stats2, gain2, shifts),
-        conv2_w,
-        (full, full, summed, padded),
-        True,
-    )
-    stats5, moved_above, moved_below = exchange(sums, (moved_grad,), 4)
-    pre_grad, sums, conv1_grad = conv_call(
-        back1_kernel,
-        info,
-        (moved_grad, moved_above, moved_below, own_first, first[None, :1], first[None, last:], stats2,
-         stats5, gain2, shifts, image, stats1, gain1),
-        conv1_w,
-        (full, summed, padded),
-        True,
-    )
-    (stats6,) = exchange(sums, (), 5)
-    image_grad = finish(info, pre_grad, stats6, image, stats1, gain1, grad_middle)
-    projected = jnp.einsum("hdp,hdc->pc", heads_out, proj_shaped, preferred_element_type=F32)
-    output = (mid + projected.reshape(image.shape) * image_window).astype(BF16)
-    grad_shifts = jnp.concatenate([stats5[:, 1] * gain2, stats5[:, 0]], axis=1).astype(BF16)
-    gains = jnp.concatenate(
-        [stats6[:, 1], stats5[:, 1] * (1.0 + shifts[:, :channels]), stats4[:, 1]], axis=0
-    )
-    vector = jnp.concatenate(
-        [
-            gains,
-            grad_shifts.astype(F32).reshape(2, channels),
-            embed_low.astype(F32).reshape(-1, channels),
-        ],
-        axis=0,
-    )
-    filled = vector.shape[0]
-    vector = jnp.pad(vector, ((0, -filled % 8), (0, 0)))
-    (conv2_total,) = reduce_weight(conv2_grad, second_all, 6)
-    conv1_total, side, vectors = reduce_weight(conv1_grad, hidden_all, 7, side, vector)
-    own_text = lax.dynamic_slice_in_dim(text_all, lax.axis_index("items"), 1, 0)
-    own_text = lax.dynamic_slice_in_dim(own_text[0], me * tokens, tokens, 2)
-    text_shaped = text_w.reshape(text_w.shape[0], HEADS, 2 * head_dim)
-    text_grad = jnp.einsum("hkt,chk->tc", own_text, text_shaped, preferred_element_type=F32)
-    text_w_grad = jnp.einsum(
-        "gtc,ghkt->chk",
-        text_cols.reshape(items, parts * tokens, text.shape[2] // parts),
-        text_all,
-        preferred_element_type=F32,
-    )
-    embed_grad = jnp.einsum(
-        "ik,ck->ic", grad_shifts, embed_w, preferred_element_type=F32
-    ) * silu_slope(embed_float)
+    embed_rows = embed.shape[1] // channels
     all_shifts = vectors[:, 3:5].reshape(items, 2 * channels).astype(BF16)
-    all_embed = vectors[:, 5:filled].reshape(items, embed.shape[1]).astype(BF16)
+    all_embed = vectors[:, 5 : 5 + embed_rows].reshape(items, embed.shape[1]).astype(BF16)
     embed_share = embed_w.shape[0] // parts
-    embed_rows = lax.dynamic_slice_in_dim(all_embed, me * embed_share, embed_share, 1)
-    embed_w_grad = jnp.einsum("ic,ik->ck", embed_rows, all_shifts, preferred_element_type=F32)
+    own_embed = lax.dynamic_slice_in_dim(all_embed, me * embed_share, embed_share, 1)
+    embed_w_grad = jnp.einsum("ic,ik->ck", own_embed, all_shifts, preferred_element_type=F32)
     gains = jnp.sum(vectors[:, :3], axis=0)
     gains = lax.dynamic_slice_in_dim(gains, me * share, share, 1)
-    qkv_total = side[:, : 3 * channels].reshape(head_dim, 3, channels)
-    qkv_total = jnp.transpose(qkv_total, (2, 1, 0)).reshape(channels, 3 * share)
     return (
-        output,
-        image_grad,
+        output[None],
+        image_grad[None],
         embed_grad,
         text_grad[None],
         gains[0],
@@ -1609,8 +1967,8 @@
         conv2_total.reshape(3, 3, channels, share),
         gains[2],
         qkv_total,
-        text_w_grad.reshape(-1, 2 * channels),
-        side[:, 3 * channels :].T,
+        text_w_grad,
+        proj_total,
     )
 
 
@@ -1648,11 +2006,12 @@
         and pixels % 512 == 0
         and tokens % 16 == 0
         and text.shape[2] % (128 * parts) == 0
+        and text.shape[2] == embed.shape[1] <= 4 * channels
     )
     if own_path:
         return own_shards(
             info, image, embed, text, gain1, conv1_w, embed_w, gain2, conv2_w, gain3, qkv_w, text_w,
-            proj_w, cotangent, image_window,
+            proj_w, cotangent,
         )
 
     embed_float = embed.astype(F32)
@@ -1734,7 +2093,7 @@
 
     attn_grad, stats = unproject(info, middle, stats3, qkv_back, qkv_turned)
     stats4, grad_above, grad_below, text_back = exchange(stats, (attn_grad,), 3, (text_grad_pair,))
-    text_back = text_back.reshape(images, HEADS, 2 * head_dim, parts * tokens)
+    text_back = text_back.reshape(images, HEADS, parts * tokens, 2 * head_dim)
     text_all = lax.all_gather(text_back, "items", axis=0, tiled=True)
     proj_grad = jnp.einsum("ipc,ihdp->chd", grad_proj, heads_out, preferred_element_type=F32)
     qkv_grad = jnp.einsum(
@@ -1769,11 +2128,11 @@
         "ihdp,hdc->ipc", heads_out, proj_shaped, preferred_element_type=F32
     ).reshape(image.shape)
     output = (middle + projected * image_window).astype(BF16)
-    own_text = lax.dynamic_slice_in_dim(text_back, me * tokens, tokens, 3)
+    own_text = lax.dynamic_slice_in_dim(text_back, me * tokens, tokens, 2)
     text_shaped = text_w.reshape(text_w.shape[0], HEADS, 2 * head_dim)
-    text_grad = jnp.einsum("ihkt,chk->itc", own_text, text_shaped, preferred_element_type=F32)
+    text_grad = jnp.einsum("ihtk,chk->itc", own_text, text_shaped, preferred_element_type=F32)
     text_w_grad = jnp.einsum(
-        "gtc,ghkt->chk", text_cols, text_all, preferred_element_type=F32
+        "gtc,ghtk->chk", text_cols, text_all, preferred_element_type=F32
     ).reshape(text_share, 2 * channels)
     scale_sum = stats5[:, 1] * gain2
     grad_shifts = jnp.concatenate([scale_sum, stats5[:, 0]], axis=1).astype(BF16)

time: 385 us -> 286 us (0.74)
  waiting for transfers between devices: 29.4 us -> 0 us
  local copies, waits for them, and re-layouts: 35.4 us -> 14 us
  matrix products: 18.9 us -> 1.32 us
  between operations: 16 us -> 0.73 us
  starting transfers between devices: 10.1 us -> 0 us
  other arithmetic: 7.29 us -> 3.01 us
    all_to_all x2 -> x0, waiting for transfers between devices: 29.4 us -> none  [swap(): lax.all_to_all(values, 'rows', split_axis=0, concat_axis=0, tiled=True)]
    dot_general x7 -> x1, matrix products: 18.9 us -> 1.32 us  [own_shards(): jnp.einsum('ic,ik->ck', own_embed, all_shifts, preferred_element_type=F32)]
    all_to_all x2 -> x0, starting transfers between devices: 9.8 us -> none  [swap(): lax.all_to_all(values, 'rows', split_axis=0, concat_axis=0, tiled=True)]
    broadcast_in_dim x3 -> x0, local copies, waits for them, and re-layouts: 5.49 us -> none  [the longest x1 2.78 us: own_shards(): own_first = first[None, 1:rows_dev + 1]]
    unnamed x99 -> x23, local copies, waits for them, and re-layouts: 17.5 us -> 13.4 us
    pallas_call x9 -> x1, Pallas kernels: 130 us -> 128 us  [backward_call(): pl.pallas_call(functools.partial(backward_kernel, items, n), out_shape=ou...]
  transfers between devices with their start and end apart: 4 -> 0, of which waited for: 1 -> 0; matrix products, arithmetic and copies ran while one was open for 11% -> 0% of each run, Pallas kernels for 24% -> 0%
where the time goes in v1:
time: 286 us; the launch traced here: 284 us
  Pallas kernels  265 us (93%)
  local copies, waits for them, and re-layouts  14 us (5%)
  other arithmetic  3.01 us (1%)
    pallas_call x1, Pallas kernels, backward_call(): pl.pallas_call(functools.partial(backward_kernel, items, n), out_shape=ou...  128 us
    pallas_call x1, Pallas kernels, forward_call(): pl.pallas_call(functools.partial(forward_kernel, items, n), out_shape=out...  74.7 us
    pallas_call x1, Pallas kernels, attention(): pl.pallas_call(functools.partial(attention_kernel, width, step, bq), out_...  62 us
    unnamed x23, local copies, waits for them, and re-layouts  13.4 us

profile of v1, /device:TPU:0, one launch (start us, length us, event | category | flops | bytes accessed | tf_op | source)
XLA Modules:
  0.0 284.0 jit_solution(16868872856274152970)
XLA Ops:
  0.6 1.2 pad_add_fusion.refs_0_
  1.9 74.7 %forward.1 = (f32[10,64,512]{2,1,0:T(8,128)}, f32[10,64,512]{2,1,0:T(8,128)}, bf16[10,64,512]{2,1,0:T(8,128)(2,1)}, bf16[4,10,64,512]{3,2,1,0:T(8,128)(2,1)}, bf...) custom-call(s32[1,3]{1,0:T(1,128)} %pad_add_fusion.refs_0_, ...), custom_call_target="tpu_custom_call" | custom-call | flops 5368709120 | bytes 62914560 | tf_op jit(solution)/shard_map/forward/pallas_call | solution.py:1211
  76.6 62.0 %shard_map.237 = (bf16[8,64,512]{2,1,0:T(8,128)(2,1)}, bf16[8,192,512]{2,1,0:T(8,128)(2,1)}, bf16[128,128]{1,0:T(8,128)(2,1)}) custom-call(s32[1,2]{1,0:T(1,128)} %ext_ref.1, bf16[8,192,512]{2,1,0:T(8,128)(2,1)} %get-tuple-element.41.qkv_ref, bf16[128,128]{1,0:T(8,128)(2,1)} %bitcast.54, bf16[8,64,512]{2,1,0:T(8,128)(2,1)} %get-tuple-element.43.go_ref), custom_call_target="tpu_custom_call" | custom-call | flops 53150220288 | bytes 4194304 | tf_op jit(solution)/shard_map/pallas_call | solution.py:155
  138.5 128.3 %backward.1 = (bf16[8,64,512]{2,1,0:T(8,128)(2,1)}, f32[8,64,512]{2,1,0:T(8,128)}, f32[4608,64]{1,0:T(8,128)}, f32[4608,64]{1,0:T(8,128)}, f32[512,192]{1,0:T(8,...) custom-call(s32[1,3]{1,0:T(1,128)} %pad_add_fusion.refs_0_, ...), custom_call_target="tpu_custom_call" | custom-call | flops 10737418240 | bytes 62914560 | tf_op jit(solution)/shard_map/backward/pallas_call | solution.py:1872
  266.8 0.9 convert.4
  267.7 0.0 copy-start
  267.8 1.3 fusion
  269.1 2.8 copy.27
  271.9 0.0 copy-done
  271.9 0.0 copy-start.2
  271.9 1.7 copy.28
  273.6 0.0 copy-start.4
  273.6 0.0 copy-start.3
  273.7 0.0 copy-start.1
  273.7 2.1 copy.29
  275.7 1.7 copy.30
  277.4 0.9 slice_reduce_fusion
  278.3 0.1 constant_dynamic-slice_fusion
  278.4 0.5 slice_bitcast_fusion.2
  278.9 1.9 copy.38
  280.8 0.0 copy-done.2
  280.8 1.0 copy.39
  281.7 0.0 copy-done.4
  281.7 0.6 copy.40
  282.3 0.0 copy-done.3
  282.3 0.7 copy.41
  283.0 0.0 copy-done.1
  283.0 1.0 copy.42
  (4 shorter events, 0.0 us)
Async XLA Ops:
  267.7 4.2 %copy-start = (f32[4608,64]{1,0:T(8,128)S(1)}, f32[4608,64]{1,0:T(8,128)}, u32[]{:S(2)}) copy-start(f32[4608,64]{1,0:T(8,128)} %get-tuple-element.61) | copy-start | bytes 3538948
  271.9 8.8 %copy-start.2 = (f32[8,64,512]{2,1,0:T(8,128)S(1)}, f32[8,64,512]{2,1,0:T(8,128)}, u32[]{:S(2)}) copy-start(f32[8,64,512]{2,1,0:T(8,128)} %get-tuple-element.56) | copy-start | bytes 3145732
  273.6 8.1 %copy-start.4 = (f32[1,2048]{1,0:T(1,128)S(1)}, f32[1,2048]{1,0:T(1,128)}, u32[]{:S(2)}) copy-start(f32[1,2048]{1,0:T(1,128)} %get-tuple-element.96) | copy-start | bytes 24580
  273.6 8.7 %copy-start.3 = (f32[16,2048]{1,0:T(8,128)S(1)}, f32[16,2048]{1,0:T(8,128)}, u32[]{:S(2)}) copy-start(f32[16,2048]{1,0:T(8,128)} %get-tuple-element.58) | copy-start | bytes 393220
  273.7 9.4 %copy-start.1 = (f32[256,1024]{1,0:T(8,128)S(1)}, f32[256,1024]{1,0:T(8,128)}, u32[]{:S(2)}) copy-start(f32[256,1024]{1,0:T(8,128)} %get-tuple-element.105) | copy-start | bytes 3145732

commit v2 on v1

--- a/solution.py
+++ b/solution.py
@@ -16,51 +16,61 @@
 def dot(a, b, ca, cb):
     return lax.dot_general(a, b, (((ca,), (cb,)), ((), ())), preferred_element_type=F32)
 
-def attention_kernel(width, step, bq, ext_ref, qkv_ref, text_ref, go_ref, out_ref, dqkv_ref, dtext_ref,
-                     kn, vn, kt, vt, s0, s1, e0, e1, dkt, dvt):
-    scores, raised = (s0, s1), (e0, e1)
-    chunks, _, span = qkv_ref.shape
-    tlen = text_ref.shape[0]
-    d = go_ref.shape[1]
-    pix = chunks * span
-    keys = pix + tlen
-    steps = keys // step
-    rows_ok, cols_ok = ext_ref[0, 0], ext_ref[0, 1]
-    def stage(c, carry):
+def nothing(*_):
+    return None
+
+
+class Attention:
+    def __init__(self, chunks, span, d, tlen, step, bq, scratch):
+        self.chunks, self.span, self.d, self.tlen, self.step, self.bq = chunks, span, d, tlen, step, bq
+        self.kn, self.vn, self.kt, self.vt, s0, s1, e0, e1, self.dkt, self.dvt = scratch
+        self.scores, self.raised = (s0, s1), (e0, e1)
+        self.pix = chunks * span
+
+    def stage_key(self, c, k, width, rows_ok, cols_ok):
+        d, span = self.d, self.span
         base = pl.multiple_of(c * span, span)
         pos = base + lax.broadcasted_iota(jnp.int32, (16, span), 1)
         row = lax.broadcasted_iota(jnp.int32, (16, span), 0)
         ok = (pos // width < rows_ok) & (pos % width < cols_ok)
         extra = jnp.where((row == 0) & jnp.logical_not(ok), NEG, 0.0)
-        k = qkv_ref[c, d:2 * d, :]
-        v = qkv_ref[c, 2 * d:, :]
-        kt[:, pl.ds(base, span)] = k
-        vt[:, pl.ds(base, span)] = v
         rest = jnp.zeros((128 - d - 16, span), F32)
+        self.kt[:, pl.ds(base, span)] = k
         ka = jnp.concatenate([k.astype(F32), extra, rest], axis=0)
+        self.kn[pl.ds(base, span), :] = ka.T.astype(BF16)
+
+    def stage_value(self, c, v):
+        d, span = self.d, self.span
+        base = pl.multiple_of(c * span, span)
+        row = lax.broadcasted_iota(jnp.int32, (16, span), 0)
+        rest = jnp.zeros((128 - d - 16, span), F32)
+        self.vt[:, pl.ds(base, span)] = v
         va = jnp.concatenate([v.astype(F32), jnp.where(row < 3, 1.0, 0.0), rest], axis=0)
-        kn[pl.ds(base, span), :] = ka.T.astype(BF16)
-        vn[pl.ds(base, span), :] = va.T.astype(BF16)
-        return carry
-    lax.fori_loop(0, chunks, stage, 0)
-    tk = text_ref[:, :d].astype(F32)
-    tv = text_ref[:, d:].astype(F32)
-    kt[:, pix:] = tk.T.astype(BF16)
-    vt[:, pix:] = tv.T.astype(BF16)
-    lanes = lax.broadcasted_iota(jnp.int32, (tlen, 128 - d), 1)
-    kn[pix:, :] = jnp.concatenate([tk, jnp.zeros((tlen, 128 - d), F32)], axis=1).astype(BF16)
-    vn[pix:, :] = jnp.concatenate([tv, jnp.where(lanes < 3, 1.0, 0.0)], axis=1).astype(BF16)
-    dkt[...] = jnp.zeros_like(dkt)
-    dvt[...] = jnp.zeros_like(dvt)
-
-    low_peak = jnp.full((8, bq), -3e38, F32)
-
-    def q_aug(c, half):
-        q = qkv_ref[c, :d, half * bq:(half + 1) * bq].astype(F32) * (d ** -0.5)
+        self.vn[pl.ds(base, span), :] = va.T.astype(BF16)
+
+    def stage_text(self, text):
+        d, tlen, pix = self.d, self.tlen, self.pix
+        tk = text[:, :d].astype(F32)
+        tv = text[:, d:].astype(F32)
+        self.kt[:, pix:] = tk.T.astype(BF16)
+        self.vt[:, pix:] = tv.T.astype(BF16)
+        lanes = lax.broadcasted_iota(jnp.int32, (tlen, 128 - d), 1)
+        rest = jnp.zeros((tlen, 128 - d), F32)
+        self.kn[pix:, :] = jnp.concatenate([tk, rest], axis=1).astype(BF16)
+        ones = jnp.where(lanes < 3, 1.0, 0.0)
+        self.vn[pix:, :] = jnp.concatenate([tv, ones], axis=1).astype(BF16)
+
+    def query(self, q):
+        d, bq = self.d, self.bq
         r = lax.broadcasted_iota(jnp.int32, (128 - d, bq), 0)
-        return jnp.concatenate([q, jnp.where(r == 0, 1.0, 0.0)], axis=0).astype(BF16)
-
-    def run(score, exp, back):
+        rest = jnp.where(r == 0, 1.0, 0.0)
+        return jnp.concatenate([q.astype(F32) * (d**-0.5), rest], axis=0).astype(BF16)
+
+    def run(self, score, exp, back):
+        d, bq, step = self.d, self.bq, self.step
+        kn, vn, kt, vt, dkt, dvt = self.kn, self.vn, self.kt, self.vt, self.dkt, self.dvt
+        scores, raised = self.scores, self.raised
+
         def body(j, carry):
             pk, total, acc, dq = carry
             at = pl.ds(pl.multiple_of(j * step, step), step)
@@ -77,79 +87,140 @@
                 raised[slot][at, :] = low
                 acc = acc + dot(vt[:, at], low, 1, 0)
             if back:
-                slot, goa, gs, q = back
+                slot, goa, q = back
                 dp = dot(vn[at, :], goa, 1, 0)
                 e = raised[slot][at, :]
                 ds = (e.astype(F32) * dp).astype(BF16)
-                dvt[:, at] += dot(gs, e, 1, 1)
+                dvt[:, at] += dot(goa[:d], e, 1, 1)
                 dkt[:, at] += dot(q, ds, 1, 1)
                 dq = dq + dot(kt[:, at], ds, 1, 0)
             return pk, total, acc, dq
-        init = (low_peak, jnp.zeros((8, bq), F32), jnp.zeros((d, bq), F32), jnp.zeros((d, bq), F32))
-        return lax.fori_loop(0, steps, body, init)
-
-    def finish_exp(c, half, total, acc):
+
+        init = (
+            jnp.full((8, bq), -3e38, F32),
+            jnp.zeros((8, bq), F32),
+            jnp.zeros((d, bq), F32),
+            jnp.zeros((d, bq), F32),
+        )
+        return lax.fori_loop(0, (self.pix + self.tlen) // step, body, init)
+
+    def attended(self, go, total, acc):
+        d, bq = self.d, self.bq
         inv = 1.0 / jnp.sum(total, axis=0, keepdims=True)
         o = acc * inv
-        cols = slice(half * bq, (half + 1) * bq)
-        out_ref[c, :, cols] = o.astype(BF16)
-        go = go_ref[c, :, cols].astype(F32)
+        go = go.astype(F32)
         nd = -jnp.sum(go * o, axis=0, keepdims=True) * inv
-        gs = go * inv
         hi = nd.astype(BF16).astype(F32)
         mid = (nd - hi).astype(BF16).astype(F32)
         lo = nd - hi - mid
         r = lax.broadcasted_iota(jnp.int32, (16, bq), 0)
         extra = jnp.where(r == 0, hi, jnp.where(r == 1, mid, jnp.where(r == 2, lo, 0.0)))
-        goa = jnp.concatenate([gs, extra, jnp.zeros((128 - d - 16, bq), F32)], axis=0).astype(BF16)
-        return goa
-
-    def put_dq(c, half, dq):
-        dqkv_ref[c, :d, half * bq:(half + 1) * bq] = (dq * (d ** -0.5)).astype(BF16)
-
-    def top(pk):
-        return jnp.max(pk, axis=0, keepdims=True)
-
-    def q_of(c, half):
-        return qkv_ref[c, :d, half * bq:(half + 1) * bq]
-
-    pk, _, _, _ = run((0, q_aug(0, 0)), None, None)
-    pk, total, acc, _ = run((1, q_aug(0, 1)), (0, top(pk)), None)
-    goa = finish_exp(0, 0, total, acc)
-
-    def two(h, carry):
-        pk, goa = carry
-        pk2, total, acc, dq = run((0, q_aug(h + 1, 0)), (1, top(pk)), (0, goa, goa[:d], q_of(h, 0)))
-        put_dq(h, 0, dq)
-        goa = finish_exp(h, 1, total, acc)
-        pk3, total, acc, dq = run((1, q_aug(h + 1, 1)), (0, top(pk2)), (1, goa, goa[:d], q_of(h, 1)))
-        put_dq(h, 1, dq)
-        return pk3, finish_exp(h + 1, 0, total, acc)
-    pk, goa = lax.fori_loop(0, chunks - 1, two, (pk, goa))
-    last = chunks - 1
-    _, total, acc, dq = run(None, (1, top(pk)), (0, goa, goa[:d], q_of(last, 0)))
-    put_dq(last, 0, dq)
-    goa = finish_exp(last, 1, total, acc)
-    _, _, _, dq = run(None, None, (1, goa, goa[:d], q_of(last, 1)))
-    put_dq(last, 1, dq)
+        rest = jnp.zeros((128 - d - 16, bq), F32)
+        return o.astype(BF16), jnp.concatenate([go * inv, extra, rest], axis=0).astype(BF16)
+
+    def attend(self, q_ref, go_ref, o_ref, dq_ref, order, scored=nothing, before=nothing, done=nothing):
+        d, bq, chunks = self.d, self.bq, self.chunks
+        self.dkt[...] = jnp.zeros_like(self.dkt)
+        self.dvt[...] = jnp.zeros_like(self.dvt)
+
+        def columns(half):
+            return slice(half * bq, (half + 1) * bq)
+
+        def q_of(h, half):
+            return q_ref[order(h), :d, columns(half)]
+
+        def finish_exp(h, half, total, acc):
+            c = order(h)
+            o, goa = self.attended(go_ref[c, :, columns(half)], total, acc)
+            o_ref[c, :, columns(half)] = o
+            return goa
+
+        def put_dq(h, half, dq):
+            dq_ref[order(h), :d, columns(half)] = (dq * (d**-0.5)).astype(BF16)
+
+        def top(pk):
+            return jnp.max(pk, axis=0, keepdims=True)
+
+        run = self.run
+        pk, _, _, _ = run((0, self.query(q_of(0, 0))), None, None)
+        scored()
+        pk, total, acc, _ = run((1, self.query(q_of(0, 1))), (0, top(pk)), None)
+        goa = finish_exp(0, 0, total, acc)
+
+        def two(h, carry):
+            pk, goa = carry
+            before(h + 1)
+            qa = self.query(q_of(h + 1, 0))
+            pk2, total, acc, dq = run((0, qa), (1, top(pk)), (0, goa, q_of(h, 0)))
+            put_dq(h, 0, dq)
+            goa = finish_exp(h, 1, total, acc)
+            qa = self.query(q_of(h + 1, 1))
+            pk3, total, acc, dq = run((1, qa), (0, top(pk2)), (1, goa, q_of(h, 1)))
+            put_dq(h, 1, dq)
+            done(h)
+            return pk3, finish_exp(h + 1, 0, total, acc)
+
+        pk, goa = lax.fori_loop(0, chunks - 1, two, (pk, goa))
+        last = chunks - 1
+        _, total, acc, dq = run(None, (1, top(pk)), (0, goa, q_of(last, 0)))
+        put_dq(last, 0, dq)
+        goa = finish_exp(last, 1, total, acc)
+        _, _, _, dq = run(None, None, (1, goa, q_of(last, 1)))
+        put_dq(last, 1, dq)
+        done(last)
+
+    def key_grad(self, at):
+        return (self.dkt[:, at] * (self.d**-0.5)).astype(BF16)
+
+    def value_grad(self, at):
+        return self.dvt[:, at].astype(BF16)
+
+    def text_grad(self, out):
+        d, pix = self.d, self.pix
+        out[:, :d] = (self.dkt[:, pix:] * (d**-0.5)).T.astype(BF16)
+        out[:, d:] = self.dvt[:, pix:].T.astype(BF16)
+
+
+def attention_scratch(chunks, span, d, tlen):
+    keys = chunks * span + tlen
+    bq = span // 2
+    lanes = keys // 128
+    step = 128 * max(n for n in range(1, 12) if lanes % n == 0)
+    shapes = [((keys, 128), BF16)] * 2 + [((d, keys), BF16)] * 2
+    shapes += [((keys, bq), F32)] * 2 + [((keys, bq), BF16)] * 2 + [((d, keys), F32)] * 2
+    return step, bq, [pltpu.VMEM(*shape) for shape in shapes]
+
+
+def attention_kernel(width, step, bq, ext_ref, qkv_ref, text_ref, go_ref, out_ref, dqkv_ref, dtext_ref, *scratch):
+    chunks, _, span = qkv_ref.shape
+    d = go_ref.shape[1]
+    att = Attention(chunks, span, d, text_ref.shape[0], step, bq, scratch)
+
+    def stage(c, carry):
+        att.stage_key(c, qkv_ref[c, d : 2 * d, :], width, ext_ref[0, 0], ext_ref[0, 1])
+        att.stage_value(c, qkv_ref[c, 2 * d :, :])
+        return carry
+
+    lax.fori_loop(0, chunks, stage, 0)
+    att.stage_text(text_ref)
+    att.attend(qkv_ref, go_ref, out_ref, dqkv_ref, lambda h: h)
 
     def finish(c, carry):
         at = pl.ds(pl.multiple_of(c * span, span), span)
-        dqkv_ref[c, d:2 * d, :] = (dkt[:, at] * (d ** -0.5)).astype(BF16)
-        dqkv_ref[c, 2 * d:, :] = dvt[:, at].astype(BF16)
+        dqkv_ref[c, d : 2 * d, :] = att.key_grad(at)
+        dqkv_ref[c, 2 * d :, :] = att.value_grad(at)
         return carry
+
     lax.fori_loop(0, chunks, finish, 0)
-    dtext_ref[:, :d] = (dkt[:, pix:] * (d ** -0.5)).T.astype(BF16)
-    dtext_ref[:, d:] = dvt[:, pix:].T.astype(BF16)
+    att.text_grad(dtext_ref)
+
 
 def attention(ext, qkv, text, go, width):
     chunks, wide, span = qkv.shape
     d = wide // 3
     tlen = text.shape[0]
     keys = chunks * span + tlen
-    bq = span // 2
-    lanes = keys // 128
-    step = 128 * max(n for n in range(1, 12) if lanes % n == 0)
+    step, bq, scratch = attention_scratch(chunks, span, d, tlen)
     vm = pl.BlockSpec(memory_space=pltpu.VMEM)
     flops = 2 * 6 * chunks * span * keys * d
     return pl.pallas_call(
@@ -161,18 +232,7 @@
         ),
         in_specs=[pl.BlockSpec(memory_space=pltpu.SMEM), vm, vm, vm],
         out_specs=(vm, vm, vm),
-        scratch_shapes=[
-            pltpu.VMEM((keys, 128), BF16),
-            pltpu.VMEM((keys, 128), BF16),
-            pltpu.VMEM((d, keys), BF16),
-            pltpu.VMEM((d, keys), BF16),
-            pltpu.VMEM((keys, bq), F32),
-            pltpu.VMEM((keys, bq), F32),
-            pltpu.VMEM((keys, bq), BF16),
-            pltpu.VMEM((keys, bq), BF16),
-            pltpu.VMEM((d, keys), F32),
-            pltpu.VMEM((d, keys), F32),
-        ],
+        scratch_shapes=scratch,
         compiler_params=pltpu.CompilerParams(vmem_limit_bytes=56 << 20),
         cost_estimate=pl.CostEstimate(
             flops=4 * flops, bytes_accessed=16 * chunks * span * d, transcendentals=chunks * span * keys
@@ -933,13 +993,15 @@
     lax.fori_loop(0, 3, step, 0)
 
 
-def forward_kernel(items, n, *refs):
+def forward_kernel(items, n, step, bq, *refs):
     (info, image, cot, text, embed, gain1, gain2, gain3, w1_in, w2_in, embed_in, text_in, qkv_in, proj_in,
-     first_out, mid_out, cot_out, hidden_all, second_all, attn_out, turned_out, qkv_pair, go_pair, text_pair,
-     text_cols, stats_out, shifts_out,
+     first_out, mid_out, cot_out, hidden_all, second_all, attn_out, turned_out, o_out, dq_out, dkv_out, dt_out,
+     dt_all, text_cols, stats_out, shifts_out,
      image_v, cot_v, text_v, w1, w2, embed_w, text_w, qkv_w, proj_w, first_v, mid_v, hidden, second, attn,
-     turned, qkv, go, text_kv, cols, shifted, acc, own, slots,
-     load, sum_send, sum_recv, edge_send, edge_recv, row_send, row_recv, item_send, item_recv) = refs
+     turned, keys, values, queries, go, text_kv, cols, shifted, acc, own, slots,
+     key_land, value_land, query_land, go_land, text_pair, o, dq, dkv, dtext,
+     load, sum_send, sum_recv, edge_send, edge_recv, row_send, row_recv, item_send, item_recv,
+     *scratch) = refs
     grid = Grid(items, n)
     item, me = grid.item, grid.me
     rows_dev, width, channels = image.shape
@@ -947,6 +1009,7 @@
     heads, head_dim, wide = HEADS, channels // HEADS, 3 * channels // HEADS
     base = me * rows_dev
     count = (info[0, 0] * info[0, 1]).astype(F32) * (channels // GROUPS)
+    att = Attention(n, pixels, head_dim, n * text.shape[0], step, bq, scratch)
 
     def inside(row):
         return window(info, 0, row, (width, channels))
@@ -1024,14 +1087,13 @@
     each_row(rows_dev, to_grad)
     for h in range(heads):
         go[h] = dot(proj_w[h * head_dim : (h + 1) * head_dim], attn[...], 1, 1).astype(BF16)
-    go_copy = scatter(2, go, go_pair)
-    own_go = fetch(go.at[me], go_pair.at[me])
+    go_copy = scatter(2, go, go_land)
+    own_go = fetch(go.at[me], go_land.at[me])
 
     stats = sums[0].result()
     stats_out[0] = stats
     average, inverse = norm_of(stats, count)
     edges[0].wait()
-    grid.loop(n, lambda k: go_copy(k).start())
 
     def to_hidden(r):
         ok = inside(base + r - 1)
@@ -1097,7 +1159,6 @@
     own[2] = row_stats(rows_dev, width, channels, middle_row)
     sums[2].start()
     edges[3].start()
-    own_go.wait()
     edges[1].wait()
     own_cot = fetch(cot_v, cot_out)
     got_qkv_w.wait()
@@ -1116,36 +1177,132 @@
 
     each_row(rows_dev, to_attn)
     own_attn = fetch(attn, attn_out)
-    qkv_copy = scatter(3, qkv, qkv_pair)
-
-    def head(k, carry):
+    key_copy = scatter(3, keys, key_land)
+    value_copy = scatter(4, values, value_land)
+    query_copy = scatter(5, queries, query_land)
+
+    def head(k):
         to = lax.rem(me + k, n)
         rows = pl.ds(pl.multiple_of(to * wide, wide), wide)
-        qkv[to] = dot(turned[rows], attn[...], 1, 1).astype(BF16)
-        return carry
-
-    def send_head(k, carry):
-        head(k, carry)
-        qkv_copy(k).start()
-        return carry
-
-    lax.fori_loop(1, n, send_head, 0)
-    head(0, 0)
-    own_qkv = fetch(qkv.at[me], qkv_pair.at[me])
+        block = dot(turned[rows], attn[...], 1, 1).astype(BF16)
+        queries[to] = block[:head_dim]
+        keys[to] = block[head_dim : 2 * head_dim]
+        values[to] = block[2 * head_dim :]
+
+    def send_head(k):
+        head(k)
+        key_copy(k).start()
+
+    grid.loop(n, send_head)
+    head(0)
+    query_land[me] = queries[me]
+    att.stage_key(me, keys[me], width, info[0, 0], info[0, 1])
+    att.stage_value(me, values[me])
+    grid.loop(n, lambda k: kv_copy(k).wait())
+    own_kv.wait()
+    att.stage_text(text_pair[...].reshape(n * text.shape[0], 2 * head_dim))
     edges[3].wait()
     own_mid = fetch(mid_v, mid_out)
 
-    grid.loop(n, lambda k: kv_copy(k).wait())
+    def source(k):
+        return lax.rem(me + n - k, n)
+
+    def stage_key(k):
+        key_copy(k).wait()
+        att.stage_key(source(k), key_land[source(k)], width, info[0, 0], info[0, 1])
+
+    grid.loop(n, stage_key)
+    grid.loop(n, lambda k: value_copy(k).start())
+
+    def scored():
+        def stage_value(k):
+            value_copy(k).wait()
+            att.stage_value(source(k), value_land[source(k)])
+
+        grid.loop(n, stage_value)
+
+        def rest(k):
+            query_copy(k).start()
+            go_copy(k).start()
+
+        grid.loop(n, rest)
+        own_go.wait()
+
+    def before(k):
+        query_copy(k).wait()
+        go_copy(k).wait()
+
+    def give(j, src, dst):
+        def copy(h):
+            to = source(h)
+            return remote(
+                src.at[to],
+                dst.at[me],
+                row_send.at[j, h],
+                row_recv.at[j, h],
+                {"items": item, "rows": to},
+            )
+
+        return copy
+
+    o_copy = give(6, o, o_out)
+    dq_copy = give(7, dq, dq_out)
+    dkv_copy = give(8, dkv, dkv_out)
+    dt_copy = give(9, dtext, dt_out)
+
+    def done(h):
+        @pl.when(h > 0)
+        def _():
+            o_copy(h).start()
+            dq_copy(h).start()
+
+    att.attend(query_land, go_land, o, dq, source, scored, before, done)
+
+    def send_keys(h):
+        at = pl.ds(pl.multiple_of(source(h) * pixels, pixels), pixels)
+        dkv[source(h), :head_dim] = att.key_grad(at)
+        dkv[source(h), head_dim:] = att.value_grad(at)
+
+    def send_next(h):
+        send_keys(h)
+        dkv_copy(h).start()
+
+    grid.loop(n, send_next)
+    send_keys(0)
+    flat = jnp.concatenate(
+        [
+            (att.dkt[:, n * pixels :] * (head_dim**-0.5)).T,
+            att.dvt[:, n * pixels :].T,
+        ],
+        axis=1,
+    )
+    for r in range(n):
+        tokens = text.shape[0]
+        dtext[r] = flat[r * tokens : (r + 1) * tokens].astype(BF16)
+    grid.loop(n, lambda h: dt_copy(h).start())
+
+    def gather_copy(k):
+        return remote(
+            dtext, dt_all.at[item, me], row_send.at[10, k], row_recv.at[10, k], grid.row(k)
+        )
+
+    grid.loop(n, lambda k: gather_copy(k).start())
+    own_o = fetch(o.at[me], o_out.at[me])
+    own_dq = fetch(dq.at[me], dq_out.at[me])
+    own_dkv = fetch(dkv.at[me], dkv_out.at[me])
+    own_dt = fetch(dtext.at[me], dt_out.at[me])
+    own_all = fetch(dtext, dt_all.at[item, me])
     grid.loop(n, lambda k: col_copy(k).wait())
     own_col.wait()
     cols_copy = spread(2, text_cols.at[item], text_cols)
     grid.loop(items, lambda k: cols_copy(k).start())
-    grid.loop(n, lambda k: go_copy(k).wait())
-    grid.loop(n, lambda k: qkv_copy(k).wait())
     grid.loop(items, lambda k: hidden_copy(k).wait())
     grid.loop(items, lambda k: second_copy(k).wait())
     grid.loop(items, lambda k: cols_copy(k).wait())
-    for c in (own_kv, own_hidden, own_first, own_second, own_cot, own_turned, own_attn, own_qkv, own_mid):
+    for copy in (o_copy, dq_copy, dkv_copy, dt_copy, gather_copy):
+        grid.loop(n, lambda h: copy(h).wait())
+    for c in (own_hidden, own_first, own_second, own_cot, own_turned, own_attn, own_mid, own_o, own_dq, own_dkv,
+              own_dt, own_all):
         c.wait()
 
 
@@ -1166,9 +1323,11 @@
         sds((items,) + padded, BF16),
         sds((pixels, channels), BF16),
         sds((3 * channels, channels), BF16),
-        sds((n, 3 * head_dim, pixels), BF16),
         sds((n, head_dim, pixels), BF16),
+        sds((n, head_dim, pixels), BF16),
+        sds((n, 2 * head_dim, pixels), BF16),
         sds((n, tokens, 2 * head_dim), BF16),
+        sds((items, n, n, tokens, 2 * head_dim), BF16),
         sds((items, n, tokens, text_width // n), BF16),
         sds((3, 8, channels), F32),
         sds((1, 2 * channels), F32),
@@ -1190,7 +1349,9 @@
         v(padded, BF16),
         v((pixels, channels), BF16),
         v((3 * channels, channels), BF16),
-        v((n, 3 * head_dim, pixels), BF16),
+        v((n, head_dim, pixels), BF16),
+        v((n, head_dim, pixels), BF16),
+        v((n, head_dim, pixels), BF16),
         v((n, head_dim, pixels), BF16),
         v((n, tokens, 2 * head_dim), BF16),
         v((n, tokens, text_width // n), BF16),
@@ -1198,24 +1359,35 @@
         v((pixels, channels), F32),
         v((3, 8, channels), F32),
         v((3, n, 8, channels), F32),
-        DMA((24,)),
+        v((n, head_dim, pixels), BF16),
+        v((n, head_dim, pixels), BF16),
+        v((n, head_dim, pixels), BF16),
+        v((n, head_dim, pixels), BF16),
+        v((n, tokens, 2 * head_dim), BF16),
+        v((n, head_dim, pixels), BF16),
+        v((n, head_dim, pixels), BF16),
+        v((n, 2 * head_dim, pixels), BF16),
+        v((n, tokens, 2 * head_dim), BF16),
+        DMA((28,)),
         DMA((3, n)),
         DMA((3, n)),
         DMA((4, 2)),
         DMA((4, 2)),
-        DMA((4, n)),
-        DMA((4, n)),
+        DMA((11, n)),
+        DMA((11, n)),
         DMA((3, items)),
         DMA((3, items)),
     ]
+    step, bq, extra = attention_scratch(n, pixels, head_dim, n * tokens)
+    scratch += extra
     return pl.pallas_call(
-        functools.partial(forward_kernel, items, n),
+        functools.partial(forward_kernel, items, n, step, bq),
         out_shape=outs,
         in_specs=[SCALARS] + [ANYWHERE] * 3 + [WHOLE] * 4 + [ANYWHERE] * 6,
-        out_specs=(ANYWHERE,) * 11 + (WHOLE,) * 2,
+        out_specs=(ANYWHERE,) * 13 + (WHOLE,) * 2,
         scratch_shapes=scratch,
         compiler_params=pltpu.CompilerParams(
-            collective_id=identity, has_side_effects=True, vmem_limit_bytes=56 << 20
+            collective_id=identity, has_side_effects=True, vmem_limit_bytes=62 << 20
         ),
         cost_estimate=pl.CostEstimate(
             flops=40 * pixels * channels * channels, bytes_accessed=60 << 20, transcendentals=0
@@ -1448,7 +1620,7 @@
 
 def backward_kernel(items, n, *refs):
     (info, embed, gain1, gain2, gain3, stats_in, shifts,
-     o_pair, dqkv_pair, dtext, first, middle, cot, image, hidden_all, second_all, attn_in, turned_in, text_cols,
+     o_in, dq_in, dkv_in, dt_in, dt_all, first, middle, cot, image, hidden_all, second_all, attn_in, turned_in, text_cols,
      proj_in, w1_in, w2_in, text_in, embed_in,
      output, image_grad, conv1_out, conv2_out, qkv_out, proj_out, vectors, text_grad, text_w_grad, embed_grad,
      weight, proj_w, qkv_turned, first_v, mid_v, cot_v, image_v, attn, cols, rows_v, dq, o, dt, own_dt,
@@ -1456,7 +1628,7 @@
      turned, quarter, part, from_core, chip_sum, from_chip, final,
      side_v, side_core, side_sum, side_item, side_total, side_chip, side_final,
      vector, vector_land, own, slots,
-     load, sum_send, sum_recv, edge_send, edge_recv, row_send, row_recv, dt_send, dt_recv, vec_send, vec_recv,
+     load, sum_send, sum_recv, edge_send, edge_recv, dt_send, dt_recv, vec_send, vec_recv,
      k_item_send, k_item_recv, k_core_send, k_core_recv, k_chip_send, k_chip_recv, k_final_send, k_final_recv,
      s_core_send, s_core_recv, s_item_send, s_item_recv, s_chip_send, s_chip_recv, s_final_send,
      s_final_recv) = refs
@@ -1481,24 +1653,18 @@
         fetched.append(c)
         return c
 
-    def scatter(j, src, dst):
-        def copy(k):
-            to = lax.rem(me + k, n)
-            return remote(src.at[to], dst.at[me], row_send.at[j, k], row_recv.at[j, k], grid.row(k))
-
-        return copy
-
-    own_dq = fetch(dqkv_pair.at[me], dq.at[me])
+    got_dq = fetch(dq_in, dq.at[:, :head_dim])
+    got_dkv = fetch(dkv_in, dq.at[:, head_dim:])
     got_turned = fetch(turned_in, qkv_turned)
     got_mid = fetch(middle, mid_v)
     got_cot = fetch(cot, cot_v)
     got_w2 = fetch(w2_in, weight)
     got_first = fetch(first, first_v)
     got_attn = fetch(attn_in, attn)
-    own_o = fetch(o_pair.at[me], o.at[me])
+    got_o = fetch(o_in, o)
     got_proj = fetch(proj_in, proj_w)
-    own_text = fetch(dtext.at[me], own_dt.at[me])
-    own_all = fetch(dtext, dt.at[item, me])
+    got_dt = fetch(dt_in, own_dt)
+    got_all = fetch(dt_all.at[item], dt.at[item])
     got_second = fetch(second_all, rows_v)
     got_image = fetch(image, image_v)
     got_cols = fetch(text_cols, cols)
@@ -1520,33 +1686,23 @@
     side = SideSum(grid, side_v, side_core, side_sum, side_item, side_total, side_chip, side_final,
                    (s_core_send, s_core_recv), (s_item_send, s_item_recv), (s_chip_send, s_chip_recv),
                    (s_final_send, s_final_recv))
-    dq_copy = scatter(0, dqkv_pair, dq)
-    o_copy = scatter(1, o_pair, o)
-    text_copy = scatter(2, dtext, own_dt)
-
-    def gather_copy(k):
-        return remote(
-            dtext, dt.at[item, me], row_send.at[3, k], row_recv.at[3, k], grid.row(k)
-        )
-
-    grid.met()
-    grid.loop(n, lambda k: dq_copy(k).start())
-    grid.loop(n, lambda k: o_copy(k).start())
-    grid.loop(n, lambda k: text_copy(k).start())
-    grid.loop(n, lambda k: gather_copy(k).start())
+
+    def dt_copy(k):
+        mine = dt.at[item]
+        return remote(mine, mine, dt_send.at[k], dt_recv.at[k], grid.peer(k))
 
     got_turned.wait()
-    own_dq.wait()
+    got_dq.wait()
+    got_dkv.wait()
 
     def unproject_head(h):
         rows = pl.ds(pl.multiple_of(h * wide, wide), wide)
         return dot(dq[h].astype(F32).T.astype(BF16), qkv_turned[rows], 1, 0)
 
-    acc[...] = unproject_head(me)
-
-    def next_head(k):
-        dq_copy(k).wait()
-        acc[...] += unproject_head(lax.rem(me + n - k, n))
+    acc[...] = unproject_head(0)
+
+    def next_head(h):
+        acc[...] += unproject_head(h)
 
     grid.loop(n, next_head)
     got_mid.wait()
@@ -1558,8 +1714,11 @@
         return value, value * ((mid_v[1 + r] - average) * inverse)
 
     own[0] = row_stats(rows_dev, width, channels, grad_row)
+    grid.met()
     sums[0].start()
     edges[0].start()
+    got_all.wait()
+    grid.loop(items, lambda k: dt_copy(k).start())
 
     got_attn.wait()
 
@@ -1579,6 +1738,14 @@
 
     each_row(rows_dev, mask_row)
 
+    got_o.wait()
+    flat_o = o[...].reshape(channels, pixels)
+    block = dot(masked[...].astype(F32).T.astype(BF16), flat_o, 1, 1).astype(BF16)
+    for r in range(n):
+        rows = block[r * share : (r + 1) * share]
+        side_v[r % 2, r // 2, :, :, 3 * channels :] = rows.reshape(items, share // items, channels)
+    side.core_copy().start()
+
     stats4 = sums[0].result()
     mean, cross = means_of(stats4, gain3[...], count)
     edges[0].wait()
@@ -1593,6 +1760,7 @@
 
     each_row(rows_dev + 2, to_grad2)
     sum2.send_grads(shifted)
+    side.over_items()
     got_w2.wait()
     conv_taps_back(shifted, weight, acc, rows_dev)
     got_first.wait()
@@ -1621,15 +1789,6 @@
     for a in range(3):
         sum2.compute(a, shifted_all)
 
-    own_o.wait()
-    grid.loop(n, lambda k: o_copy(k).wait())
-    flat_o = o[...].reshape(channels, pixels)
-    block = dot(masked[...].astype(F32).T.astype(BF16), flat_o, 1, 1).astype(BF16)
-    for r in range(n):
-        rows = block[r * share : (r + 1) * share]
-        side_v[r % 2, r // 2, :, :, 3 * channels :] = rows.reshape(items, share // items, channels)
-    side.core_copy().start()
-
     stats5 = sums[1].result()
     factor = gain2[...] * (1.0 + scale)
     mean, cross = means_of(stats5, factor, count)
@@ -1642,6 +1801,7 @@
 
     each_row(rows_dev + 2, to_grad1)
     sum1.send_grads(shifted)
+    side.over_chips()
     for a in range(3):
         sum2.over_chips(a)
     got_w1.wait()
@@ -1663,7 +1823,6 @@
         fetch(text_in.at[:, j * channels : (j + 1) * channels], weight.at[j * tall : (j + 1) * tall])
         for j in range(2)
     ]
-    side.over_items()
     got_hidden.wait()
     shift_rows()
     sum1.wait_grads()
@@ -1675,7 +1834,7 @@
     sum1.over_chips(2)
     for a in range(3):
         sum2.over_items(a)
-    side.over_chips()
+    side.spread()
 
     stats6 = sums[2].result()
     e = embed[...].astype(F32)
@@ -1697,14 +1856,6 @@
     grid.loop(items, lambda k: vector_copy(k).start())
     vector_land[item] = vector[...]
 
-    grid.loop(n, lambda k: gather_copy(k).wait())
-    own_all.wait()
-
-    def dt_copy(k):
-        mine = dt.at[item]
-        return remote(mine, mine, dt_send.at[k], dt_recv.at[k], grid.peer(k))
-
-    grid.loop(items, lambda k: dt_copy(k).start())
     mean, cross = means_of(stats6, gain1[...], count)
 
     def finish_row(r):
@@ -1714,7 +1865,6 @@
 
     each_row(rows_dev, finish_row)
     put_image = fetch(image_out, image_grad)
-    side.spread()
 
     got_proj.wait()
     acc[...] = dot(flat_o.astype(F32).T.astype(BF16), proj_w[...], 1, 0)
@@ -1726,8 +1876,7 @@
     each_row(rows_dev, output_row)
     put_output = fetch(out_v, output)
 
-    own_text.wait()
-    grid.loop(n, lambda k: text_copy(k).wait())
+    got_dt.wait()
     for c in got_text_w:
         c.wait()
     half = heads // 2
@@ -1774,8 +1923,8 @@
 
 def backward_call(info, embed, gains, stats, shifts, arrays, identity):
     items, n = lax.axis_size("items"), lax.axis_size("rows")
-    o_pair, dqkv_pair, dtext = arrays[:3]
-    image, text_cols, text_w = arrays[6], arrays[11], arrays[15]
+    o_pair, _, _, dtext = arrays[:4]
+    image, text_cols, text_w = arrays[8], arrays[13], arrays[17]
     rows_dev, width, channels = image.shape
     pixels = rows_dev * width
     head_dim = channels // HEADS
@@ -1809,7 +1958,7 @@
         v((pixels, channels), BF16),
         v(text_cols.shape, BF16),
         v((items,) + padded, BF16),
-        v(dqkv_pair.shape, BF16),
+        v((n, 3 * head_dim, pixels), BF16),
         v(o_pair.shape, BF16),
         v((items, n) + dtext.shape, BF16),
         v(dtext.shape, BF16),
@@ -1846,8 +1995,6 @@
         DMA((3, n)),
         DMA((2, 2)),
         DMA((2, 2)),
-        DMA((4, n)),
-        DMA((4, n)),
         DMA((items,)),
         DMA((items,)),
         DMA((items,)),
@@ -1895,8 +2042,8 @@
     head_dim = channels // HEADS
     tokens = text.shape[1]
     share = channels // parts
-    (first, middle, cot, hidden_all, second_all, attn_flat, qkv_turned, qkv_pair, go_pair, text_pair, text_cols,
-     stats, shifts) = forward_call(
+    (first, middle, cot, hidden_all, second_all, attn_flat, qkv_turned, attended, dq, dkv, own_dt, all_dt,
+     text_cols, stats, shifts) = forward_call(
         info,
         image[0],
         cotangent[0],
@@ -1913,11 +2060,6 @@
         ),
         0,
     )
-    stats1, stats2, stats3 = stats[0:1], stats[1:2], stats[2:3]
-    attended, qkv_grad_pair, text_grad_pair = attention(
-        info[:, :2], qkv_pair, text_pair.reshape(parts * tokens, 2 * head_dim), go_pair, width
-    )
-
     text_w_rows = text_cols.shape[3]
     (output, image_grad, conv1_total, conv2_total, qkv_total, proj_total, vectors, text_grad, text_w_grad,
      embed_grad) = backward_call(
@@ -1928,8 +2070,10 @@
         shifts,
         (
             attended,
-            qkv_grad_pair,
-            text_grad_pair.reshape(parts, tokens, 2 * head_dim),
+            dq,
+            dkv,
+            own_dt,
+            all_dt,
             first,
             middle,
             cot,

time: 286 us -> 258 us (0.902)
  Pallas kernels: 265 us -> 238 us
    pallas_call x1, Pallas kernels: 128 us -> 80.8 us  [backward_call(): pl.pallas_call(functools.partial(backward_kernel, items, n), out_shape=ou...]
    pallas_call x2 -> x1, Pallas kernels: 137 us -> 157 us  [forward_call(): pl.pallas_call(functools.partial(forward_kernel, items, n, step, bq), out...]
where the time goes in v2:
time: 258 us; the launch traced here: 257 us
  Pallas kernels  238 us (92%)
  local copies, waits for them, and re-layouts  14 us (5%)
  other arithmetic  3.01 us (1%)
    pallas_call x1, Pallas kernels, forward_call(): pl.pallas_call(functools.partial(forward_kernel, items, n, step, bq), out...  157 us
    pallas_call x1, Pallas kernels, backward_call(): pl.pallas_call(functools.partial(backward_kernel, items, n), out_shape=ou...  80.8 us
    unnamed x23, local copies, waits for them, and re-layouts  13.4 us

profile of v2, /device:TPU:0, one launch (start us, length us, event | category | flops | bytes accessed | tf_op | source)
XLA Modules:
  0.0 257.0 jit_solution(13232509397222712316)
XLA Ops:
  0.6 1.2 pad_add_fusion.refs_0_
  1.9 157.1 %forward.1 = (f32[10,64,512]{2,1,0:T(8,128)}, f32[10,64,512]{2,1,0:T(8,128)}, bf16[10,64,512]{2,1,0:T(8,128)(2,1)}, bf16[4,10,64,512]{3,2,1,0:T(8,128)(2,1)}, bf...) custom-call(s32[1,3]{1,0:T(1,128)} %pad_add_fusion.refs_0_, ...), custom_call_target="tpu_custom_call" | custom-call | flops 5368709120 | bytes 62914560 | tf_op jit(solution)/shard_map/forward/pallas_call | solution.py:1383
  159.0 80.8 %backward.1 = (bf16[8,64,512]{2,1,0:T(8,128)(2,1)}, f32[8,64,512]{2,1,0:T(8,128)}, f32[4608,64]{1,0:T(8,128)}, f32[4608,64]{1,0:T(8,128)}, f32[512,192]{1,0:T(8,...) custom-call(s32[1,3]{1,0:T(1,128)} %pad_add_fusion.refs_0_, ...), custom_call_target="tpu_custom_call" | custom-call | flops 10737418240 | bytes 62914560 | tf_op jit(solution)/shard_map/backward/pallas_call | solution.py:2019
  239.8 0.9 convert.4
  240.7 0.0 copy-start
  240.8 1.3 fusion
  242.2 2.8 %copy.27 = f32[3,3,512,64]{2,3,1,0:T(8,128)} copy(f32[3,3,512,64]{3,2,1,0:T(8,128)} %bitcast.35) | data formatting | bytes 2359296
  245.0 0.0 copy-done
  245.0 0.0 copy-start.2
  245.0 1.7 copy.28
  246.7 0.0 copy-start.4
  246.7 0.0 copy-start.3
  246.7 0.0 copy-start.1
  246.7 2.1 copy.29
  248.7 1.7 copy.30
  250.5 0.9 slice_reduce_fusion
  251.3 0.1 constant_dynamic-slice_fusion
  251.4 0.5 slice_bitcast_fusion.2
  251.9 1.9 copy.38
  253.8 0.0 copy-done.2
  253.8 1.0 copy.39
  254.8 0.0 copy-done.4
  254.8 0.6 copy.40
  255.4 0.0 copy-done.3
  255.4 0.7 copy.41
  256.0 0.0 copy-done.1
  256.0 1.0 copy.42
  (4 shorter events, 0.0 us)
Async XLA Ops:
  240.7 4.2 %copy-start = (f32[4608,64]{1,0:T(8,128)S(1)}, f32[4608,64]{1,0:T(8,128)}, u32[]{:S(2)}) copy-start(f32[4608,64]{1,0:T(8,128)} %get-tuple-element.59) | copy-start | bytes 3538948
  245.0 8.8 %copy-start.2 = (f32[8,64,512]{2,1,0:T(8,128)S(1)}, f32[8,64,512]{2,1,0:T(8,128)}, u32[]{:S(2)}) copy-start(f32[8,64,512]{2,1,0:T(8,128)} %get-tuple-element.54) | copy-start | bytes 3145732
  246.7 8.1 %copy-start.4 = (f32[1,2048]{1,0:T(1,128)S(1)}, f32[1,2048]{1,0:T(1,128)}, u32[]{:S(2)}) copy-start(f32[1,2048]{1,0:T(1,128)} %get-tuple-element.94) | copy-start | bytes 24580
  246.7 8.7 %copy-start.3 = (f32[16,2048]{1,0:T(8,128)S(1)}, f32[16,2048]{1,0:T(8,128)}, u32[]{:S(2)}) copy-start(f32[16,2048]{1,0:T(8,128)} %get-tuple-element.56) | copy-start | bytes 393220
  246.7 9.4 %copy-start.1 = (f32[256,1024]{1,0:T(8,128)S(1)}, f32[256,1024]{1,0:T(8,128)}, u32[]{:S(2)}) copy-start(f32[256,1024]{1,0:T(8,128)} %get-tuple-element.103) | copy-start | bytes 3145732

commit v3 on v2

--- a/solution.py
+++ b/solution.py
@@ -386,32 +386,37 @@
     )(stats, *rows, *given)
 
 
-def group_sums(rows):
-    channels = rows.shape[1]
+def group_matrix(channels):
     size = channels // GROUPS
     one = lax.broadcasted_iota(jnp.int32, (channels, channels), 0) // size
     two = lax.broadcasted_iota(jnp.int32, (channels, channels), 1) // size
-    same = jnp.where(one == two, 1.0, 0.0).astype(BF16)
-    high = rows.astype(BF16)
-    rest = rows - high.astype(F32)
-    mid = rest.astype(BF16)
-    tail = (rest - mid.astype(F32)).astype(BF16)
-    return dot(high, same, 1, 0) + dot(mid, same, 1, 0) + dot(tail, same, 1, 0)
+    return jnp.where(one == two, 1.0, 0.0).astype(BF16)
+
+
+def group_sums(rows, same=None):
+    if same is None:
+        same = group_matrix(rows.shape[1])
+    high = rows.astype(BF16).astype(F32)
+    mid = (rows - high).astype(BF16).astype(F32)
+    tail = rows - high - mid
+    sums = dot(jnp.concatenate([high, mid, tail], axis=0).astype(BF16), same, 1, 0)
+    n = rows.shape[0]
+    return sums[:n] + sums[n : 2 * n] + sums[2 * n :]
 
 
 def image_count(info, i, channels):
     return (info[i, 0] * info[i, 1]).astype(F32) * (channels // GROUPS)
 
 
-def norm_of(stats, count):
-    sums = group_sums(stats)
+def norm_of(stats, count, same=None):
+    sums = group_sums(stats, same)
     average = sums[0:1] / count
     square = sums[1:2] / count
     return average, lax.rsqrt(square - average * average + EPS)
 
 
-def means_of(stats, weight, count):
-    sums = group_sums(stats * weight)
+def means_of(stats, weight, count, same=None):
+    sums = group_sums(stats * weight, same)
     return sums[0:1] / count, sums[1:2] / count
 
 
@@ -999,7 +1004,7 @@
      dt_all, text_cols, stats_out, shifts_out,
      image_v, cot_v, text_v, w1, w2, embed_w, text_w, qkv_w, proj_w, first_v, mid_v, hidden, second, attn,
      turned, keys, values, queries, go, text_kv, cols, shifted, acc, own, slots,
-     key_land, value_land, query_land, go_land, text_pair, o, dq, dkv, dtext,
+     key_land, value_land, query_land, go_land, text_pair, o, dq, dkv, dtext, same,
      load, sum_send, sum_recv, edge_send, edge_recv, row_send, row_recv, item_send, item_recv,
      *scratch) = refs
     grid = Grid(items, n)
@@ -1040,6 +1045,7 @@
     grid.greet()
     for e in edges:
         e.clear()
+    same[...] = group_matrix(channels)
     got_image.wait()
 
     def start_row(r):
@@ -1092,7 +1098,7 @@
 
     stats = sums[0].result()
     stats_out[0] = stats
-    average, inverse = norm_of(stats, count)
+    average, inverse = norm_of(stats, count, same[...])
     edges[0].wait()
 
     def to_hidden(r):
@@ -1133,7 +1139,7 @@
 
     stats = sums[1].result()
     stats_out[1] = stats
-    average, inverse = norm_of(stats, count)
+    average, inverse = norm_of(stats, count, same[...])
     edges[2].wait()
     own_first = fetch(first_v, first_out)
 
@@ -1169,7 +1175,7 @@
 
     stats = sums[2].result()
     stats_out[2] = stats
-    average, inverse = norm_of(stats, count)
+    average, inverse = norm_of(stats, count, same[...])
 
     def to_attn(r):
         value = (mid_v[1 + r] - average) * inverse * inside(base + r) * gain3[...]
@@ -1368,6 +1374,7 @@
         v((n, head_dim, pixels), BF16),
         v((n, 2 * head_dim, pixels), BF16),
         v((n, tokens, 2 * head_dim), BF16),
+        v((channels, channels), BF16),
         DMA((28,)),
         DMA((3, n)),
         DMA((3, n)),
@@ -1496,14 +1503,9 @@
         for k in range(1, self.grid.items):
             self.final_copy(a, k).start()
 
-    def put(self, a, out):
+    def wait_final(self, a):
         for k in range(1, self.grid.items):
             self.final_copy(a, k).wait()
-        channels = self.final.shape[4]
-        for b in range(3):
-            rows = [self.final[a, q, b].astype(F32) for q in range(self.grid.items)]
-            at = (a * 3 + b) * channels
-            out[at : at + channels] = jnp.concatenate(rows, axis=0).T
 
 
 class SideSum:
@@ -1587,16 +1589,9 @@
         for k in range(1, self.grid.items):
             self.final_copy(k).start()
 
-    def put(self, qkv_out, proj_out):
+    def wait_final(self):
         for k in range(1, self.grid.items):
             self.final_copy(k).wait()
-        rows = jnp.concatenate(
-            [self.final[q].astype(F32) for q in range(self.grid.items)], axis=0
-        )
-        share, channels = rows.shape[0], rows.shape[1] // 4
-        for w in range(3):
-            qkv_out[:, w * share : (w + 1) * share] = rows[:, w * channels : (w + 1) * channels].T
-        proj_out[...] = rows[:, 3 * channels :].T
 
 
 def conv_taps_back(shifted, weight, acc, rows_dev):
@@ -1622,9 +1617,9 @@
     (info, embed, gain1, gain2, gain3, stats_in, shifts,
      o_in, dq_in, dkv_in, dt_in, dt_all, first, middle, cot, image, hidden_all, second_all, attn_in, turned_in, text_cols,
      proj_in, w1_in, w2_in, text_in, embed_in,
-     output, image_grad, conv1_out, conv2_out, qkv_out, proj_out, vectors, text_grad, text_w_grad, embed_grad,
+     output, image_grad, text_grad, text_w_grad, embed_grad, final_out, side_out, vectors,
      weight, proj_w, qkv_turned, first_v, mid_v, cot_v, image_v, attn, cols, rows_v, dq, o, dt, own_dt,
-     grad_v, grad_mid, moved_v, pre, acc, shifted, shifted_all, masked, out_v, image_out,
+     grad_v, grad_mid, moved_v, pre, acc, shifted, shifted_all, masked, out_v, image_out, text_v, text_w_v, embed_v, same,
      turned, quarter, part, from_core, chip_sum, from_chip, final,
      side_v, side_core, side_sum, side_item, side_total, side_chip, side_final,
      vector, vector_land, own, slots,
@@ -1675,6 +1670,7 @@
     ]
     for e in edges:
         e.clear()
+    same[...] = group_matrix(channels)
     sums = [Sums(grid, own.at[j], slots.at[j], sum_send.at[j], sum_recv.at[j]) for j in range(3)]
     kernel_sums = [
         KernelSum(grid, turned.at[j], quarter.at[j], part.at[j], from_core.at[j], chip_sum.at[j], from_chip.at[j],
@@ -1706,7 +1702,7 @@
 
     grid.loop(n, next_head)
     got_mid.wait()
-    average, inverse = norm_of(stats_in[2], count)
+    average, inverse = norm_of(stats_in[2], count, same[...])
 
     def grad_row(r):
         value = acc[pl.ds(r * width, width)] * inside(base + r)
@@ -1747,7 +1743,7 @@
     side.core_copy().start()
 
     stats4 = sums[0].result()
-    mean, cross = means_of(stats4, gain3[...], count)
+    mean, cross = means_of(stats4, gain3[...], count, same[...])
     edges[0].wait()
 
     def to_grad2(r):
@@ -1764,7 +1760,7 @@
     got_w2.wait()
     conv_taps_back(shifted, weight, acc, rows_dev)
     got_first.wait()
-    average2, inverse2 = norm_of(stats_in[1], count)
+    average2, inverse2 = norm_of(stats_in[1], count, same[...])
 
     def moved_row(r):
         ok = inside(base + r)
@@ -1791,7 +1787,7 @@
 
     stats5 = sums[1].result()
     factor = gain2[...] * (1.0 + scale)
-    mean, cross = means_of(stats5, factor, count)
+    mean, cross = means_of(stats5, factor, count, same[...])
     edges[1].wait()
 
     def to_grad1(r):
@@ -1807,7 +1803,7 @@
     got_w1.wait()
     conv_taps_back(shifted, weight, acc, rows_dev)
     got_image.wait()
-    average1, inverse1 = norm_of(stats_in[0], count)
+    average1, inverse1 = norm_of(stats_in[0], count, same[...])
 
     def pre_row(r):
         ok = inside(base + r)
@@ -1856,7 +1852,7 @@
     grid.loop(items, lambda k: vector_copy(k).start())
     vector_land[item] = vector[...]
 
-    mean, cross = means_of(stats6, gain1[...], count)
+    mean, cross = means_of(stats6, gain1[...], count, same[...])
 
     def finish_row(r):
         normal = (image_v[r].astype(F32) - average1) * inverse1
@@ -1885,7 +1881,8 @@
         lhs = jnp.concatenate([own_dt[j * half + h] for h in range(half)], axis=1)
         term = dot(lhs, weight[j * tall : (j + 1) * tall], 1, 1)
         total = term if total is None else total + term
-    text_grad[...] = total
+    text_v[...] = total
+    put_text = fetch(text_v, text_grad)
     got_embed_w = [
         fetch(embed_in.at[:, j * channels : (j + 1) * channels], weight.at[j * tall : (j + 1) * tall])
         for j in range(2)
@@ -1893,7 +1890,8 @@
     for a in range(3):
         sum1.over_items(a)
     for a in range(3):
-        sum2.put(a, conv2_out)
+        sum2.wait_final(a)
+    put_final2 = fetch(final.at[0], final_out.at[0])
 
     grid.loop(items, lambda k: dt_copy(k).wait())
     got_cols.wait()
@@ -1901,7 +1899,8 @@
     flat_cols = cols[...].reshape(tokens, cols.shape[2]).astype(F32).T.astype(BF16)
     for h in range(heads):
         rhs = jnp.concatenate([dt[g, h].reshape(tokens // items, 2 * head_dim) for g in range(items)], axis=0)
-        text_w_grad[:, h * 2 * head_dim : (h + 1) * 2 * head_dim] = dot(flat_cols, rhs, 1, 0)
+        text_w_v[:, h * 2 * head_dim : (h + 1) * 2 * head_dim] = dot(flat_cols, rhs, 1, 0)
+    put_text_w = fetch(text_w_v, text_w_grad)
 
     for c in got_embed_w:
         c.wait()
@@ -1911,14 +1910,124 @@
         lhs = jnp.broadcast_to(lhs, (8, channels)).astype(BF16)
         term = dot(lhs, weight[j * tall : (j + 1) * tall], 1, 1)
         total = term if total is None else total + term
-    embed_grad[...] = total[0:1] * silu_slope(e)
-    side.put(qkv_out, proj_out)
+    embed_v[...] = total[0:1] * silu_slope(e)
+    put_embed = fetch(embed_v, embed_grad)
+    grid.loop(items, lambda k: vector_copy(k).wait())
+    put_vectors = fetch(vector_land, vectors)
+    side.wait_final()
+    put_side = fetch(side_final, side_out)
     for a in range(3):
-        sum1.put(a, conv1_out)
-    grid.loop(items, lambda k: vector_copy(k).wait())
-    vectors[...] = vector_land[...]
-    put_image.wait()
-    put_output.wait()
+        sum1.wait_final(a)
+    put_final1 = fetch(final.at[1], final_out.at[1])
+    for c in (put_image, put_output, put_text, put_final2, put_text_w, put_embed, put_vectors, put_side, put_final1):
+        c.wait()
+
+
+def finalize_kernel(final, side, vectors, output_in, image_in, text_in, text_w_in, embed_in,
+                    output, image_grad, text_grad, text_w_grad, embed_grad, conv2, conv1, qkv, proj, embed_w,
+                    gain1, gain2, gain3,
+                    final_v, side_v, vector_v, conv_v, qkv_v, proj_v, embed_w_v, output_v, image_v, text_v, text_w_v,
+                    embed_v, load):
+    started = []
+
+    def fetch(src, dst):
+        c = pltpu.make_async_copy(src, dst, load.at[len(started)])
+        c.start()
+        started.append(c)
+        return c
+
+    got = [fetch(final.at[j], final_v.at[j]) for j in range(2)]
+    got_vectors = fetch(vectors, vector_v)
+    got_side = fetch(side, side_v)
+    through = ((image_in, image_v, image_grad), (text_w_in, text_w_v, text_w_grad), (output_in, output_v, output),
+               (text_in, text_v, text_grad), (embed_in, embed_v, embed_grad))
+    got_through = [fetch(src, held) for src, held, _ in through]
+    me = lax.axis_index("rows")
+    items, rows, channels = side_v.shape[0], side_v.shape[1], side_v.shape[2] // 4
+    share = items * rows
+    for j, out in enumerate((conv2, conv1)):
+        got[j].wait()
+        for a in range(3):
+            for b in range(3):
+                for q in range(items):
+                    conv_v[j, a * 3 + b, q * rows : (q + 1) * rows] = final_v[j, a, q, b].astype(F32)
+        fetch(conv_v.at[j], out)
+    for c, (_, held, dst) in zip(got_through, through):
+        c.wait()
+        fetch(held, dst)
+    got_vectors.wait()
+    total = vector_v[0]
+    for g in range(1, items):
+        total = total + vector_v[g]
+    own = me * share
+    block = channels // 4
+    part = total[:, :block]
+    for j in range(1, 4):
+        part = jnp.where(own // block == j, total[:, j * block : (j + 1) * block], part)
+    mine = part[:, :share]
+    for j in range(1, block // share):
+        mine = jnp.where(lax.rem(own, block) == j * share, part[:, j * share : (j + 1) * share], mine)
+    for j, out in enumerate((gain1, gain2, gain3)):
+        out[...] = mine[j : j + 1]
+    wide = embed_w_v.shape[0]
+    start = me * wide
+    line = lax.broadcasted_iota(jnp.int32, (16, 1), 0)
+    lhs = jnp.zeros((16, wide), F32)
+    rhs = jnp.zeros((16, 2 * channels), F32)
+    for g in range(items):
+        row = vector_v[g, pl.ds(5 + start // channels, 1)]
+        piece = row[:, :wide]
+        for j in range(1, channels // wide):
+            piece = jnp.where(lax.rem(start, channels) == j * wide, row[:, j * wide : (j + 1) * wide], piece)
+        lhs = jnp.where(line == g, piece, lhs)
+        both = jnp.concatenate([vector_v[g, 3:4], vector_v[g, 4:5]], axis=1)
+        rhs = jnp.where(line == g, both, rhs)
+    embed_w_v[...] = dot(lhs.astype(BF16), rhs.astype(BF16), 0, 0)
+    fetch(embed_w_v, embed_w)
+    got_side.wait()
+    for q in range(items):
+        for w in range(3):
+            at = w * share + q * rows
+            qkv_v[at : at + rows] = side_v[q, :, w * channels : (w + 1) * channels].astype(F32)
+        proj_v[q * rows : (q + 1) * rows] = side_v[q, :, 3 * channels :].astype(F32)
+    fetch(qkv_v, qkv)
+    fetch(proj_v, proj)
+    for j, c in enumerate(started):
+        if j > 8:
+            c.wait()
+
+
+def finalize_call(arrays, share):
+    final, side, vectors, output, image_grad, text_grad, text_w_grad, embed_grad = arrays
+    channels = output.shape[-1]
+    n = channels // share
+    sds = jax.ShapeDtypeStruct
+    kernels = (9, share, channels)
+    embed_w = (embed_grad.shape[1] // n, 2 * channels)
+    outs = [sds(a.shape, a.dtype) for a in arrays[3:]]
+    outs += [sds(kernels, F32)] * 2
+    outs += [sds((3 * share, channels), F32), sds((share, channels), F32), sds(embed_w, F32)]
+    outs += [sds((1, share), F32)] * 3
+    v = pltpu.VMEM
+    return pl.pallas_call(
+        finalize_kernel,
+        out_shape=tuple(outs),
+        in_specs=[ANYWHERE] * len(arrays),
+        out_specs=(ANYWHERE,) * 10 + (WHOLE,) * 3,
+        scratch_shapes=[
+            v(final.shape, BF16),
+            v(side.shape, BF16),
+            v(vectors.shape, F32),
+            v((2,) + kernels, F32),
+            v((3 * share, channels), F32),
+            v((share, channels), F32),
+            v(embed_w, F32),
+            *[v(a.shape, a.dtype) for a in arrays[3:]],
+            DMA((24,)),
+        ],
+        compiler_params=pltpu.CompilerParams(vmem_limit_bytes=62 << 20),
+        name="finalize",
+    )(*arrays)
 
 
 def backward_call(info, embed, gains, stats, shifts, arrays, identity):
@@ -1937,14 +2046,12 @@
     outs = (
         sds(image.shape, BF16),
         sds(image.shape, F32),
-        sds((9 * channels, share), F32),
-        sds((9 * channels, share), F32),
-        sds((channels, 3 * share), F32),
-        sds((channels, share), F32),
-        sds((items, 16, channels), F32),
         sds((tokens, text_w.shape[0]), F32),
         sds((text_w.shape[0] // n, 2 * channels), F32),
         sds(embed.shape, F32),
+        sds((2, 3, items, 3, rows, channels), BF16),
+        sds((items, rows, 4 * channels), BF16),
+        sds((items, 16, channels), F32),
     )
     v = pltpu.VMEM
     scratch = [
@@ -1972,6 +2079,10 @@
         v((pixels, channels), BF16),
         v(image.shape, BF16),
         v(image.shape, F32),
+        v((tokens, text_w.shape[0]), F32),
+        v((text_w.shape[0] // n, 2 * channels), F32),
+        v(embed.shape, F32),
+        v((channels, channels), BF16),
         v((2, items, channels // items, pixels), BF16),
         v((2, items, channels // items, pixels), BF16),
         v((2, 3, 2, 3, chips * rows, channels), BF16),
@@ -2020,7 +2131,7 @@
         functools.partial(backward_kernel, items, n),
         out_shape=outs,
         in_specs=[SCALARS] + [WHOLE] * 6 + [ANYWHERE] * len(arrays),
-        out_specs=(ANYWHERE,) * 2 + (WHOLE,) * 8,
+        out_specs=(ANYWHERE,) * 8,
         scratch_shapes=scratch,
         compiler_params=pltpu.CompilerParams(
             collective_id=identity, has_side_effects=True, vmem_limit_bytes=62 << 20
@@ -2033,7 +2144,7 @@
 
 
 def own_shards(
-    info, image, embed, text, gain1, conv1_w, embed_w, gain2, conv2_w, gain3, qkv_w, text_w, proj_w,
+    extent, image, embed, text, gain1, conv1_w, embed_w, gain2, conv2_w, gain3, qkv_w, text_w, proj_w,
     cotangent,
 ):
     _, rows_dev, width, channels = image.shape
@@ -2044,7 +2155,7 @@
     share = channels // parts
     (first, middle, cot, hidden_all, second_all, attn_flat, qkv_turned, attended, dq, dkv, own_dt, all_dt,
      text_cols, stats, shifts) = forward_call(
-        info,
+        extent,
         image[0],
         cotangent[0],
         text[0],
@@ -2061,9 +2172,8 @@
         0,
     )
     text_w_rows = text_cols.shape[3]
-    (output, image_grad, conv1_total, conv2_total, qkv_total, proj_total, vectors, text_grad, text_w_grad,
-     embed_grad) = backward_call(
-        info,
+    output, image_grad, text_grad, text_w_grad, embed_grad, final, side, vectors = backward_call(
+        extent,
         embed,
         (gain1, gain2, gain3),
         stats,
@@ -2091,28 +2201,28 @@
         ),
         1,
     )
-    embed_rows = embed.shape[1] // channels
-    all_shifts = vectors[:, 3:5].reshape(items, 2 * channels).astype(BF16)
-    all_embed = vectors[:, 5 : 5 + embed_rows].reshape(items, embed.shape[1]).astype(BF16)
-    embed_share = embed_w.shape[0] // parts
-    own_embed = lax.dynamic_slice_in_dim(all_embed, me * embed_share, embed_share, 1)
-    embed_w_grad = jnp.einsum("ic,ik->ck", own_embed, all_shifts, preferred_element_type=F32)
-    gains = jnp.sum(vectors[:, :3], axis=0)
-    gains = lax.dynamic_slice_in_dim(gains, me * share, share, 1)
+    (output, image_grad, text_grad, text_w_grad, embed_grad, conv2, conv1, qkv, proj, embed_w_grad, norm1, norm2,
+     norm3) = finalize_call(
+        (final, side, vectors, output, image_grad, text_grad, text_w_grad, embed_grad), share
+    )
+
+    def kernel(values):
+        return jnp.swapaxes(values.reshape(3, 3, share, channels), 2, 3)
+
     return (
         output[None],
         image_grad[None],
         embed_grad,
         text_grad[None],
-        gains[0],
-        conv1_total.reshape(3, 3, channels, share),
+        norm1[0],
+        kernel(conv1),
         embed_w_grad,
-        gains[1],
-        conv2_total.reshape(3, 3, channels, share),
-        gains[2],
-        qkv_total,
+        norm2[0],
+        kernel(conv2),
+        norm3[0],
+        qkv.T,
         text_w_grad,
-        proj_total,
+        proj.T,
     )
 
 
@@ -2154,7 +2264,7 @@
     )
     if own_path:
         return own_shards(
-            info, image, embed, text, gain1, conv1_w, embed_w, gain2, conv2_w, gain3, qkv_w, text_w,
+            extent, image, embed, text, gain1, conv1_w, embed_w, gain2, conv2_w, gain3, qkv_w, text_w,
             proj_w, cotangent,
         )
 

time: 258 us -> 242 us (0.938)
  local copies, waits for them, and re-layouts: 14 us -> 0 us
  other arithmetic: 3.01 us -> 0 us
    unnamed x23 -> x0, local copies, waits for them, and re-layouts: 13.4 us -> none
    pallas_call x0 -> x1, Pallas kernels: none -> 4.69 us  [finalize_call(): pl.pallas_call(finalize_kernel, out_shape=tuple(outs), in_specs=[ANYWHERE...]
where the time goes in v3:
time: 242 us; the launch traced here: 241 us
  Pallas kernels  240 us (99%)
    pallas_call x1, Pallas kernels, forward_call(): pl.pallas_call(functools.partial(forward_kernel, items, n, step, bq), out...  157 us
    pallas_call x1, Pallas kernels, backward_call(): pl.pallas_call(functools.partial(backward_kernel, items, n), out_shape=ou...  78.4 us

profile of v3, /device:TPU:0, one launch (start us, length us, event | category | flops | bytes accessed | tf_op | source)
XLA Modules:
  0.0 240.9 jit_solution(13079804428749726918)
XLA Ops:
  0.6 157.0 %forward.1 = (f32[10,64,512]{2,1,0:T(8,128)}, f32[10,64,512]{2,1,0:T(8,128)}, bf16[10,64,512]{2,1,0:T(8,128)(2,1)}, bf16[4,10,64,512]{3,2,1,0:T(8,128)(2,1)}, bf...) custom-call(s32[1,2]{1,0:T(1,128)} %refs_0_.3, ...), custom_call_target="tpu_custom_call" | custom-call | flops 5368709120 | bytes 62914560 | tf_op jit(solution)/shard_map/forward/pallas_call | solution.py:1390
  157.6 78.4 %backward.1 = (bf16[8,64,512]{2,1,0:T(8,128)(2,1)}, f32[8,64,512]{2,1,0:T(8,128)}, f32[16,2048]{1,0:T(8,128)}, f32[256,1024]{1,0:T(8,128)}, f32[1,2048]{1,0:T(1,...) custom-call(s32[1,2]{1,0:T(1,128)} %refs_0_.3, ...), custom_call_target="tpu_custom_call" | custom-call | flops 10737418240 | bytes 62914560 | tf_op jit(solution)/shard_map/backward/pallas_call | solution.py:2130
  236.0 4.7 %finalize.1 = (bf16[8,64,512]{2,1,0:T(8,128)(2,1)}, f32[8,64,512]{2,1,0:T(8,128)}, f32[16,2048]{1,0:T(8,128)}, f32[256,1024]{1,0:T(8,128)}, f32[1,2048]{1,0:T(1,...) custom-call(bf16[2,3,4,3,16,512]{5,4,3,2,1,0:T(8,128)(2,1)} %get-tup, ...), custom_call_target="tpu_custom_call" | custom-call | tf_op jit(solution)/shard_map/finalize/pallas_call | solution.py:2012

commit v4 on v3

--- a/solution.py
+++ b/solution.py
@@ -118,7 +118,7 @@
         rest = jnp.zeros((128 - d - 16, bq), F32)
         return o.astype(BF16), jnp.concatenate([go * inv, extra, rest], axis=0).astype(BF16)
 
-    def attend(self, q_ref, go_ref, o_ref, dq_ref, order, scored=nothing, before=nothing, done=nothing):
+    def attend(self, q_ref, go_ref, o_ref, dq_ref, order, before=nothing, done=nothing):
         d, bq, chunks = self.d, self.bq, self.chunks
         self.dkt[...] = jnp.zeros_like(self.dkt)
         self.dvt[...] = jnp.zeros_like(self.dvt)
@@ -143,7 +143,6 @@
 
         run = self.run
         pk, _, _, _ = run((0, self.query(q_of(0, 0))), None, None)
-        scored()
         pk, total, acc, _ = run((1, self.query(q_of(0, 1))), (0, top(pk)), None)
         goa = finish_exp(0, 0, total, acc)
 
@@ -902,14 +901,29 @@
             self.own, self.slots.at[self.grid.me], self.send.at[k], self.recv.at[k], self.grid.row(k)
         )
 
-    def start(self):
+    def start(self, stats):
+        lines, lanes = self.own.shape
+        half = lines // 2
+        at = lax.broadcasted_iota(jnp.int32, (lines, lanes), 0)
+        packed = jnp.zeros((lines, lanes), F32)
+        for j in range(lines):
+            piece = stats[j // half : j // half + 1, (j % half) * lanes : (j % half + 1) * lanes]
+            packed = jnp.where(at == j, piece, packed)
+        self.own[...] = packed
         self.grid.loop(self.grid.n, lambda k: self.copy(k).start())
-        self.slots[self.grid.me] = self.own[...]
+        self.slots[self.grid.me] = packed
 
     def result(self):
         self.grid.loop(self.grid.n, lambda k: self.copy(k).wait())
         slots = self.slots
-        return lax.fori_loop(1, self.grid.n, lambda k, s: s + slots[k], slots[0])
+        total = lax.fori_loop(1, self.grid.n, lambda k, s: s + slots[k], slots[0])
+        half = total.shape[0] // 2
+        rows = [
+            jnp.concatenate([total[r * half + j : r * half + j + 1] for j in range(half)], axis=1)
+            for r in range(2)
+        ]
+        at = lax.broadcasted_iota(jnp.int32, (8, rows[0].shape[1]), 0)
+        return jnp.where(at == 0, rows[0], jnp.where(at == 1, rows[1], 0.0))
 
 
 class Edges:
@@ -1000,19 +1014,21 @@
 
 def forward_kernel(items, n, step, bq, *refs):
     (info, image, cot, text, embed, gain1, gain2, gain3, w1_in, w2_in, embed_in, text_in, qkv_in, proj_in,
-     first_out, mid_out, cot_out, hidden_all, second_all, attn_out, turned_out, o_out, dq_out, dkv_out, dt_out,
-     dt_all, text_cols, stats_out, shifts_out,
-     image_v, cot_v, text_v, w1, w2, embed_w, text_w, qkv_w, proj_w, first_v, mid_v, hidden, second, attn,
-     turned, keys, values, queries, go, text_kv, cols, shifted, acc, own, slots,
-     key_land, value_land, query_land, go_land, text_pair, o, dq, dkv, dtext, same,
+     first_out, mid_out, cot_out, hidden_all, second_all, attn_out, turned_out, output, query_part, side_out, dkv_out,
+     dt_out, dt_all, text_cols, stats_out, shifts_out,
+     image_v, cot_v, text_v, w1, w2, wide_w, qkv_w, proj_w, first_v, mid_v, hidden, second, attn,
+     turned, pairs, queries, go, text_kv, cols, shifted, acc, own, slots,
+     pair_land, query_land, go_land, text_pair, o, dq, dkv, dtext, same, o_land, dq_land, masked, out_v, query_acc,
+     side_v, side_core, side_sum, side_item, side_total, cols_land,
      load, sum_send, sum_recv, edge_send, edge_recv, row_send, row_recv, item_send, item_recv,
-     *scratch) = refs
+     s_core_send, s_core_recv, s_item_send, s_item_recv, *scratch) = refs
     grid = Grid(items, n)
     item, me = grid.item, grid.me
     rows_dev, width, channels = image.shape
     pixels = rows_dev * width
     heads, head_dim, wide = HEADS, channels // HEADS, 3 * channels // HEADS
     base = me * rows_dev
+    share_rows = channels // n
     count = (info[0, 0] * info[0, 1]).astype(F32) * (channels // GROUPS)
     att = Attention(n, pixels, head_dim, n * text.shape[0], step, bq, scratch)
 
@@ -1032,9 +1048,8 @@
     got_cot = fetch(cot, cot_v.at[center])
     got_proj = fetch(proj_in, proj_w)
     got_text = fetch(text, text_v)
-    got_text_w = fetch(text_in, text_w)
+    got_text_w = fetch(text_in, wide_w)
     got_w1 = fetch(w1_in, w1)
-    got_embed_w = fetch(embed_in, embed_w)
     got_w2 = fetch(w2_in, w2)
     got_qkv_w = fetch(qkv_in, qkv_w)
     edges = [
@@ -1055,16 +1070,17 @@
         v = start_row(r)
         return v, v * v
 
-    own[0] = row_stats(rows_dev, width, channels, start_stats)
+    stats = row_stats(rows_dev, width, channels, start_stats)
     grid.met()
-    sums[0].start()
+    sums[0].start(stats)
     edges[0].start()
     got_cot.wait()
     edges[1].start()
 
     got_text.wait()
     got_text_w.wait()
-    text_all = dot(text_v[...], text_w[...], 1, 0).astype(BF16)
+    text_all = dot(text_v[...], wide_w[...], 1, 0).astype(BF16)
+    got_embed_w = fetch(embed_in, wide_w)
     share = text_v.shape[1] // n
     for h in range(heads):
         text_kv[h] = text_all[:, h * 2 * head_dim : (h + 1) * 2 * head_dim]
@@ -1079,20 +1095,20 @@
         return copy
 
     kv_copy = scatter(0, text_kv, text_pair)
-    col_copy = scatter(1, cols, text_cols.at[item])
+    col_copy = scatter(1, cols, cols_land)
     grid.loop(n, lambda k: kv_copy(k).start())
     grid.loop(n, lambda k: col_copy(k).start())
     own_kv = fetch(text_kv.at[me], text_pair.at[me])
-    own_col = fetch(cols.at[me], text_cols.at[item, me])
+    cols_land[me] = cols[me]
 
     got_proj.wait()
 
     def to_grad(r):
-        attn[pl.ds(r * width, width)] = (cot_v[1 + r].astype(F32) * inside(base + r)).astype(BF16)
+        masked[pl.ds(r * width, width)] = (cot_v[1 + r].astype(F32) * inside(base + r)).astype(BF16)
 
     each_row(rows_dev, to_grad)
     for h in range(heads):
-        go[h] = dot(proj_w[h * head_dim : (h + 1) * head_dim], attn[...], 1, 1).astype(BF16)
+        go[h] = dot(proj_w[h * head_dim : (h + 1) * head_dim], masked[...], 1, 1).astype(BF16)
     go_copy = scatter(2, go, go_land)
     own_go = fetch(go.at[me], go_land.at[me])
 
@@ -1127,14 +1143,14 @@
         first_v[1 + r] = value
         return value, value * value
 
-    own[1] = row_stats(rows_dev, width, channels, first_row)
-    sums[1].start()
+    stats = row_stats(rows_dev, width, channels, first_row)
+    sums[1].start(stats)
     edges[2].start()
 
     e = embed[...].astype(F32)
     low = (e * sigmoid(e)).astype(BF16)
     got_embed_w.wait()
-    shifts_out[...] = dot(low, embed_w[...], 1, 0)
+    shifts_out[...] = dot(low, wide_w[...], 1, 0)
     scale, shift = shifts_out[:, :channels], shifts_out[:, channels:]
 
     stats = sums[1].result()
@@ -1162,8 +1178,8 @@
         mid_v[1 + r] = value
         return value, value * value
 
-    own[2] = row_stats(rows_dev, width, channels, middle_row)
-    sums[2].start()
+    stats = row_stats(rows_dev, width, channels, middle_row)
+    sums[2].start(stats)
     edges[3].start()
     edges[1].wait()
     own_cot = fetch(cot_v, cot_out)
@@ -1183,27 +1199,25 @@
 
     each_row(rows_dev, to_attn)
     own_attn = fetch(attn, attn_out)
-    key_copy = scatter(3, keys, key_land)
-    value_copy = scatter(4, values, value_land)
-    query_copy = scatter(5, queries, query_land)
+    pair_copy = scatter(3, pairs, pair_land)
+    query_copy = scatter(4, queries, query_land)
 
     def head(k):
         to = lax.rem(me + k, n)
         rows = pl.ds(pl.multiple_of(to * wide, wide), wide)
         block = dot(turned[rows], attn[...], 1, 1).astype(BF16)
         queries[to] = block[:head_dim]
-        keys[to] = block[head_dim : 2 * head_dim]
-        values[to] = block[2 * head_dim :]
+        pairs[to] = block[head_dim:]
 
     def send_head(k):
         head(k)
-        key_copy(k).start()
+        pair_copy(k).start()
 
     grid.loop(n, send_head)
     head(0)
     query_land[me] = queries[me]
-    att.stage_key(me, keys[me], width, info[0, 0], info[0, 1])
-    att.stage_value(me, values[me])
+    att.stage_key(me, pairs[me, :head_dim], width, info[0, 0], info[0, 1])
+    att.stage_value(me, pairs[me, head_dim:])
     grid.loop(n, lambda k: kv_copy(k).wait())
     own_kv.wait()
     att.stage_text(text_pair[...].reshape(n * text.shape[0], 2 * head_dim))
@@ -1213,26 +1227,20 @@
     def source(k):
         return lax.rem(me + n - k, n)
 
-    def stage_key(k):
-        key_copy(k).wait()
-        att.stage_key(source(k), key_land[source(k)], width, info[0, 0], info[0, 1])
-
-    grid.loop(n, stage_key)
-    grid.loop(n, lambda k: value_copy(k).start())
-
-    def scored():
-        def stage_value(k):
-            value_copy(k).wait()
-            att.stage_value(source(k), value_land[source(k)])
-
-        grid.loop(n, stage_value)
-
-        def rest(k):
-            query_copy(k).start()
-            go_copy(k).start()
-
-        grid.loop(n, rest)
-        own_go.wait()
+    def stage_pair(k):
+        pair_copy(k).wait()
+        c = source(k)
+        att.stage_key(c, pair_land[c, :head_dim], width, info[0, 0], info[0, 1])
+        att.stage_value(c, pair_land[c, head_dim:])
+
+    grid.loop(n, stage_pair)
+
+    def send_rest(k):
+        query_copy(k).start()
+        go_copy(k).start()
+
+    grid.loop(n, send_rest)
+    own_go.wait()
 
     def before(k):
         query_copy(k).wait()
@@ -1251,10 +1259,10 @@
 
         return copy
 
-    o_copy = give(6, o, o_out)
-    dq_copy = give(7, dq, dq_out)
-    dkv_copy = give(8, dkv, dkv_out)
-    dt_copy = give(9, dtext, dt_out)
+    o_copy = give(5, o, o_land)
+    dq_copy = give(6, dq, dq_land)
+    dkv_copy = give(7, dkv, dkv_out)
+    dt_copy = give(8, dtext, dt_out)
 
     def done(h):
         @pl.when(h > 0)
@@ -1262,7 +1270,11 @@
             o_copy(h).start()
             dq_copy(h).start()
 
-    att.attend(query_land, go_land, o, dq, source, scored, before, done)
+    grid.loop(n, lambda k: col_copy(k).wait())
+    cols_copy = spread(2, cols_land, text_cols)
+    grid.loop(items, lambda k: cols_copy(k).start())
+    own_cols = fetch(cols_land, text_cols.at[item])
+    att.attend(query_land, go_land, o, dq, source, before, done)
 
     def send_keys(h):
         at = pl.ds(pl.multiple_of(source(h) * pixels, pixels), pixels)
@@ -1289,26 +1301,57 @@
 
     def gather_copy(k):
         return remote(
-            dtext, dt_all.at[item, me], row_send.at[10, k], row_recv.at[10, k], grid.row(k)
+            dtext, dt_all.at[item, me], row_send.at[9, k], row_recv.at[9, k], grid.row(k)
         )
 
     grid.loop(n, lambda k: gather_copy(k).start())
-    own_o = fetch(o.at[me], o_out.at[me])
-    own_dq = fetch(dq.at[me], dq_out.at[me])
     own_dkv = fetch(dkv.at[me], dkv_out.at[me])
     own_dt = fetch(dtext.at[me], dt_out.at[me])
     own_all = fetch(dtext, dt_all.at[item, me])
-    grid.loop(n, lambda k: col_copy(k).wait())
-    own_col.wait()
-    cols_copy = spread(2, text_cols.at[item], text_cols)
-    grid.loop(items, lambda k: cols_copy(k).start())
+
+    o_land[me] = o[me]
+    dq_land[me] = dq[me]
+    grid.loop(n, lambda h: o_copy(h).wait())
+    grid.loop(n, lambda h: dq_copy(h).wait())
+    side = SideSum(grid, side_v, side_core, side_sum, side_item, side_total, None, None,
+                   (s_core_send, s_core_recv), (s_item_send, s_item_recv), None, None)
+
+    def query_head(h):
+        block = dot(dq_land[h], attn[...], 1, 0).astype(BF16)
+        side.put_head(h, block, 0)
+
+    each_row(heads, query_head)
+    flat_o = o_land[...].reshape(channels, pixels)
+    block = dot(masked[...].astype(F32).T.astype(BF16), flat_o, 1, 1).astype(BF16)
+    for r in range(n):
+        side.put_head(r, block[r * share_rows : (r + 1) * share_rows], 1)
+    side.core_copy().start()
+    query_acc[...] = jnp.zeros_like(query_acc)
+
+    def unproject_query(h):
+        rows = pl.ds(pl.multiple_of(h * wide, wide), head_dim)
+        query_acc[...] += dot(dq_land[h].astype(F32).T.astype(BF16), turned[rows], 1, 0)
+
+    each_row(heads, unproject_query)
+    put_query = fetch(query_acc, query_part)
+    side.over_items()
+    acc[...] = dot(flat_o.astype(F32).T.astype(BF16), proj_w[...], 1, 0)
+
+    def output_row(r):
+        value = mid_v[1 + r] + acc[pl.ds(r * width, width)] * inside(base + r)
+        out_v[r] = value.astype(BF16)
+
+    each_row(rows_dev, output_row)
+    put_output = fetch(out_v, output)
+    side.sum_items()
+    put_side = fetch(side_total, side_out)
     grid.loop(items, lambda k: hidden_copy(k).wait())
     grid.loop(items, lambda k: second_copy(k).wait())
     grid.loop(items, lambda k: cols_copy(k).wait())
-    for copy in (o_copy, dq_copy, dkv_copy, dt_copy, gather_copy):
+    for copy in (dkv_copy, dt_copy, gather_copy):
         grid.loop(n, lambda h: copy(h).wait())
-    for c in (own_hidden, own_first, own_second, own_cot, own_turned, own_attn, own_mid, own_o, own_dq, own_dkv,
-              own_dt, own_all):
+    for c in (own_hidden, own_first, own_second, own_cot, own_turned, own_attn, own_mid, own_dkv, own_dt, own_all,
+              own_cols, put_query, put_output, put_side):
         c.wait()
 
 
@@ -1319,7 +1362,9 @@
     padded = (rows_dev + 2, width, channels)
     tokens, text_width = text.shape
     head_dim = channels // HEADS
-    w1, w2, embed_w, text_w, qkv_w, proj_w = weights
+    w1, w2, _, text_w, qkv_w, proj_w = weights
+    chips = n // 2
+    rows = channels // n // items
     sds = jax.ShapeDtypeStruct
     outs = (
         sds(padded, F32),
@@ -1329,8 +1374,9 @@
         sds((items,) + padded, BF16),
         sds((pixels, channels), BF16),
         sds((3 * channels, channels), BF16),
-        sds((n, head_dim, pixels), BF16),
-        sds((n, head_dim, pixels), BF16),
+        sds(image.shape, BF16),
+        sds((pixels, channels), F32),
+        sds((chips, rows, 2 * channels), BF16),
         sds((n, 2 * head_dim, pixels), BF16),
         sds((n, tokens, 2 * head_dim), BF16),
         sds((items, n, n, tokens, 2 * head_dim), BF16),
@@ -1345,7 +1391,6 @@
         v(text.shape, BF16),
         v(w1.shape, BF16),
         v(w2.shape, BF16),
-        v(embed_w.shape, BF16),
         v(text_w.shape, BF16),
         v(qkv_w.shape, BF16),
         v(proj_w.shape, BF16),
@@ -1355,18 +1400,16 @@
         v(padded, BF16),
         v((pixels, channels), BF16),
         v((3 * channels, channels), BF16),
-        v((n, head_dim, pixels), BF16),
-        v((n, head_dim, pixels), BF16),
+        v((n, 2 * head_dim, pixels), BF16),
         v((n, head_dim, pixels), BF16),
         v((n, head_dim, pixels), BF16),
         v((n, tokens, 2 * head_dim), BF16),
         v((n, tokens, text_width // n), BF16),
         v((rows_dev + 2, width, 3 * channels), BF16),
         v((pixels, channels), F32),
-        v((3, 8, channels), F32),
-        v((3, n, 8, channels), F32),
-        v((n, head_dim, pixels), BF16),
-        v((n, head_dim, pixels), BF16),
+        v((3, channels // 64, 128), F32),
+        v((3, n, channels // 64, 128), F32),
+        v((n, 2 * head_dim, pixels), BF16),
         v((n, head_dim, pixels), BF16),
         v((n, head_dim, pixels), BF16),
         v((n, tokens, 2 * head_dim), BF16),
@@ -1375,15 +1418,30 @@
         v((n, 2 * head_dim, pixels), BF16),
         v((n, tokens, 2 * head_dim), BF16),
         v((channels, channels), BF16),
+        v((n, head_dim, pixels), BF16),
+        v((n, head_dim, pixels), BF16),
+        v((pixels, channels), BF16),
+        v(image.shape, BF16),
+        v((pixels, channels), F32),
+        v((2, chips, items, rows, 2 * channels), BF16),
+        v((chips, items, rows, 2 * channels), BF16),
+        v((items, chips, rows, 2 * channels), BF16),
+        v((items, chips, rows, 2 * channels), BF16),
+        v((chips, rows, 2 * channels), BF16),
+        v((n, tokens, text_width // n), BF16),
         DMA((28,)),
         DMA((3, n)),
         DMA((3, n)),
         DMA((4, 2)),
         DMA((4, 2)),
-        DMA((11, n)),
-        DMA((11, n)),
+        DMA((10, n)),
+        DMA((10, n)),
         DMA((3, items)),
         DMA((3, items)),
+        DMA((1,)),
+        DMA((1,)),
+        DMA((items,)),
+        DMA((items,)),
     ]
     step, bq, extra = attention_scratch(n, pixels, head_dim, n * tokens)
     scratch += extra
@@ -1391,7 +1449,7 @@
         functools.partial(forward_kernel, items, n, step, bq),
         out_shape=outs,
         in_specs=[SCALARS] + [ANYWHERE] * 3 + [WHOLE] * 4 + [ANYWHERE] * 6,
-        out_specs=(ANYWHERE,) * 13 + (WHOLE,) * 2,
+        out_specs=(ANYWHERE,) * 14 + (WHOLE,) * 2,
         scratch_shapes=scratch,
         compiler_params=pltpu.CompilerParams(
             collective_id=identity, has_side_effects=True, vmem_limit_bytes=62 << 20
@@ -1564,13 +1622,23 @@
             {"items": grid.item, "rows": to * 2 + self.core},
         )
 
-    def over_chips(self):
+    def put_head(self, h, block, j):
+        items, rows = self.values.shape[2], self.values.shape[3]
+        channels = block.shape[1]
+        at = slice(j * channels, (j + 1) * channels)
+        core, chip = (h % 2, h // 2) if isinstance(h, int) else (lax.rem(h, 2), h // 2)
+        self.values[core, chip, :, :, at] = block.reshape(items, rows, channels)
+
+    def sum_items(self):
         for k in range(1, self.grid.items):
             self.item_copy(k).wait()
         total = self.core_sum[self.grid.item].astype(F32)
         for k in range(1, self.grid.items):
             total = total + self.from_item[k].astype(F32)
-        self.item_sum[...] = total.astype(BF16)
+        self.item_sum[:, :, : total.shape[2]] = total.astype(BF16)
+
+    def over_chips(self):
+        self.sum_items()
         for k in range(1, self.chips):
             self.chip_copy(k).start()
 
@@ -1615,15 +1683,15 @@
 
 def backward_kernel(items, n, *refs):
     (info, embed, gain1, gain2, gain3, stats_in, shifts,
-     o_in, dq_in, dkv_in, dt_in, dt_all, first, middle, cot, image, hidden_all, second_all, attn_in, turned_in, text_cols,
-     proj_in, w1_in, w2_in, text_in, embed_in,
-     output, image_grad, text_grad, text_w_grad, embed_grad, final_out, side_out, vectors,
-     weight, proj_w, qkv_turned, first_v, mid_v, cot_v, image_v, attn, cols, rows_v, dq, o, dt, own_dt,
-     grad_v, grad_mid, moved_v, pre, acc, shifted, shifted_all, masked, out_v, image_out, text_v, text_w_v, embed_v, same,
+     query_part, side_in, dkv_in, dt_in, dt_all, first, middle, cot, image, hidden_all, second_all, attn_in,
+     turned_in, text_cols, w1_in, w2_in, text_in, embed_in,
+     image_grad, text_grad, text_w_grad, embed_grad, final_out, side_out, vectors,
+     weight, qkv_turned, first_v, mid_v, cot_v, image_v, attn, cols, rows_v, dkv, dt, own_dt,
+     grad_v, grad_mid, moved_v, pre, acc, shifted, shifted_all, image_out, text_v, text_w_v, embed_v, same,
      turned, quarter, part, from_core, chip_sum, from_chip, final,
      side_v, side_core, side_sum, side_item, side_total, side_chip, side_final,
      vector, vector_land, own, slots,
-     load, sum_send, sum_recv, edge_send, edge_recv, dt_send, dt_recv, vec_send, vec_recv,
+     load, sum_send, sum_recv, edge_send, edge_recv, dt_send, dt_recv, dt_core_send, dt_core_recv, vec_send, vec_recv,
      k_item_send, k_item_recv, k_core_send, k_core_recv, k_chip_send, k_chip_recv, k_final_send, k_final_recv,
      s_core_send, s_core_recv, s_item_send, s_item_recv, s_chip_send, s_chip_recv, s_final_send,
      s_final_recv) = refs
@@ -1648,16 +1716,15 @@
         fetched.append(c)
         return c
 
-    got_dq = fetch(dq_in, dq.at[:, :head_dim])
-    got_dkv = fetch(dkv_in, dq.at[:, head_dim:])
+    got_query = fetch(query_part, acc)
+    got_dkv = fetch(dkv_in, dkv)
     got_turned = fetch(turned_in, qkv_turned)
     got_mid = fetch(middle, mid_v)
     got_cot = fetch(cot, cot_v)
     got_w2 = fetch(w2_in, weight)
     got_first = fetch(first, first_v)
     got_attn = fetch(attn_in, attn)
-    got_o = fetch(o_in, o)
-    got_proj = fetch(proj_in, proj_w)
+    got_side = fetch(side_in, side_total.at[:, :, 2 * channels :])
     got_dt = fetch(dt_in, own_dt)
     got_all = fetch(dt_all.at[item], dt.at[item])
     got_second = fetch(second_all, rows_v)
@@ -1683,24 +1750,28 @@
                    (s_core_send, s_core_recv), (s_item_send, s_item_recv), (s_chip_send, s_chip_recv),
                    (s_final_send, s_final_recv))
 
+    core = lax.rem(me, 2)
+    half = heads // 2
+    core_heads = pl.ds(core * half, half)
+
     def dt_copy(k):
-        mine = dt.at[item]
+        mine = dt.at[item, core_heads]
         return remote(mine, mine, dt_send.at[k], dt_recv.at[k], grid.peer(k))
 
+    def dt_core_copy(k):
+        mine = dt.at[lax.rem(item + k, items), core_heads]
+        sibling = {"items": item, "rows": me + 1 - 2 * core}
+        return remote(mine, mine, dt_core_send.at[k], dt_core_recv.at[k], sibling)
+
     got_turned.wait()
-    got_dq.wait()
     got_dkv.wait()
+    got_query.wait()
 
     def unproject_head(h):
-        rows = pl.ds(pl.multiple_of(h * wide, wide), wide)
-        return dot(dq[h].astype(F32).T.astype(BF16), qkv_turned[rows], 1, 0)
-
-    acc[...] = unproject_head(0)
-
-    def next_head(h):
-        acc[...] += unproject_head(h)
-
-    grid.loop(n, next_head)
+        rows = pl.ds(pl.multiple_of(h * wide + head_dim, head_dim), 2 * head_dim)
+        acc[...] += dot(dkv[h].astype(F32).T.astype(BF16), qkv_turned[rows], 1, 0)
+
+    each_row(heads, unproject_head)
     got_mid.wait()
     average, inverse = norm_of(stats_in[2], count, same[...])
 
@@ -1709,38 +1780,21 @@
         grad_v[1 + r] = value
         return value, value * ((mid_v[1 + r] - average) * inverse)
 
-    own[0] = row_stats(rows_dev, width, channels, grad_row)
+    stats = row_stats(rows_dev, width, channels, grad_row)
     grid.met()
-    sums[0].start()
+    sums[0].start(stats)
     edges[0].start()
-    got_all.wait()
-    grid.loop(items, lambda k: dt_copy(k).start())
 
     got_attn.wait()
 
     def qkv_head(h):
-        block = dot(dq[h], attn[...], 1, 0).astype(BF16)
-        for w in range(3):
-            rows = block[w * head_dim : (w + 1) * head_dim]
-            side_v[lax.rem(h, 2), h // 2, :, :, w * channels : (w + 1) * channels] = rows.reshape(
-                items, share // items, channels
-            )
+        block = dot(dkv[h], attn[...], 1, 0).astype(BF16)
+        for w in range(2):
+            side.put_head(h, block[w * head_dim : (w + 1) * head_dim], w)
 
     each_row(heads, qkv_head)
+    side.core_copy().start()
     got_cot.wait()
-
-    def mask_row(r):
-        masked[pl.ds(r * width, width)] = (cot_v[1 + r].astype(F32) * inside(base + r)).astype(BF16)
-
-    each_row(rows_dev, mask_row)
-
-    got_o.wait()
-    flat_o = o[...].reshape(channels, pixels)
-    block = dot(masked[...].astype(F32).T.astype(BF16), flat_o, 1, 1).astype(BF16)
-    for r in range(n):
-        rows = block[r * share : (r + 1) * share]
-        side_v[r % 2, r // 2, :, :, 3 * channels :] = rows.reshape(items, share // items, channels)
-    side.core_copy().start()
 
     stats4 = sums[0].result()
     mean, cross = means_of(stats4, gain3[...], count, same[...])
@@ -1756,7 +1810,6 @@
 
     each_row(rows_dev + 2, to_grad2)
     sum2.send_grads(shifted)
-    side.over_items()
     got_w2.wait()
     conv_taps_back(shifted, weight, acc, rows_dev)
     got_first.wait()
@@ -1769,8 +1822,8 @@
         moved_v[1 + r] = value
         return value, value * normal
 
-    own[1] = row_stats(rows_dev, width, channels, moved_row)
-    sums[1].start()
+    stats = row_stats(rows_dev, width, channels, moved_row)
+    sums[1].start(stats)
     edges[1].start()
     got_w1 = fetch(w1_in, weight)
     got_second.wait()
@@ -1782,8 +1835,13 @@
     shift_rows()
     got_hidden = fetch(hidden_all, rows_v)
     sum2.wait_grads()
-    for a in range(3):
-        sum2.compute(a, shifted_all)
+    side.over_items()
+    sum2.compute(0, shifted_all)
+    sum2.compute(1, shifted_all)
+    sum2.over_chips(0)
+    sum2.compute(2, shifted_all)
+    sum2.over_chips(1)
+    sum2.over_chips(2)
 
     stats5 = sums[1].result()
     factor = gain2[...] * (1.0 + scale)
@@ -1797,9 +1855,6 @@
 
     each_row(rows_dev + 2, to_grad1)
     sum1.send_grads(shifted)
-    side.over_chips()
-    for a in range(3):
-        sum2.over_chips(a)
     got_w1.wait()
     conv_taps_back(shifted, weight, acc, rows_dev)
     got_image.wait()
@@ -1812,16 +1867,20 @@
         pre[r] = value
         return value, value * normal
 
-    own[2] = row_stats(rows_dev, width, channels, pre_row)
-    sums[2].start()
+    stats = row_stats(rows_dev, width, channels, pre_row)
+    sums[2].start(stats)
     tall = text_in.shape[0]
     got_text_w = [
         fetch(text_in.at[:, j * channels : (j + 1) * channels], weight.at[j * tall : (j + 1) * tall])
         for j in range(2)
     ]
+    got_side.wait()
+    side.over_chips()
     got_hidden.wait()
     shift_rows()
     sum1.wait_grads()
+    got_all.wait()
+    grid.loop(items, lambda k: dt_copy(k).start())
     sum1.compute(0, shifted_all)
     sum1.compute(1, shifted_all)
     sum1.over_chips(0)
@@ -1831,6 +1890,8 @@
     for a in range(3):
         sum2.over_items(a)
     side.spread()
+    grid.loop(items, lambda k: dt_copy(k).wait())
+    grid.loop(items, lambda k: dt_core_copy(k).start())
 
     stats6 = sums[2].result()
     e = embed[...].astype(F32)
@@ -1862,20 +1923,9 @@
     each_row(rows_dev, finish_row)
     put_image = fetch(image_out, image_grad)
 
-    got_proj.wait()
-    acc[...] = dot(flat_o.astype(F32).T.astype(BF16), proj_w[...], 1, 0)
-
-    def output_row(r):
-        value = mid_v[1 + r] + acc[pl.ds(r * width, width)] * inside(base + r)
-        out_v[r] = value.astype(BF16)
-
-    each_row(rows_dev, output_row)
-    put_output = fetch(out_v, output)
-
     got_dt.wait()
     for c in got_text_w:
         c.wait()
-    half = heads // 2
     total = None
     for j in range(2):
         lhs = jnp.concatenate([own_dt[j * half + h] for h in range(half)], axis=1)
@@ -1893,7 +1943,7 @@
         sum2.wait_final(a)
     put_final2 = fetch(final.at[0], final_out.at[0])
 
-    grid.loop(items, lambda k: dt_copy(k).wait())
+    grid.loop(items, lambda k: dt_core_copy(k).wait())
     got_cols.wait()
     tokens = cols.shape[0] * cols.shape[1]
     flat_cols = cols[...].reshape(tokens, cols.shape[2]).astype(F32).T.astype(BF16)
@@ -1919,7 +1969,7 @@
     for a in range(3):
         sum1.wait_final(a)
     put_final1 = fetch(final.at[1], final_out.at[1])
-    for c in (put_image, put_output, put_text, put_final2, put_text_w, put_embed, put_vectors, put_side, put_final1):
+    for c in (put_image, put_text, put_final2, put_text_w, put_embed, put_vectors, put_side, put_final1):
         c.wait()
 
 
@@ -1987,7 +2037,7 @@
     got_side.wait()
     for q in range(items):
         for w in range(3):
-            at = w * share + q * rows
+            at = (w + 1) % 3 * share + q * rows
             qkv_v[at : at + rows] = side_v[q, :, w * channels : (w + 1) * channels].astype(F32)
         proj_v[q * rows : (q + 1) * rows] = side_v[q, :, 3 * channels :].astype(F32)
     fetch(qkv_v, qkv)
@@ -2032,8 +2082,8 @@
 
 def backward_call(info, embed, gains, stats, shifts, arrays, identity):
     items, n = lax.axis_size("items"), lax.axis_size("rows")
-    o_pair, _, _, dtext = arrays[:4]
-    image, text_cols, text_w = arrays[8], arrays[13], arrays[17]
+    dtext = arrays[3]
+    image, text_cols, text_w = arrays[8], arrays[13], arrays[16]
     rows_dev, width, channels = image.shape
     pixels = rows_dev * width
     head_dim = channels // HEADS
@@ -2044,7 +2094,6 @@
     tokens = dtext.shape[1]
     sds = jax.ShapeDtypeStruct
     outs = (
-        sds(image.shape, BF16),
         sds(image.shape, F32),
         sds((tokens, text_w.shape[0]), F32),
         sds((text_w.shape[0] // n, 2 * channels), F32),
@@ -2056,7 +2105,6 @@
     v = pltpu.VMEM
     scratch = [
         v((9 * channels, channels), BF16),
-        v((channels, channels), BF16),
         v((3 * channels, channels), BF16),
         v(padded, F32),
         v(padded, F32),
@@ -2065,8 +2113,7 @@
         v((pixels, channels), BF16),
         v(text_cols.shape, BF16),
         v((items,) + padded, BF16),
-        v((n, 3 * head_dim, pixels), BF16),
-        v(o_pair.shape, BF16),
+        v((n, 2 * head_dim, pixels), BF16),
         v((items, n) + dtext.shape, BF16),
         v(dtext.shape, BF16),
         v(padded, F32),
@@ -2076,8 +2123,6 @@
         v((pixels, channels), F32),
         v((rows_dev + 2, width, 3 * channels), BF16),
         v((items, rows_dev + 2, width, 3 * channels), BF16),
-        v((pixels, channels), BF16),
-        v(image.shape, BF16),
         v(image.shape, F32),
         v((tokens, text_w.shape[0]), F32),
         v((text_w.shape[0] // n, 2 * channels), F32),
@@ -2090,22 +2135,24 @@
         v((2, 3, chips, 3, rows, channels), BF16),
         v((2, 3, chips, 3, rows, channels), BF16),
         v((2, 3, items, 3, rows, channels), BF16),
-        v((2, chips, items, rows, 4 * channels), BF16),
-        v((chips, items, rows, 4 * channels), BF16),
-        v((items, chips, rows, 4 * channels), BF16),
-        v((items, chips, rows, 4 * channels), BF16),
+        v((2, chips, items, rows, 2 * channels), BF16),
+        v((chips, items, rows, 2 * channels), BF16),
+        v((items, chips, rows, 2 * channels), BF16),
+        v((items, chips, rows, 2 * channels), BF16),
         v((chips, rows, 4 * channels), BF16),
         v((chips, rows, 4 * channels), BF16),
         v((items, rows, 4 * channels), BF16),
         v((16, channels), F32),
         v((items, 16, channels), F32),
-        v((3, 8, channels), F32),
-        v((3, n, 8, channels), F32),
+        v((3, channels // 64, 128), F32),
+        v((3, n, channels // 64, 128), F32),
         DMA((32,)),
         DMA((3, n)),
         DMA((3, n)),
         DMA((2, 2)),
         DMA((2, 2)),
+        DMA((items,)),
+        DMA((items,)),
         DMA((items,)),
         DMA((items,)),
         DMA((items,)),
@@ -2131,7 +2178,7 @@
         functools.partial(backward_kernel, items, n),
         out_shape=outs,
         in_specs=[SCALARS] + [WHOLE] * 6 + [ANYWHERE] * len(arrays),
-        out_specs=(ANYWHERE,) * 8,
+        out_specs=(ANYWHERE,) * 7,
         scratch_shapes=scratch,
         compiler_params=pltpu.CompilerParams(
             collective_id=identity, has_side_effects=True, vmem_limit_bytes=62 << 20
@@ -2153,8 +2200,8 @@
     head_dim = channels // HEADS
     tokens = text.shape[1]
     share = channels // parts
-    (first, middle, cot, hidden_all, second_all, attn_flat, qkv_turned, attended, dq, dkv, own_dt, all_dt,
-     text_cols, stats, shifts) = forward_call(
+    (first, middle, cot, hidden_all, second_all, attn_flat, qkv_turned, output, query_part, side_part, dkv, own_dt,
+     all_dt, text_cols, stats, shifts) = forward_call(
         extent,
         image[0],
         cotangent[0],
@@ -2172,15 +2219,15 @@
         0,
     )
     text_w_rows = text_cols.shape[3]
-    output, image_grad, text_grad, text_w_grad, embed_grad, final, side, vectors = backward_call(
+    image_grad, text_grad, text_w_grad, embed_grad, final, side, vectors = backward_call(
         extent,
         embed,
         (gain1, gain2, gain3),
         stats,
         shifts,
         (
-            attended,
-            dq,
+            query_part,
+            side_part,
             dkv,
             own_dt,
             all_dt,
@@ -2193,7 +2240,6 @@
             attn_flat,
             qkv_turned,
             text_cols.reshape(items * parts, tokens, text_w_rows),
-            proj_w,
             conv1_w.reshape(9 * channels, channels),
             conv2_w.reshape(9 * channels, channels),
             text_w,
@@ -2258,6 +2304,7 @@
         and parts == HEADS
         and channels % (16 * items * parts) == 0
         and pixels % 512 == 0
+        and channels % 512 == 0
         and tokens % 16 == 0
         and text.shape[2] % (128 * parts) == 0
         and text.shape[2] == embed.shape[1] <= 4 * channels

time: 242 us -> 220 us (0.909)
  Pallas kernels: 240 us -> 219 us
    pallas_call x1, Pallas kernels: 78.4 us -> 62.4 us  [backward_call(): pl.pallas_call(functools.partial(backward_kernel, items, n), out_shape=ou...]
    pallas_call x1, Pallas kernels: 157 us -> 152 us  [forward_call(): pl.pallas_call(functools.partial(forward_kernel, items, n, step, bq), out...]
where the time goes in v4:
time: 220 us
  Pallas kernels  219 us (100%)
    pallas_call x1, Pallas kernels, forward_call(): pl.pallas_call(functools.partial(forward_kernel, items, n, step, bq), out...  152 us
    pallas_call x1, Pallas kernels, backward_call(): pl.pallas_call(functools.partial(backward_kernel, items, n), out_shape=ou...  62.4 us
    pallas_call x1, Pallas kernels, finalize_call(): pl.pallas_call(finalize_kernel, out_shape=tuple(outs), in_specs=[ANYWHERE...  4.69 us

profile of v4, /device:TPU:0, one launch (start us, length us, event | category | flops | bytes accessed | tf_op | source)
XLA Modules:
  0.0 219.6 jit_solution(7479435010912891153)
XLA Ops:
  0.6 151.8 %forward.1 = (f32[10,64,512]{2,1,0:T(8,128)}, f32[10,64,512]{2,1,0:T(8,128)}, bf16[10,64,512]{2,1,0:T(8,128)(2,1)}, bf16[4,10,64,512]{3,2,1,0:T(8,128)(2,1)}, bf...) custom-call(s32[1,2]{1,0:T(1,128)} %refs_0_.3, ...), custom_call_target="tpu_custom_call" | custom-call | flops 5368709120 | bytes 62914560 | tf_op jit(solution)/shard_map/forward/pallas_call | solution.py:1448
  152.4 62.4 %backward.1 = (f32[8,64,512]{2,1,0:T(8,128)}, f32[16,2048]{1,0:T(8,128)}, f32[256,1024]{1,0:T(8,128)}, f32[1,2048]{1,0:T(1,128)}, bf16[2,3,4,3,16,512]{5,4,3,2,1...) custom-call(s32[1,2]{1,0:T(1,128)} %refs_0_.3, bf16[1,2048]{1,0:T(2,128)(2,1)} %refs_1_.1, ...), custom_call_target="tpu_custom_call" | custom-call | flops 10737418240 | bytes 62914560 | tf_op jit(solution)/shard_map/backward/pallas_call | solution.py:2177
  214.8 4.7 %finalize.1 = (bf16[8,64,512]{2,1,0:T(8,128)(2,1)}, f32[8,64,512]{2,1,0:T(8,128)}, f32[16,2048]{1,0:T(8,128)}, f32[256,1024]{1,0:T(8,128)}, f32[1,2048]{1,0:T(1,...) custom-call(bf16[2,3,4,3,16,512]{5,4,3,2,1,0:T(8,128)(2,1)} %get-tup, ...), custom_call_target="tpu_custom_call" | custom-call | tf_op jit(solution)/shard_map/finalize/pallas_call | solution.py:2062

commit v5 on v4

--- a/solution.py
+++ b/solution.py
@@ -1015,7 +1015,7 @@
 def forward_kernel(items, n, step, bq, *refs):
     (info, image, cot, text, embed, gain1, gain2, gain3, w1_in, w2_in, embed_in, text_in, qkv_in, proj_in,
      first_out, mid_out, cot_out, hidden_all, second_all, attn_out, turned_out, output, query_part, side_out, dkv_out,
-     dt_out, dt_all, text_cols, stats_out, shifts_out,
+     dt_out, text_cols, stats_out, shifts_out,
      image_v, cot_v, text_v, w1, w2, wide_w, qkv_w, proj_w, first_v, mid_v, hidden, second, attn,
      turned, pairs, queries, go, text_kv, cols, shifted, acc, own, slots,
      pair_land, query_land, go_land, text_pair, o, dq, dkv, dtext, same, o_land, dq_land, masked, out_v, query_acc,
@@ -1262,7 +1262,6 @@
     o_copy = give(5, o, o_land)
     dq_copy = give(6, dq, dq_land)
     dkv_copy = give(7, dkv, dkv_out)
-    dt_copy = give(8, dtext, dt_out)
 
     def done(h):
         @pl.when(h > 0)
@@ -1297,17 +1296,9 @@
     for r in range(n):
         tokens = text.shape[0]
         dtext[r] = flat[r * tokens : (r + 1) * tokens].astype(BF16)
-    grid.loop(n, lambda h: dt_copy(h).start())
-
-    def gather_copy(k):
-        return remote(
-            dtext, dt_all.at[item, me], row_send.at[9, k], row_recv.at[9, k], grid.row(k)
-        )
-
-    grid.loop(n, lambda k: gather_copy(k).start())
+
     own_dkv = fetch(dkv.at[me], dkv_out.at[me])
-    own_dt = fetch(dtext.at[me], dt_out.at[me])
-    own_all = fetch(dtext, dt_all.at[item, me])
+    own_dt = fetch(dtext, dt_out)
 
     o_land[me] = o[me]
     dq_land[me] = dq[me]
@@ -1348,9 +1339,8 @@
     grid.loop(items, lambda k: hidden_copy(k).wait())
     grid.loop(items, lambda k: second_copy(k).wait())
     grid.loop(items, lambda k: cols_copy(k).wait())
-    for copy in (dkv_copy, dt_copy, gather_copy):
-        grid.loop(n, lambda h: copy(h).wait())
-    for c in (own_hidden, own_first, own_second, own_cot, own_turned, own_attn, own_mid, own_dkv, own_dt, own_all,
+    grid.loop(n, lambda h: dkv_copy(h).wait())
+    for c in (own_hidden, own_first, own_second, own_cot, own_turned, own_attn, own_mid, own_dkv, own_dt,
               own_cols, put_query, put_output, put_side):
         c.wait()
 
@@ -1379,7 +1369,6 @@
         sds((chips, rows, 2 * channels), BF16),
         sds((n, 2 * head_dim, pixels), BF16),
         sds((n, tokens, 2 * head_dim), BF16),
-        sds((items, n, n, tokens, 2 * head_dim), BF16),
         sds((items, n, tokens, text_width // n), BF16),
         sds((3, 8, channels), F32),
         sds((1, 2 * channels), F32),
@@ -1434,8 +1423,8 @@
         DMA((3, n)),
         DMA((4, 2)),
         DMA((4, 2)),
-        DMA((10, n)),
-        DMA((10, n)),
+        DMA((8, n)),
+        DMA((8, n)),
         DMA((3, items)),
         DMA((3, items)),
         DMA((1,)),
@@ -1449,7 +1438,7 @@
         functools.partial(forward_kernel, items, n, step, bq),
         out_shape=outs,
         in_specs=[SCALARS] + [ANYWHERE] * 3 + [WHOLE] * 4 + [ANYWHERE] * 6,
-        out_specs=(ANYWHERE,) * 14 + (WHOLE,) * 2,
+        out_specs=(ANYWHERE,) * 13 + (WHOLE,) * 2,
         scratch_shapes=scratch,
         compiler_params=pltpu.CompilerParams(
             collective_id=identity, has_side_effects=True, vmem_limit_bytes=62 << 20
@@ -1683,15 +1672,15 @@
 
 def backward_kernel(items, n, *refs):
     (info, embed, gain1, gain2, gain3, stats_in, shifts,
-     query_part, side_in, dkv_in, dt_in, dt_all, first, middle, cot, image, hidden_all, second_all, attn_in,
+     query_part, side_in, dkv_in, dt_in, first, middle, cot, image, hidden_all, second_all, attn_in,
      turned_in, text_cols, w1_in, w2_in, text_in, embed_in,
      image_grad, text_grad, text_w_grad, embed_grad, final_out, side_out, vectors,
-     weight, qkv_turned, first_v, mid_v, cot_v, image_v, attn, cols, rows_v, dkv, dt, own_dt,
+     weight, qkv_turned, first_v, mid_v, cot_v, image_v, attn, cols, rows_v, dkv, dtext, dt, own_dt,
      grad_v, grad_mid, moved_v, pre, acc, shifted, shifted_all, image_out, text_v, text_w_v, embed_v, same,
      turned, quarter, part, from_core, chip_sum, from_chip, final,
      side_v, side_core, side_sum, side_item, side_total, side_chip, side_final,
      vector, vector_land, own, slots,
-     load, sum_send, sum_recv, edge_send, edge_recv, dt_send, dt_recv, dt_core_send, dt_core_recv, vec_send, vec_recv,
+     load, sum_send, sum_recv, edge_send, edge_recv, text_send, text_recv, dt_send, dt_recv, dt_core_send, dt_core_recv, vec_send, vec_recv,
      k_item_send, k_item_recv, k_core_send, k_core_recv, k_chip_send, k_chip_recv, k_final_send, k_final_recv,
      s_core_send, s_core_recv, s_item_send, s_item_recv, s_chip_send, s_chip_recv, s_final_send,
      s_final_recv) = refs
@@ -1725,8 +1714,7 @@
     got_first = fetch(first, first_v)
     got_attn = fetch(attn_in, attn)
     got_side = fetch(side_in, side_total.at[:, :, 2 * channels :])
-    got_dt = fetch(dt_in, own_dt)
-    got_all = fetch(dt_all.at[item], dt.at[item])
+    got_dt = fetch(dt_in, dtext)
     got_second = fetch(second_all, rows_v)
     got_image = fetch(image, image_v)
     got_cols = fetch(text_cols, cols)
@@ -1750,16 +1738,23 @@
                    (s_core_send, s_core_recv), (s_item_send, s_item_recv), (s_chip_send, s_chip_recv),
                    (s_final_send, s_final_recv))
 
-    core = lax.rem(me, 2)
+    core, chip, chips = lax.rem(me, 2), me // 2, n // 2
     half = heads // 2
-    core_heads = pl.ds(core * half, half)
+
+    def text_copy(k):
+        to = lax.rem(me + k, n)
+        return remote(dtext.at[to], own_dt.at[me], text_send.at[0, k], text_recv.at[0, k], grid.row(k))
+
+    def gather_copy(k):
+        to = {"items": item, "rows": lax.rem(chip + k, chips) * 2 + core}
+        return remote(dtext, dt.at[item, core, chip], text_send.at[1, k], text_recv.at[1, k], to)
 
     def dt_copy(k):
-        mine = dt.at[item, core_heads]
+        mine = dt.at[item, core]
         return remote(mine, mine, dt_send.at[k], dt_recv.at[k], grid.peer(k))
 
     def dt_core_copy(k):
-        mine = dt.at[lax.rem(item + k, items), core_heads]
+        mine = dt.at[lax.rem(item + k, items), core]
         sibling = {"items": item, "rows": me + 1 - 2 * core}
         return remote(mine, mine, dt_core_send.at[k], dt_core_recv.at[k], sibling)
 
@@ -1785,6 +1780,7 @@
     sums[0].start(stats)
     edges[0].start()
 
+
     got_attn.wait()
 
     def qkv_head(h):
@@ -1797,6 +1793,11 @@
     got_cot.wait()
 
     stats4 = sums[0].result()
+    got_dt.wait()
+    grid.loop(n, lambda k: text_copy(k).start())
+    grid.loop(chips, lambda k: gather_copy(k).start())
+    own_dt[me] = dtext[me]
+    dt[item, core, chip] = dtext[...]
     mean, cross = means_of(stats4, gain3[...], count, same[...])
     edges[0].wait()
 
@@ -1879,16 +1880,18 @@
     got_hidden.wait()
     shift_rows()
     sum1.wait_grads()
-    got_all.wait()
+    grid.loop(chips, lambda k: gather_copy(k).wait())
     grid.loop(items, lambda k: dt_copy(k).start())
+    dt_core_copy(0).start()
     sum1.compute(0, shifted_all)
+    sum2.over_items(0)
+    sum1.over_chips(0)
     sum1.compute(1, shifted_all)
-    sum1.over_chips(0)
+    sum2.over_items(1)
+    sum1.over_chips(1)
     sum1.compute(2, shifted_all)
-    sum1.over_chips(1)
     sum1.over_chips(2)
-    for a in range(3):
-        sum2.over_items(a)
+    sum2.over_items(2)
     side.spread()
     grid.loop(items, lambda k: dt_copy(k).wait())
     grid.loop(items, lambda k: dt_core_copy(k).start())
@@ -1923,7 +1926,7 @@
     each_row(rows_dev, finish_row)
     put_image = fetch(image_out, image_grad)
 
-    got_dt.wait()
+    grid.loop(n, lambda k: text_copy(k).wait())
     for c in got_text_w:
         c.wait()
     total = None
@@ -1943,12 +1946,13 @@
         sum2.wait_final(a)
     put_final2 = fetch(final.at[0], final_out.at[0])
 
+    dt_core_copy(0).wait()
     grid.loop(items, lambda k: dt_core_copy(k).wait())
     got_cols.wait()
     tokens = cols.shape[0] * cols.shape[1]
     flat_cols = cols[...].reshape(tokens, cols.shape[2]).astype(F32).T.astype(BF16)
     for h in range(heads):
-        rhs = jnp.concatenate([dt[g, h].reshape(tokens // items, 2 * head_dim) for g in range(items)], axis=0)
+        rhs = jnp.concatenate([dt[g, h % 2, h // 2].reshape(tokens // items, 2 * head_dim) for g in range(items)], axis=0)
         text_w_v[:, h * 2 * head_dim : (h + 1) * 2 * head_dim] = dot(flat_cols, rhs, 1, 0)
     put_text_w = fetch(text_w_v, text_w_grad)
 
@@ -2083,7 +2087,7 @@
 def backward_call(info, embed, gains, stats, shifts, arrays, identity):
     items, n = lax.axis_size("items"), lax.axis_size("rows")
     dtext = arrays[3]
-    image, text_cols, text_w = arrays[8], arrays[13], arrays[16]
+    image, text_cols, text_w = arrays[7], arrays[12], arrays[15]
     rows_dev, width, channels = image.shape
     pixels = rows_dev * width
     head_dim = channels // HEADS
@@ -2114,7 +2118,8 @@
         v(text_cols.shape, BF16),
         v((items,) + padded, BF16),
         v((n, 2 * head_dim, pixels), BF16),
-        v((items, n) + dtext.shape, BF16),
+        v(dtext.shape, BF16),
+        v((items, 2, chips) + dtext.shape, BF16),
         v(dtext.shape, BF16),
         v(padded, F32),
         v(padded, F32),
@@ -2151,6 +2156,8 @@
         DMA((3, n)),
         DMA((2, 2)),
         DMA((2, 2)),
+        DMA((2, n)),
+        DMA((2, n)),
         DMA((items,)),
         DMA((items,)),
         DMA((items,)),
@@ -2200,8 +2207,8 @@
     head_dim = channels // HEADS
     tokens = text.shape[1]
     share = channels // parts
-    (first, middle, cot, hidden_all, second_all, attn_flat, qkv_turned, output, query_part, side_part, dkv, own_dt,
-     all_dt, text_cols, stats, shifts) = forward_call(
+    (first, middle, cot, hidden_all, second_all, attn_flat, qkv_turned, output, query_part, side_part, dkv, dtext,
+     text_cols, stats, shifts) = forward_call(
         extent,
         image[0],
         cotangent[0],
@@ -2229,8 +2236,7 @@
             query_part,
             side_part,
             dkv,
-            own_dt,
-            all_dt,
+            dtext,
             first,
             middle,
             cot,
@@ -2303,6 +2309,7 @@
         images == 1
         and parts == HEADS
         and channels % (16 * items * parts) == 0
+        and parts == 8
         and pixels % 512 == 0
         and channels % 512 == 0
         and tokens % 16 == 0

time: 220 us -> 215 us (0.977)
  Pallas kernels: 219 us -> 214 us
    pallas_call x1, Pallas kernels: 152 us -> 146 us  [forward_call(): pl.pallas_call(functools.partial(forward_kernel, items, n, step, bq), out...]
where the time goes in v5:
time: 215 us; the launch traced here: 214 us
  Pallas kernels  214 us (100%)
    pallas_call x1, Pallas kernels, forward_call(): pl.pallas_call(functools.partial(forward_kernel, items, n, step, bq), out...  146 us
    pallas_call x1, Pallas kernels, backward_call(): pl.pallas_call(functools.partial(backward_kernel, items, n), out_shape=ou...  62.8 us
    pallas_call x1, Pallas kernels, finalize_call(): pl.pallas_call(finalize_kernel, out_shape=tuple(outs), in_specs=[ANYWHERE...  4.68 us

profile of v5, /device:TPU:0, one launch (start us, length us, event | category | flops | bytes accessed | tf_op | source)
XLA Modules:
  0.0 214.5 jit_solution(6892038335956538931)
XLA Ops:
  0.6 146.2 %forward.1 = (f32[10,64,512]{2,1,0:T(8,128)}, f32[10,64,512]{2,1,0:T(8,128)}, bf16[10,64,512]{2,1,0:T(8,128)(2,1)}, bf16[4,10,64,512]{3,2,1,0:T(8,128)(2,1)}, bf...) custom-call(s32[1,2]{1,0:T(1,128)} %refs_0_.3, ...), custom_call_target="tpu_custom_call" | custom-call | flops 5368709120 | bytes 62914560 | tf_op jit(solution)/shard_map/forward/pallas_call | solution.py:1437
  146.9 62.8 %backward.1 = (f32[8,64,512]{2,1,0:T(8,128)}, f32[16,2048]{1,0:T(8,128)}, f32[256,1024]{1,0:T(8,128)}, f32[1,2048]{1,0:T(1,128)}, bf16[2,3,4,3,16,512]{5,4,3,2,1...) custom-call(s32[1,2]{1,0:T(1,128)} %refs_0_.3, bf16[1,2048]{1,0:T(2,128)(2,1)} %refs_1_.1, ...), custom_call_target="tpu_custom_call" | custom-call | flops 10737418240 | bytes 62914560 | tf_op jit(solution)/shard_map/backward/pallas_call | solution.py:2184
  209.6 4.7 %finalize.1 = (bf16[8,64,512]{2,1,0:T(8,128)(2,1)}, f32[8,64,512]{2,1,0:T(8,128)}, f32[16,2048]{1,0:T(8,128)}, f32[256,1024]{1,0:T(8,128)}, f32[1,2048]{1,0:T(1,...) custom-call(bf16[2,3,4,3,16,512]{5,4,3,2,1,0:T(8,128)(2,1)} %get-tup, ...), custom_call_target="tpu_custom_call" | custom-call | tf_op jit(solution)/shard_map/finalize/pallas_call | solution.py:2066

commit v6 on v5

--- a/solution.py
+++ b/solution.py
@@ -1023,6 +1023,7 @@
      load, sum_send, sum_recv, edge_send, edge_recv, row_send, row_recv, item_send, item_recv,
      s_core_send, s_core_recv, s_item_send, s_item_recv, *scratch) = refs
     grid = Grid(items, n)
+    grid.greet()
     item, me = grid.item, grid.me
     rows_dev, width, channels = image.shape
     pixels = rows_dev * width
@@ -1057,7 +1058,6 @@
         for j, field in enumerate((image_v, cot_v, first_v, mid_v))
     ]
     sums = [Sums(grid, own.at[j], slots.at[j], sum_send.at[j], sum_recv.at[j]) for j in range(3)]
-    grid.greet()
     for e in edges:
         e.clear()
     same[...] = group_matrix(channels)
@@ -1116,6 +1116,7 @@
     stats_out[0] = stats
     average, inverse = norm_of(stats, count, same[...])
     edges[0].wait()
+    grid.loop(n // 2, lambda k: go_copy(k).start())
 
     def to_hidden(r):
         ok = inside(base + r - 1)
@@ -1237,7 +1238,10 @@
 
     def send_rest(k):
         query_copy(k).start()
-        go_copy(k).start()
+
+        @pl.when(k >= n // 2)
+        def _():
+            go_copy(k).start()
 
     grid.loop(n, send_rest)
     own_go.wait()

time: 215 us -> 214 us (level)
    pallas_call x1, Pallas kernels: 146 us -> 143 us  [forward_call(): pl.pallas_call(functools.partial(forward_kernel, items, n, step, bq), out...]
where the time goes in v6:
time: 214 us; the launch traced here: 213 us
  Pallas kernels  212 us (99%)
    pallas_call x1, Pallas kernels, forward_call(): pl.pallas_call(functools.partial(forward_kernel, items, n, step, bq), out...  143 us
    pallas_call x1, Pallas kernels, backward_call(): pl.pallas_call(functools.partial(backward_kernel, items, n), out_shape=ou...  64 us
    pallas_call x1, Pallas kernels, finalize_call(): pl.pallas_call(finalize_kernel, out_shape=tuple(outs), in_specs=[ANYWHERE...  4.68 us

profile of v6, /device:TPU:0, one launch (start us, length us, event | category | flops | bytes accessed | tf_op | source)
XLA Modules:
  0.0 212.8 jit_solution(12398965696030503597)
XLA Ops:
  0.6 143.2 %forward.1 = (f32[10,64,512]{2,1,0:T(8,128)}, f32[10,64,512]{2,1,0:T(8,128)}, bf16[10,64,512]{2,1,0:T(8,128)(2,1)}, bf16[4,10,64,512]{3,2,1,0:T(8,128)(2,1)}, bf...) custom-call(s32[1,2]{1,0:T(1,128)} %refs_0_.3, ...), custom_call_target="tpu_custom_call" | custom-call | flops 5368709120 | bytes 62914560 | tf_op jit(solution)/shard_map/forward/pallas_call | solution.py:1441
  143.9 64.0 %backward.1 = (f32[8,64,512]{2,1,0:T(8,128)}, f32[16,2048]{1,0:T(8,128)}, f32[256,1024]{1,0:T(8,128)}, f32[1,2048]{1,0:T(1,128)}, bf16[2,3,4,3,16,512]{5,4,3,2,1...) custom-call(s32[1,2]{1,0:T(1,128)} %refs_0_.3, bf16[1,2048]{1,0:T(2,128)(2,1)} %refs_1_.1, ...), custom_call_target="tpu_custom_call" | custom-call | flops 10737418240 | bytes 62914560 | tf_op jit(solution)/shard_map/backward/pallas_call | solution.py:2188
  207.9 4.7 %finalize.1 = (bf16[8,64,512]{2,1,0:T(8,128)(2,1)}, f32[8,64,512]{2,1,0:T(8,128)}, f32[16,2048]{1,0:T(8,128)}, f32[256,1024]{1,0:T(8,128)}, f32[1,2048]{1,0:T(1,...) custom-call(bf16[2,3,4,3,16,512]{5,4,3,2,1,0:T(8,128)(2,1)} %get-tup, ...), custom_call_target="tpu_custom_call" | custom-call | tf_op jit(solution)/shard_map/finalize/pallas_call | solution.py:2070

commit v7 on v6

--- a/solution.py
+++ b/solution.py
@@ -90,7 +90,7 @@
                 slot, goa, q = back
                 dp = dot(vn[at, :], goa, 1, 0)
                 e = raised[slot][at, :]
-                ds = (e.astype(F32) * dp).astype(BF16)
+                ds = e * dp.astype(BF16)
                 dvt[:, at] += dot(goa[:d], e, 1, 1)
                 dkt[:, at] += dot(q, ds, 1, 1)
                 dq = dq + dot(kt[:, at], ds, 1, 0)

time: 214 us -> 214 us (level)
  no operation moved by 1% of the time
where the time goes in v7:
time: 214 us; the launch traced here: 212 us
  Pallas kernels  212 us (99%)
    pallas_call x1, Pallas kernels, forward_call(): pl.pallas_call(functools.partial(forward_kernel, items, n, step, bq), out...  143 us
    pallas_call x1, Pallas kernels, backward_call(): pl.pallas_call(functools.partial(backward_kernel, items, n), out_shape=ou...  64.1 us
    pallas_call x1, Pallas kernels, finalize_call(): pl.pallas_call(finalize_kernel, out_shape=tuple(outs), in_specs=[ANYWHERE...  4.69 us

profile of v7, /device:TPU:0, one launch (start us, length us, event | category | flops | bytes accessed | tf_op | source)
XLA Modules:
  0.0 212.4 jit_solution(2195972402519010233)
XLA Ops:
  0.6 142.8 %forward.1 = (f32[10,64,512]{2,1,0:T(8,128)}, f32[10,64,512]{2,1,0:T(8,128)}, bf16[10,64,512]{2,1,0:T(8,128)(2,1)}, bf16[4,10,64,512]{3,2,1,0:T(8,128)(2,1)}, bf...) custom-call(s32[1,2]{1,0:T(1,128)} %refs_0_.3, ...), custom_call_target="tpu_custom_call" | custom-call | flops 5368709120 | bytes 62914560 | tf_op jit(solution)/shard_map/forward/pallas_call | solution.py:1441
  143.5 64.1 %backward.1 = (f32[8,64,512]{2,1,0:T(8,128)}, f32[16,2048]{1,0:T(8,128)}, f32[256,1024]{1,0:T(8,128)}, f32[1,2048]{1,0:T(1,128)}, bf16[2,3,4,3,16,512]{5,4,3,2,1...) custom-call(s32[1,2]{1,0:T(1,128)} %refs_0_.3, bf16[1,2048]{1,0:T(2,128)(2,1)} %refs_1_.1, ...), custom_call_target="tpu_custom_call" | custom-call | flops 10737418240 | bytes 62914560 | tf_op jit(solution)/shard_map/backward/pallas_call | solution.py:2188
  207.6 4.7 %finalize.1 = (bf16[8,64,512]{2,1,0:T(8,128)(2,1)}, f32[8,64,512]{2,1,0:T(8,128)}, f32[16,2048]{1,0:T(8,128)}, f32[256,1024]{1,0:T(8,128)}, f32[1,2048]{1,0:T(1,...) custom-call(bf16[2,3,4,3,16,512]{5,4,3,2,1,0:T(8,128)(2,1)} %get-tup, ...), custom_call_target="tpu_custom_call" | custom-call | tf_op jit(solution)/shard_map/finalize/pallas_call | solution.py:2070
